TPU v7x, 512 devices: a whole 4x8x8 slice. The times are simulated.
512 devices in a mesh: dict: 16 (over z, core), scan: 32 (over x, y).
Axes of the slice: x: 4, y: 8, z: 8, core: 2. Of those that a mesh axis runs over, the one named last changes fastest.
Arguments:
- patterns: float32 [512, 256, 3600], P('scan', 'dict'), may hold values from -63 to 63
- background: float32 [3600], replicated, may hold values from -6 to 6
- templates: bfloat16 [2048, 3600], P('dict'), may hold values from -19.5 to 19.5
- grain_id: int32 [512, 256], P('scan', 'dict'), may hold values from 0 to 127
- keep_mask: int32 [512, 256], P('scan', 'dict'), may hold values 0 or 1
- grain_row: int32 [128], replicated, may hold values from 0 to 127, each once
Outputs:
- max_score: float32 [512, 256], P('scan', 'dict')
- grain_patterns: float32 [128, 3600], P('scan')
Inputs may be any that keep to these rules, and one draw needn't show every extreme that they name: grain_row holds each of 0 to 127 once.
All inputs are finite; a program needn't handle non-finite values. No bound on the sum of `keep_mask` on one device may be relied on, other than what follows from the above.
Results may differ from a plain program's by a relative error of at most 0.0045.
Values may be sent and summed in bfloat16 or wider, within the bound.
No kernel may reach another device: no remote copies, remote signals or barrier semaphores. Data moves between devices by JAX's collectives and lax.ppermute only.
A program may use at most 128 MiB of HBM per device.

v0:
```python
import math

import jax
import jax.numpy as jnp
from jax import lax
from jax.sharding import PartitionSpec as P


def with_halo(block, sides, width):
    for axis, dim in sides:
        count = lax.axis_size(axis)
        forward = [(i, i + 1) for i in range(count - 1)]
        backward = [(target, source) for source, target in forward]
        low = lax.ppermute(
            lax.slice_in_dim(block, block.shape[dim] - width, None, axis=dim), axis, forward
        )
        high = lax.ppermute(lax.slice_in_dim(block, 0, width, axis=dim), axis, backward)
        block = jnp.concatenate([low, block, high], axis=dim)
    return block


def unit_rows(values):
    mean_square = jnp.mean(values * values, axis=-1, keepdims=True)
    return values * lax.rsqrt(mean_square + 1e-05)


def filter_points(measured, background):
    centered = measured - background
    centered = centered - jnp.mean(centered, axis=-1, keepdims=True)
    return unit_rows(centered).astype(jnp.bfloat16)


def shards(patterns, background, templates, grain_id, keep_mask, grain_row):
    tile_rows, tile_cols, pixels = patterns.shape
    filtered = filter_points(patterns, background)
    padded = with_halo(filtered, (("dict", 1), ("scan", 0)), 1)
    neighbour = jnp.zeros((tile_rows, tile_cols, pixels), jnp.float32)
    for row_shift in range(3):
        for col_shift in range(3):
            neighbour = neighbour + padded[
                row_shift : row_shift + tile_rows, col_shift : col_shift + tile_cols
            ].astype(jnp.float32)
    indexed = unit_rows(neighbour).astype(jnp.bfloat16).reshape(tile_rows * tile_cols, pixels)
    point_count = indexed.shape[0]
    centered_panel = templates.astype(jnp.float32)
    centered_panel = centered_panel - jnp.mean(centered_panel, axis=-1, keepdims=True)
    unit_panel = unit_rows(centered_panel).astype(jnp.bfloat16)
    lowest = jnp.full((point_count,), -1e30, jnp.float32)
    scores = lax.dot_general(
        indexed,
        lax.all_gather(unit_panel, "dict", axis=0, tiled=True),
        (((1,), (1,)), ((), ())),
        preferred_element_type=jnp.float32,
    )
    best_dot = jnp.maximum(lowest, jnp.max(scores, axis=1))
    root_inverse = 1.0 / math.sqrt(pixels)
    max_score = (best_dot * root_inverse).reshape(tile_rows, tile_cols)
    point_grain = grain_id.reshape(-1)
    point_keep = keep_mask.reshape(-1)
    grain_count = grain_row.shape[0]
    grain_index = jnp.arange(grain_count, dtype=jnp.int32)
    matches = point_grain[:, None] == grain_index[None, :]
    point_row = jnp.sum(jnp.where(matches, grain_row[None, :], 0), axis=1)
    selector = ((point_row[:, None] == grain_index[None, :]) & (point_keep[:, None] == 1)).astype(
        jnp.bfloat16
    )
    partial_rows = lax.psum_scatter(
        lax.dot_general(
            selector, indexed, (((0,), (0,)), ((), ())), preferred_element_type=jnp.float32
        ).astype(jnp.bfloat16),
        "scan",
        scatter_dimension=0,
        tiled=True,
    ).astype(jnp.float32)
    grain_total = lax.psum(partial_rows, "dict")
    grain_patterns = unit_rows(grain_total)
    return (max_score, grain_patterns)


def solution(mesh):
    return jax.shard_map(
        shards,
        mesh=mesh,
        in_specs=(
            P("scan", "dict", None),
            P(),
            P("dict", None),
            P("scan", "dict"),
            P("scan", "dict"),
            P(),
        ),
        out_specs=(P("scan", "dict"), P("scan", None)),
        check_vma=False,
    )
```

profile of v0, /device:TPU:1, one launch (start us, length us, event | category | flops | bytes accessed | tf_op | source)
XLA Modules:
  0.0 275.0 jit_solution(5418159544022952343)
XLA Ops:
  8.1 3.4 %fusion = f32[16,16]{0,1:T(8,128)S(1)} fusion(f32[16,16,3600]{2,1,0:T(8,128)} %param.6, f32[3600]{0:T(1024)} %param.7), kind=kLoop, calls=%fused_computation.9 | loop fusion | flops 1842944 | bytes 3701824 | tf_op jit(solution)/shard_map/reduce_sum | solution.py:29
  11.5 1.2 multiply_reduce_fusion.1
  12.8 1.7 multiply_convert_fusion.1
  14.5 8.8 %collective-permute-start.1 = (bf16[16,1,3600]{2,0,1:T(8,128)(2,1)S(1)}, bf16[16,1,3600]{2,0,1:T(8,128)(2,1)S(1)}, u32[]{:S(2)}, u32[]{:S(2)}) collective-permute-start(bf16[16,1,3600]{2,0,1:T(8,128)(2,1)S(1)} %get-tuple-element.9), channel_id=1, source_target_pairs={{32,0},{64,32},{96,64},{128,96},{160,128},{192,160},{224,192},{256... | collective-permute-start | bytes 345608 | tf_op jit(solution)/shard_map/ppermute | solution.py:17
  23.3 1.9 collective-permute-start
  25.7 0.5 fusion.3
  26.2 0.8 collective-permute-done
  27.5 1.3 collective-permute-start.2
  28.8 0.7 copy.20
  29.5 1.3 collective-permute-start.3
  31.1 1.9 collective-permute-done.2
  33.3 4.7 %collective-permute-done.3 = bf16[1,18,3600]{2,1,0:T(8,128)(2,1)} collective-permute-done((bf16[1,18,3600]{2,1,0:T(8,128)(2,1)}, bf16[1,18,3600]{2,1,0:T(8,128)(2,1)}, u32[]{:S(2)}, u32[]{:S(2)}) %collective-permute-start.3) | collective-permute-done | bytes 129632 | tf_op jit(solution)/shard_map/ppermute | solution.py:17
  38.0 1.1 copy.21
  39.1 2.9 %maximum_maximum_fusion = (bf16[17,18,3600]{2,0,1:T(8,128)(2,1)S(1)}, bf16[17,18,3600]{2,0,1:T(8,128)(2,1)S(1)}) fusion(bf16[16,1,3600]{2,0,1:T(8,128)(2,1)S(1)} %collective-permute-done.1, bf16[16,16,3600]{2,0,1:T(8,128)(2,1)S(1)} %multiply_convert_fusion.1, bf16[16,1,3600]{2,0,1:T(8,128)(2,1)S(1)} %collective-permute-done, ...), kind=kLoop, calls=%fused_computation.7 | loop fusion | flops 17625600 | bytes 6739200 | tf_op jit(solution)/shard_map/concatenate | solution.py:18
  42.0 4.5 %multiply_reduce_fusion = (f32[16,16]{0,1:T(8,128)S(1)}, f32[16,16,3600]{2,0,1:T(8,128)S(1)}) fusion(bf16[17,18,3600]{2,0,1:T(8,128)(2,1)S(1)} %get-tuple-element.5, bf16[16,1,3600]{2,0,1:T(8,128)(2,1)S(1)} %collective-permute-done.1, bf16[16,16,3600]{2,0,1:T(8,128)(2,1)S(1)} %multiply_convert_fusion.1, bf16[16,1,3600]{2,0,1:T(8,128)(2,1)S(1)} %collective-permute-done, ...), kind=kLoop, calls=%fused_computation.3 | loop fusion | flops 19353344 | bytes 16820224 | tf_op jit(solution)/shard_map/reduce_sum | solution.py:23
  47.2 1.5 convolution_convert_fusion
  48.8 1.2 fusion.4
  50.0 1.3 dynamic-slice
  51.9 156.3 %all-reduce.3.cloned.1.call-done = bf16[128,3600]{1,0:T(8,128)(2,1)} async-done(((bf16[128,3600]{1,0:T(8,128)(2,1)}), bf16[128,3600]{1,0:T(8,128)(2,1)}) %all-reduce.3.cloned.1.call-update) | async-done | bytes 921616
  208.3 0.8 dynamic-slice_convert_fusion
  209.1 48.6 %psum.7 = f32[4,3600]{1,0:T(4,128)S(1)} all-reduce(f32[4,3600]{1,0:T(4,128)S(1)} %dynamic-slice_convert_fusion), channel_id=1, replica_groups=mesh['dict'=16,'scan'=32] {'dict'}, use_global_device_ids=true, to_apply=%region_8.9 | all-reduce | flops 14400 | bytes 115200 | tf_op jit(solution)/shard_map/psum | solution.py:75
  257.9 0.7 broadcast_multiply_fusion
  258.6 8.3 %convolution_reduce_fusion = f32[256]{0:T(256)S(1)} fusion(bf16[256,3600]{1,0:T(8,128)(2,1)S(1)} %bitcast.6, bf16[2048,3600]{0,1:T(8,128)(2,1)} %all-gather.2.cloned.1.call-done), kind=kOutput, calls=%fused_computation.18 | convolution fusion | flops 3775397632 | bytes 16589824 | tf_op jit(solution)/shard_map/dot_general | solution.py:49
  266.9 0.7 mul.65
  (37 shorter events, 2.6 us)
Async XLA Ops:
  8.0 3.5 %copy-start.2 = (f32[3600]{0:T(1024)S(1)}, f32[3600]{0:T(1024)}, u32[]{:S(2)}) copy-start(f32[3600]{0:T(1024)} %param.7) | copy-start | bytes 43204
  8.0 200.3 %all-reduce.3.cloned.1.call-start = ((), (), s32[]{:S(2)}) async-start(), calls=%async_computation.1 | async-start | bytes 1900544
  8.1 3.4 %copy-start = (f32[16,16,3600]{2,1,0:T(8,128)S(1)}, f32[16,16,3600]{2,1,0:T(8,128)}, u32[]{:S(2)}) copy-start(f32[16,16,3600]{2,1,0:T(8,128)} %param.6) | copy-start | bytes 11059204
  12.7 12.5 %copy-start.1 = (bf16[128,3600]{0,1:T(8,128)(2,1)S(1)}, bf16[128,3600]{0,1:T(8,128)(2,1)}, u32[]{:S(2)}) copy-start(bf16[128,3600]{0,1:T(8,128)(2,1)} %param.8) | copy-start | bytes 2764804
  12.7 13.0 %copy-start.3 = (s32[16,16]{1,0:T(8,128)S(1)}, s32[16,16]{1,0:T(8,128)}, u32[]{:S(2)}) copy-start(s32[16,16]{1,0:T(8,128)} %param.10) | copy-start | bytes 3076
  14.4 16.4 %copy-start.4 = (s32[16,16]{1,0:T(8,128)S(1)}, s32[16,16]{1,0:T(8,128)}, u32[]{:S(2)}) copy-start(s32[16,16]{1,0:T(8,128)} %param.9) | copy-start | bytes 3076
  14.4 16.5 %copy-start.5 = (s32[128]{0:T(128)S(1)}, s32[128]{0:T(128)}, u32[]{:S(2)}) copy-start(s32[128]{0:T(128)} %param.11) | copy-start | bytes 1540
  14.5 11.7 %collective-permute-start.1 = (bf16[16,1,3600]{2,0,1:T(8,128)(2,1)S(1)}, bf16[16,1,3600]{2,0,1:T(8,128)(2,1)S(1)}, u32[]{:S(2)}, u32[]{:S(2)}) collective-permute-start(bf16[16,1,3600]{2,0,1:T(8,128)(2,1)S(1)} %get-tuple-element.9), channel_id=1, source_target_pairs={{32,0},{64,32},{96,64},{128,96},{160,128},{192,160},{224,192},{256... | collective-permute-start | bytes 345608 | tf_op jit(solution)/shard_map/ppermute | solution.py:17
  23.3 3.7 %collective-permute-start = (bf16[16,1,3600]{2,0,1:T(8,128)(2,1)S(1)}, bf16[16,1,3600]{2,0,1:T(8,128)(2,1)S(1)}, u32[]{:S(2)}, u32[]{:S(2)}) collective-permute-start(bf16[16,1,3600]{2,0,1:T(8,128)(2,1)S(1)} %get-tuple-element.8), channel_id=1, source_target_pairs={{0,32},{32,64},{64,96},{96,128},{128,160},{160,192},{192,224},{224... | collective-permute-start | bytes 345608 | tf_op jit(solution)/shard_map/ppermute | solution.py:14
  27.5 5.6 %collective-permute-start.2 = (bf16[1,18,3600]{2,1,0:T(8,128)(2,1)S(1)}, bf16[1,18,3600]{2,1,0:T(8,128)(2,1)S(1)}, u32[]{:S(2)}, u32[]{:S(2)}) collective-permute-start(bf16[1,18,3600]{2,1,0:T(8,128)(2,1)S(1)} %copy.18), channel_id=1, source_target_pairs={{0,1},{1,2},{2,3},{3,4},{4,5},{5,6},{6,7},{7,8},{8,9},{9,10},{10,1... | collective-permute-start | bytes 388808 | tf_op jit(solution)/shard_map/ppermute | solution.py:14
  29.5 8.5 %collective-permute-start.3 = (bf16[1,18,3600]{2,1,0:T(8,128)(2,1)}, bf16[1,18,3600]{2,1,0:T(8,128)(2,1)}, u32[]{:S(2)}, u32[]{:S(2)}) collective-permute-start(bf16[1,18,3600]{2,1,0:T(8,128)(2,1)} %copy.20), channel_id=1, source_target_pairs={{1,0},{2,1},{3,2},{4,3},{5,4},{6,5},{7,6},{8,7},{9,8},{10,9},{11,1... | collective-permute-start | bytes 388808 | tf_op jit(solution)/shard_map/ppermute | solution.py:17
  48.8 209.8 %all-gather.2.cloned.1.call-start = ((), (), s32[]{:S(2)}) async-start(), calls=%async_computation | async-start | bytes 15667200 | tf_op jit(solution)/shard_map/all_gather | solution.py:51
Sparse Core Ops, SparseCore 0:
  48.9 159.3 all-reduce.2
Sparse Core Ops, SparseCore 1:
  51.3 99.5 all-gather.1
where the time goes:
time: 276 us; the launch traced here: 275 us
  waiting for transfers between devices  164 us (59%)
  blocking collectives  48.6 us (18%)
  other arithmetic  18.5 us (7%)
  between operations  16.3 us (6%)
  starting transfers between devices  13.4 us (5%)
  matrix products  9.8 us (4%)
  local copies, waits for them, and re-layouts  4.55 us (2%)
    unnamed x3, waiting for transfers between devices  156 us
    psum x1, blocking collectives, shards(): grain_total = lax.psum(partial_rows, 'dict')  48.6 us
    ppermute x2, starting transfers between devices, with_halo(): lax.ppermute(lax.slice_in_dim(block, 0, width, axis=dim), axis, backward)  10.1 us
    dot_general x1, matrix products, shards(): lax.dot_general(indexed, lax.all_gather(unit_panel, 'dict', axis=0, tiled...  8.27 us
    reduce_sum x4, other arithmetic, unit_rows(): mean_square = jnp.mean(values * values, axis=-1, keepdims=True)  6.37 us
  transfers between devices with their start and end apart: 6, of which 4 were waited for; matrix products, arithmetic and copies ran while one was open for 2% of the time, Pallas kernels for 0%

commit v1 on v0

--- a/solution.py
+++ b/solution.py
@@ -32,6 +32,11 @@
 
 def shards(patterns, background, templates, grain_id, keep_mask, grain_row):
     tile_rows, tile_cols, pixels = patterns.shape
+    centered_panel = templates.astype(jnp.float32)
+    centered_panel = centered_panel - jnp.mean(centered_panel, axis=-1, keepdims=True)
+    unit_panel = unit_rows(centered_panel).astype(jnp.bfloat16)
+    panels = lax.all_gather(unit_panel, "dict", axis=0, tiled=True)
+    patterns, unit_panel = lax.optimization_barrier((patterns, unit_panel))
     filtered = filter_points(patterns, background)
     padded = with_halo(filtered, (("dict", 1), ("scan", 0)), 1)
     neighbour = jnp.zeros((tile_rows, tile_cols, pixels), jnp.float32)
@@ -41,20 +46,6 @@
                 row_shift : row_shift + tile_rows, col_shift : col_shift + tile_cols
             ].astype(jnp.float32)
     indexed = unit_rows(neighbour).astype(jnp.bfloat16).reshape(tile_rows * tile_cols, pixels)
-    point_count = indexed.shape[0]
-    centered_panel = templates.astype(jnp.float32)
-    centered_panel = centered_panel - jnp.mean(centered_panel, axis=-1, keepdims=True)
-    unit_panel = unit_rows(centered_panel).astype(jnp.bfloat16)
-    lowest = jnp.full((point_count,), -1e30, jnp.float32)
-    scores = lax.dot_general(
-        indexed,
-        lax.all_gather(unit_panel, "dict", axis=0, tiled=True),
-        (((1,), (1,)), ((), ())),
-        preferred_element_type=jnp.float32,
-    )
-    best_dot = jnp.maximum(lowest, jnp.max(scores, axis=1))
-    root_inverse = 1.0 / math.sqrt(pixels)
-    max_score = (best_dot * root_inverse).reshape(tile_rows, tile_cols)
     point_grain = grain_id.reshape(-1)
     point_keep = keep_mask.reshape(-1)
     grain_count = grain_row.shape[0]
@@ -64,16 +55,22 @@
     selector = ((point_row[:, None] == grain_index[None, :]) & (point_keep[:, None] == 1)).astype(
         jnp.bfloat16
     )
-    partial_rows = lax.psum_scatter(
-        lax.dot_general(
-            selector, indexed, (((0,), (0,)), ((), ())), preferred_element_type=jnp.float32
-        ).astype(jnp.bfloat16),
-        "scan",
-        scatter_dimension=0,
-        tiled=True,
-    ).astype(jnp.float32)
-    grain_total = lax.psum(partial_rows, "dict")
+    partial_rows = lax.dot_general(
+        selector, indexed, (((0,), (0,)), ((), ())), preferred_element_type=jnp.float32
+    ).astype(jnp.bfloat16)
+    owners = lax.axis_size("scan")
+    owned = grain_count // owners
+    parts = lax.all_to_all(partial_rows.reshape(owners, owned, pixels), "scan", 0, 0, tiled=True)
+    group_total = jnp.sum(parts.astype(jnp.float32), axis=0).astype(jnp.bfloat16)
+    group_totals = lax.all_gather(group_total, "dict", axis=0, tiled=False)
+    grain_total = jnp.sum(group_totals.astype(jnp.float32), axis=0)
     grain_patterns = unit_rows(grain_total)
+    panels, grain_patterns = lax.optimization_barrier((panels, grain_patterns))
+    scores = lax.dot_general(
+        indexed, panels, (((1,), (1,)), ((), ())), preferred_element_type=jnp.float32
+    )
+    root_inverse = 1.0 / math.sqrt(pixels)
+    max_score = (jnp.max(scores, axis=1) * root_inverse).reshape(tile_rows, tile_cols)
     return (max_score, grain_patterns)
 
 

time: 276 us -> 134 us (0.49)
  waiting for transfers between devices: 164 us -> 7.86 us
  blocking collectives: 48.6 us -> 60.4 us
  other arithmetic: 18.5 us -> 21.8 us
    unnamed x3 -> x1, waiting for transfers between devices: 156 us -> 0.02 us
    psum x1 -> x0, blocking collectives: 48.6 us -> none  [shards(): grain_total = lax.psum(partial_rows, 'dict')]
    all_to_all x0 -> x1, blocking collectives: none -> 35.3 us  [shards(): lax.all_to_all(partial_rows.reshape(owners, owned, pixels), 'scan', 0, 0,...]
    all_gather x0 -> x1, blocking collectives: none -> 25.1 us  [shards(): group_totals = lax.all_gather(group_total, 'dict', axis=0, tiled=False)]
    ppermute x2, starting transfers between devices: 3.22 us -> 8.6 us  [with_halo(): lax.ppermute(lax.slice_in_dim(block, block.shape[dim] - width, None, axis...]
    ppermute x2, starting transfers between devices: 10.1 us -> 5.99 us  [with_halo(): lax.ppermute(lax.slice_in_dim(block, 0, width, axis=dim), axis, backward)]
  transfers between devices with their start and end apart: 6 -> 5, of which waited for: 4 -> 4; matrix products, arithmetic and copies ran while one was open for 2% -> 16% of each run, Pallas kernels for 0% -> 0%
where the time goes in v1:
time: 134 us; the launch traced here: 133 us
  blocking collectives  60.4 us (45%)
  other arithmetic  21.8 us (16%)
  starting transfers between devices  14.6 us (11%)
  between operations  14.3 us (11%)
  matrix products  10.1 us (8%)
  waiting for transfers between devices  7.86 us (6%)
  local copies, waits for them, and re-layouts  4.43 us (3%)
    all_to_all x1, blocking collectives, shards(): lax.all_to_all(partial_rows.reshape(owners, owned, pixels), 'scan', 0, 0,...  35.3 us
    all_gather x1, blocking collectives, shards(): group_totals = lax.all_gather(group_total, 'dict', axis=0, tiled=False)  25.1 us
    ppermute x2, starting transfers between devices, with_halo(): lax.ppermute(lax.slice_in_dim(block, block.shape[dim] - width, None, axis...  8.6 us
    dot_general x1, matrix products, shards(): lax.dot_general(indexed, panels, (((1,), (1,)), ((), ())), preferred_elem...  8.24 us
    reduce_sum x4, other arithmetic, unit_rows(): mean_square = jnp.mean(values * values, axis=-1, keepdims=True)  7.56 us
    ppermute x2, starting transfers between devices, with_halo(): lax.ppermute(lax.slice_in_dim(block, 0, width, axis=dim), axis, backward)  5.99 us
    ppermute x2, waiting for transfers between devices, with_halo(): lax.ppermute(lax.slice_in_dim(block, 0, width, axis=dim), axis, backward)  5.78 us
    reduce_sum x1, other arithmetic, filter_points(): centered = centered - jnp.mean(centered, axis=-1, keepdims=True)  3.38 us
  transfers between devices with their start and end apart: 5, of which 4 were waited for; matrix products, arithmetic and copies ran while one was open for 16% of the time, Pallas kernels for 0%

profile of v1, /device:TPU:1, one launch (start us, length us, event | category | flops | bytes accessed | tf_op | source)
XLA Modules:
  0.0 133.5 jit_solution(237869246852707550)
XLA Ops:
  7.2 1.7 %convert_reduce_fusion = f32[128]{0:T(128)S(1)} fusion(bf16[128,3600]{0,1:T(8,128)(2,1)} %param.8), kind=kLoop, calls=%fused_computation.11 | loop fusion | flops 921472 | bytes 922112 | tf_op jit(solution)/shard_map/reduce_sum | solution.py:36
  8.9 1.7 %fusion.3 = f32[128]{0:T(128)S(1)} fusion(bf16[128,3600]{0,1:T(8,128)(2,1)} %param.8, f32[128]{0:T(128)S(1)} %broadcast_multiply_fusion.3), kind=kLoop, calls=%fused_computation.16 | loop fusion | flops 1843072 | bytes 922624 | tf_op jit(solution)/shard_map/reduce_sum | solution.py:23
  10.6 2.4 %fusion.4 = bf16[128,3600]{0,1:T(8,128)(2,1)} fusion(bf16[128,3600]{0,1:T(8,128)(2,1)} %param.8, f32[128]{0:T(128)S(1)} %add_rsqrt_fusion.3, f32[128]{0:T(128)S(1)} %broadcast_multiply_fusion.3), kind=kLoop, calls=%fused_computation.17 | loop fusion | flops 1843200 | bytes 1844224 | tf_op jit(solution)/shard_map/convert_element_type | solution.py:37
  13.0 3.4 %fusion = f32[16,16]{0,1:T(8,128)S(1)} fusion(f32[16,16,3600]{2,1,0:T(8,128)} %param.6, f32[3600]{0:T(1024)S(1)} %copy-done.1), kind=kLoop, calls=%fused_computation.9 | loop fusion | flops 1842944 | bytes 3701824 | tf_op jit(solution)/shard_map/reduce_sum | solution.py:29
  16.4 1.2 multiply_reduce_fusion.1
  17.7 1.7 %multiply_convert_fusion.1 = bf16[16,16,3600]{2,0,1:T(8,128)(2,1)S(1)} fusion(f32[16,16,3600]{2,1,0:T(8,128)S(1)} %copy-done, f32[16,16]{0,1:T(8,128)S(1)} %add_rsqrt_fusion.1, f32[16,16]{0,1:T(8,128)S(1)} %broadcast_multiply_fusion.1, f32[3600]{0:T(1024)S(1)} %copy-done.1), kind=kLoop, calls=%fused_computation.5 | loop fusion | flops 3686400 | bytes 5546048 | tf_op jit(solution)/shard_map/convert_element_type | solution.py:30
  19.4 5.4 %collective-permute-start = (bf16[16,1,3600]{2,0,1:T(8,128)(2,1)S(1)}, bf16[16,1,3600]{2,0,1:T(8,128)(2,1)S(1)}, u32[]{:S(2)}, u32[]{:S(2)}) collective-permute-start(bf16[16,1,3600]{2,0,1:T(8,128)(2,1)S(1)} %get-tuple-element.14), channel_id=1, source_target_pairs={{0,32},{32,64},{64,96},{96,128},{128,160},{160,192},{192,224},{224... | collective-permute-start | bytes 345608 | tf_op jit(solution)/shard_map/ppermute | solution.py:14
  24.8 4.7 %collective-permute-start.1 = (bf16[16,1,3600]{2,0,1:T(8,128)(2,1)S(1)}, bf16[16,1,3600]{2,0,1:T(8,128)(2,1)S(1)}, u32[]{:S(2)}, u32[]{:S(2)}) collective-permute-start(bf16[16,1,3600]{2,0,1:T(8,128)(2,1)S(1)} %get-tuple-element.15), channel_id=1, source_target_pairs={{32,0},{64,32},{96,64},{128,96},{160,128},{192,160},{224,192},{256... | collective-permute-start | bytes 345608 | tf_op jit(solution)/shard_map/ppermute | solution.py:17
  29.5 1.4 %collective-permute-done.1 = bf16[16,1,3600]{2,0,1:T(8,128)(2,1)S(1)} collective-permute-done((bf16[16,1,3600]{2,0,1:T(8,128)(2,1)S(1)}, bf16[16,1,3600]{2,0,1:T(8,128)(2,1)S(1)}, u32[]{:S(2)}, u32[]{:S(2)}) %collective-permute-start.1) | collective-permute-done | bytes 115232 | tf_op jit(solution)/shard_map/ppermute | solution.py:17
  31.4 3.2 %collective-permute-start.2 = (bf16[1,18,3600]{2,1,0:T(8,128)(2,1)S(1)}, bf16[1,18,3600]{2,1,0:T(8,128)(2,1)S(1)}, u32[]{:S(2)}, u32[]{:S(2)}) collective-permute-start(bf16[1,18,3600]{2,1,0:T(8,128)(2,1)S(1)} %copy.22), channel_id=1, source_target_pairs={{0,1},{1,2},{2,3},{3,4},{4,5},{5,6},{6,7},{7,8},{8,9},{9,10},{10,1... | collective-permute-start | bytes 388808 | tf_op jit(solution)/shard_map/ppermute | solution.py:14
  34.6 1.3 collective-permute-start.3
  36.3 0.7 collective-permute-done.2
  37.2 4.3 %collective-permute-done.3 = bf16[1,18,3600]{2,1,0:T(8,128)(2,1)S(1)} collective-permute-done((bf16[1,18,3600]{2,1,0:T(8,128)(2,1)S(1)}, bf16[1,18,3600]{2,1,0:T(8,128)(2,1)S(1)}, u32[]{:S(2)}, u32[]{:S(2)}) %collective-permute-start.3) | collective-permute-done | bytes 129632 | tf_op jit(solution)/shard_map/ppermute | solution.py:17
  41.8 2.9 %maximum_maximum_fusion = (bf16[17,18,3600]{2,0,1:T(8,128)(2,1)S(1)}, bf16[17,18,3600]{2,0,1:T(8,128)(2,1)S(1)}) fusion(bf16[16,1,3600]{2,0,1:T(8,128)(2,1)S(1)} %collective-permute-done.1, bf16[16,16,3600]{2,0,1:T(8,128)(2,1)S(1)} %multiply_convert_fusion.1, bf16[16,1,3600]{2,0,1:T(8,128)(2,1)S(1)} %collective-permute-done, ...), kind=kLoop, calls=%fused_computation.7 | loop fusion | flops 17625600 | bytes 6739200 | tf_op jit(solution)/shard_map/concatenate | solution.py:18
  44.7 4.5 %multiply_reduce_fusion = (f32[16,16]{0,1:T(8,128)S(1)}, f32[16,16,3600]{2,0,1:T(8,128)S(1)}) fusion(bf16[17,18,3600]{2,0,1:T(8,128)(2,1)S(1)} %get-tuple-element.11, bf16[16,1,3600]{2,0,1:T(8,128)(2,1)S(1)} %collective-permute-done.1, bf16[16,16,3600]{2,0,1:T(8,128)(2,1)S(1)} %multiply_convert_fusion.1, bf16[16,1,3600]{2,0,1:T(8,128)(2,1)S(1)} %collective-permute-done, ...), kind=kLoop, calls=%fused_computation.3 | loop fusion | flops 19353344 | bytes 16820224 | tf_op jit(solution)/shard_map/reduce_sum | solution.py:23
  49.8 1.9 %convolution_convert_fusion = bf16[128,3600]{0,1:T(8,128)(2,1)} fusion(bf16[256,3600]{1,0:T(8,128)(2,1)S(1)} %bitcast.5, s32[256]{0:T(256)S(1)} %select_reduce_fusion, pred[256]{0:T(512)(128)(4,1)S(1)} %eq.51), kind=kOutput, calls=%fused_computation | convolution fusion | flops 236455936 | bytes 2766080 | tf_op jit(solution)/shard_map/dot_general | solution.py:58
  51.7 1.6 %copy.27 = bf16[128,3600]{1,0:T(8,128)(2,1)S(1)} copy(bf16[128,3600]{0,1:T(8,128)(2,1)} %convolution_convert_fusion) | data formatting | bytes 1843200 | tf_op jit(solution)/shard_map/convert_element_type | solution.py:60
  53.3 1.2 reshape.68
  54.5 35.3 %all_to_all.5 = bf16[32,4,3600]{2,1,0:T(4,128)(2,1)S(1)} all-to-all(bf16[32,4,3600]{2,1,0:T(4,128)(2,1)} %reshape.68), channel_id=1, replica_groups=mesh['dict'=16,'scan'=32] {'scan'}, dimensions={0} | all-to-all | bytes 1843200 | tf_op jit(solution)/shard_map/all_to_all | solution.py:63
  90.2 25.1 %all-gather.1 = bf16[16,4,3600]{2,1,0:T(4,128)(2,1)S(1)} all-gather(bf16[1,4,3600]{2,1,0:T(4,128)(2,1)S(1)} %bitcast.7), channel_id=2, replica_groups=mesh['dict'=16,'scan'=32] {'dict'}, dimensions={0}, use_global_device_ids=true | all-gather | bytes 489600 | tf_op jit(solution)/shard_map/all_gather | solution.py:65
  115.6 0.7 broadcast_multiply_fusion
  116.3 1.4 %all-gather.4.cloned.1.call-done = bf16[2048,3600]{0,1:T(8,128)(2,1)} async-done(((bf16[128,3600]{0,1:T(8,128)(2,1)}), bf16[2048,3600]{0,1:T(8,128)(2,1)}) %all-gather.4.cloned.1.call-update) | async-done | bytes 14745616 | tf_op jit(solution)/shard_map/all_gather | solution.py:38
  117.7 8.2 %convolution_reduce_fusion = f32[256]{0:T(256)S(1)} fusion(bf16[256,3600]{1,0:T(8,128)(2,1)S(1)} %bitcast.6, bf16[2048,3600]{0,1:T(8,128)(2,1)} %all-gather.4.cloned.1.call-done), kind=kOutput, calls=%fused_computation.18 | convolution fusion | flops 3775397632 | bytes 16589824 | tf_op jit(solution)/shard_map/dot_general | solution.py:69
  126.0 0.7 mul.68
  (35 shorter events, 2.8 us)
Async XLA Ops:
  7.2 5.8 %copy-start.1 = (f32[3600]{0:T(1024)S(1)}, f32[3600]{0:T(1024)}, u32[]{:S(2)}) copy-start(f32[3600]{0:T(1024)} %param.7) | copy-start | bytes 43204
  7.2 110.5 %all-gather.4.cloned.1.call-start = ((), (), s32[]{:S(2)}) async-start(), calls=%async_computation.1 | async-start | bytes 15667200 | tf_op jit(solution)/shard_map/all_gather | solution.py:38
  13.0 3.4 %copy-start = (f32[16,16,3600]{2,1,0:T(8,128)S(1)}, f32[16,16,3600]{2,1,0:T(8,128)}, u32[]{:S(2)}) copy-start(f32[16,16,3600]{2,1,0:T(8,128)} %param.6) | copy-start | bytes 11059204
  17.6 18.3 %copy-start.2 = (s32[16,16]{1,0:T(8,128)S(1)}, s32[16,16]{1,0:T(8,128)}, u32[]{:S(2)}) copy-start(s32[16,16]{1,0:T(8,128)} %param.10) | copy-start | bytes 3076
  17.7 18.4 %copy-start.3 = (s32[16,16]{1,0:T(8,128)S(1)}, s32[16,16]{1,0:T(8,128)}, u32[]{:S(2)}) copy-start(s32[16,16]{1,0:T(8,128)} %param.9) | copy-start | bytes 3076
  17.7 18.5 %copy-start.4 = (s32[128]{0:T(128)S(1)}, s32[128]{0:T(128)}, u32[]{:S(2)}) copy-start(s32[128]{0:T(128)} %param.11) | copy-start | bytes 1540
  19.4 10.1 %collective-permute-start = (bf16[16,1,3600]{2,0,1:T(8,128)(2,1)S(1)}, bf16[16,1,3600]{2,0,1:T(8,128)(2,1)S(1)}, u32[]{:S(2)}, u32[]{:S(2)}) collective-permute-start(bf16[16,1,3600]{2,0,1:T(8,128)(2,1)S(1)} %get-tuple-element.14), channel_id=1, source_target_pairs={{0,32},{32,64},{64,96},{96,128},{128,160},{160,192},{192,224},{224... | collective-permute-start | bytes 345608 | tf_op jit(solution)/shard_map/ppermute | solution.py:14
  24.8 6.2 %collective-permute-start.1 = (bf16[16,1,3600]{2,0,1:T(8,128)(2,1)S(1)}, bf16[16,1,3600]{2,0,1:T(8,128)(2,1)S(1)}, u32[]{:S(2)}, u32[]{:S(2)}) collective-permute-start(bf16[16,1,3600]{2,0,1:T(8,128)(2,1)S(1)} %get-tuple-element.15), channel_id=1, source_target_pairs={{32,0},{64,32},{96,64},{128,96},{160,128},{192,160},{224,192},{256... | collective-permute-start | bytes 345608 | tf_op jit(solution)/shard_map/ppermute | solution.py:17
  31.4 5.6 %collective-permute-start.2 = (bf16[1,18,3600]{2,1,0:T(8,128)(2,1)S(1)}, bf16[1,18,3600]{2,1,0:T(8,128)(2,1)S(1)}, u32[]{:S(2)}, u32[]{:S(2)}) collective-permute-start(bf16[1,18,3600]{2,1,0:T(8,128)(2,1)S(1)} %copy.22), channel_id=1, source_target_pairs={{0,1},{1,2},{2,3},{3,4},{4,5},{5,6},{6,7},{7,8},{8,9},{9,10},{10,1... | collective-permute-start | bytes 388808 | tf_op jit(solution)/shard_map/ppermute | solution.py:14
  34.6 6.9 %collective-permute-start.3 = (bf16[1,18,3600]{2,1,0:T(8,128)(2,1)S(1)}, bf16[1,18,3600]{2,1,0:T(8,128)(2,1)S(1)}, u32[]{:S(2)}, u32[]{:S(2)}) collective-permute-start(bf16[1,18,3600]{2,1,0:T(8,128)(2,1)S(1)} %copy.24), channel_id=1, source_target_pairs={{1,0},{2,1},{3,2},{4,3},{5,4},{6,5},{7,6},{8,7},{9,8},{10,9},{11,1... | collective-permute-start | bytes 388808 | tf_op jit(solution)/shard_map/ppermute | solution.py:17
Sparse Core Ops, SparseCore 0:
  13.1 104.5 all-gather.3

commit v2 on v1

v2 whole, which is shorter than its diff:
```python
import math

import jax
import jax.numpy as jnp
from jax import lax
from jax.experimental import pallas as pl
from jax.experimental.pallas import tpu as pltpu
from jax.sharding import Mesh
from jax.sharding import PartitionSpec as P

SCAN = ("x", "y")
DICT = ("z", "core")
EVERY = ("z", "core", "x", "y")
EPS = 1e-05
VMEM = pltpu.VMEM


def normalise_templates(panel_ref, out_ref, whole_ref):
    panel = panel_ref[...].astype(jnp.float32)
    pixels = panel.shape[0]
    panel = panel - jnp.sum(panel, axis=0, keepdims=True) * (1.0 / pixels)
    mean_square = jnp.sum(panel * panel, axis=0, keepdims=True) * (1.0 / pixels)
    panel = panel * lax.rsqrt(mean_square + EPS)
    whole_ref[...] = panel.T.astype(jnp.bfloat16)
    held = out_ref.shape[0]
    parity = (lax.axis_index("x") + lax.axis_index("y")) & 1
    out_ref[...] = whole_ref[pl.ds(pl.multiple_of(parity * held, held), held), :]


def filter_tile(background_ref, tile_ref, out_ref, low_ref, high_ref, low, high):
    background = background_ref[...]
    rows, _, pixels = tile_ref.shape
    for row in range(rows):
        values = tile_ref[row] - background
        values = values - jnp.sum(values, axis=-1, keepdims=True) * (1.0 / pixels)
        mean_square = jnp.sum(values * values, axis=-1, keepdims=True) * (1.0 / pixels)
        values = (values * lax.rsqrt(mean_square + EPS)).astype(jnp.bfloat16)
        out_ref[row] = values
        low[row : row + 1, :] = values[:1].astype(jnp.float32)
        high[row : row + 1, :] = values[-1:].astype(jnp.float32)
    low_ref[...] = low[...].astype(jnp.bfloat16)
    high_ref[...] = high[...].astype(jnp.bfloat16)


def neighbour_sums(
    point_row_ref, tile_ref, low_ref, high_ref, above_ref, below_ref, out_ref, sums_ref, low_pad, high_pad, shift, ends
):
    rows, cols, pixels = tile_ref.shape
    above, below = above_ref[...].astype(jnp.float32), below_ref[...].astype(jnp.float32)
    for pad, side_ref, corner in ((low_pad, low_ref, cols), (high_pad, high_ref, cols + 1)):
        pad[0:1, :] = above[corner : corner + 1]
        pad[1 : rows + 1, :] = side_ref[...].astype(jnp.float32)
        pad[rows + 1 : rows + 2, :] = below[corner : corner + 1]

    for row in range(rows):
        for side, pad in enumerate((low_pad, high_pad)):
            ends[row, side : side + 1, :] = pad[row : row + 1, :] + pad[row + 1 : row + 2, :] + pad[row + 2 : row + 3, :]

    def one_row(row, before, middle, after):
        column = before + middle + after
        shift[7:8, :] = ends[row, 0:1, :]
        shift[8 : 8 + cols, :] = column
        shift[8 + cols : 9 + cols, :] = ends[row, 1:2, :]
        total = column + shift[7 : 7 + cols, :] + shift[9 : 9 + cols, :]
        mean_square = jnp.sum(total * total, axis=-1, keepdims=True) * (1.0 / pixels)
        values = (total * lax.rsqrt(mean_square + EPS)).astype(jnp.bfloat16)
        out_ref[pl.ds(pl.multiple_of(row * cols, cols), cols), :] = values

    def line(row):
        return tile_ref[row].astype(jnp.float32)

    one_row(0, above[:cols], line(0), line(1))

    def inner(row, carry):
        one_row(row, line(row - 1), line(row), line(row + 1))
        return carry

    lax.fori_loop(1, rows - 1, inner, 0)
    one_row(rows - 1, line(rows - 2), line(rows - 1), below[:cols])
    grains = sums_ref.shape[0]
    k = lax.broadcasted_iota(jnp.int32, (grains, rows * cols), 0)
    half = grains // 2
    grain = (k % half) // 2 * 4 + k // half * 2 + k % 2
    selector = jnp.where(grain == point_row_ref[...], 1.0, 0.0).astype(jnp.bfloat16)
    step = 1024
    for start in range(0, pixels, step):
        stop = min(start + step, pixels)
        sums_ref[:, start:stop] = jnp.dot(
            selector, out_ref[:, start:stop], preferred_element_type=jnp.float32
        ).astype(jnp.bfloat16)


def best_scores(own_ref, other_ref, panel_ref, own_best_ref, other_best_ref):
    first = pl.program_id(0) == 0
    for points_ref, best_ref in ((own_ref, own_best_ref), (other_ref, other_best_ref)):
        scores = lax.dot_general(
            panel_ref[...],
            points_ref[...],
            (((1,), (1,)), ((), ())),
            preferred_element_type=jnp.float32,
        )
        best = jnp.max(scores, axis=0, keepdims=True)

        @pl.when(first)
        def _(best=best, best_ref=best_ref):
            best_ref[...] = best

        @pl.when(jnp.logical_not(first))
        def _(best=best, best_ref=best_ref):
            best_ref[...] = jnp.maximum(best_ref[...], best)


def params(mebibytes):
    return pltpu.CompilerParams(vmem_limit_bytes=mebibytes << 20)


def shards(patterns, background, templates, grain_id, keep_mask, grain_row):
    tile_rows, tile_cols, pixels = patterns.shape
    points = tile_rows * tile_cols
    held = templates.shape[0] // 2
    bf16, f32 = jnp.bfloat16, jnp.float32

    panel = pl.pallas_call(
        normalise_templates,
        out_shape=jax.ShapeDtypeStruct((held, pixels), bf16),
        in_specs=[pl.BlockSpec(memory_space=VMEM)],
        out_specs=pl.BlockSpec(memory_space=VMEM),
        scratch_shapes=[VMEM((2 * held, pixels), bf16)],
        compiler_params=params(10),
        name="normalise_templates",
    )(templates.T)
    panels = lax.all_gather(panel, DICT, axis=0, tiled=True)

    background, panel = lax.optimization_barrier((background, panel))
    block = 8
    filtered, low_edge, high_edge = pl.pallas_call(
        filter_tile,
        grid=(tile_rows // block,),
        out_shape=(
            jax.ShapeDtypeStruct((tile_rows, tile_cols, pixels), bf16),
            jax.ShapeDtypeStruct((tile_rows, pixels), bf16),
            jax.ShapeDtypeStruct((tile_rows, pixels), bf16),
        ),
        in_specs=[
            pl.BlockSpec((1, pixels), lambda i: (0, 0)),
            pl.BlockSpec((block, tile_cols, pixels), lambda i: (i, 0, 0)),
        ],
        out_specs=(
            pl.BlockSpec((block, tile_cols, pixels), lambda i: (i, 0, 0)),
            pl.BlockSpec((block, pixels), lambda i: (i, 0)),
            pl.BlockSpec((block, pixels), lambda i: (i, 0)),
        ),
        scratch_shapes=[VMEM((block, pixels), f32)] * 2,
        compiler_params=params(56),
        name="filter_tile",
    )(background.reshape(1, pixels), patterns)
    columns = lax.axis_size(DICT)
    forward = [(i, i + 1) for i in range(columns - 1)]
    backward = [(i + 1, i) for i in range(columns - 1)]
    low = lax.ppermute(high_edge, DICT, forward)
    high = lax.ppermute(low_edge, DICT, backward)

    def strip(row):
        return jnp.concatenate([filtered[row], low[row : row + 1], high[row : row + 1]], axis=0)

    lines = lax.axis_size(SCAN)
    forward = [(i, i + 1) for i in range(lines - 1)]
    backward = [(i + 1, i) for i in range(lines - 1)]
    above = lax.ppermute(strip(tile_rows - 1), SCAN, forward)
    below = lax.ppermute(strip(0), SCAN, backward)

    grain_count = grain_row.shape[0]
    grain_index = jnp.arange(grain_count, dtype=jnp.int32)
    matches = grain_id.reshape(-1)[:, None] == grain_index[None, :]
    point_row = jnp.sum(jnp.where(matches, grain_row[None, :], 0), axis=1)
    point_row = jnp.where(keep_mask.reshape(-1) == 1, point_row, -1).reshape(1, points)

    indexed, sums = pl.pallas_call(
        neighbour_sums,
        out_shape=(
            jax.ShapeDtypeStruct((points, pixels), bf16),
            jax.ShapeDtypeStruct((grain_count, pixels), bf16),
        ),
        in_specs=[pl.BlockSpec(memory_space=VMEM)] * 6,
        out_specs=[pl.BlockSpec(memory_space=VMEM)] * 2,
        scratch_shapes=[VMEM((24, pixels), f32)] * 2
        + [VMEM((32, pixels), f32), VMEM((tile_rows, 2, pixels), f32)],
        compiler_params=params(12),
        name="neighbour_sums",
    )(point_row, filtered, low, high, above, below)

    xs, ys = lax.axis_size("x"), lax.axis_size("y")
    trade = []
    for z in range(lax.axis_size("z")):
        for x in range(xs):
            for y in range(ys):
                at = z * 2 * xs * ys
                trade.append((at + x * ys + y, at + (x ^ 1) * ys + y))
                trade.append((at + xs * ys + x * ys + y, at + xs * ys + x * ys + (y ^ 1)))
    other = lax.ppermute(indexed.reshape(patterns.shape), EVERY, trade).reshape(points, pixels)

    halves = lax.all_to_all(
        sums.reshape(2, grain_count // 2, pixels), "core", 0, 0, tiled=True
    )
    chip_sums = jnp.sum(halves.astype(f32), axis=0).astype(bf16)
    parts = lax.all_to_all(chip_sums.reshape(lines, -1, pixels), SCAN, 0, 0, tiled=True)
    group_total = jnp.sum(parts.astype(f32), axis=0).astype(bf16)

    block = 256
    scored, group_total = lax.optimization_barrier((other, group_total))
    own_best, other_best = pl.pallas_call(
        best_scores,
        grid=(panels.shape[0] // block,),
        out_shape=(jax.ShapeDtypeStruct((1, points), f32),) * 2,
        in_specs=[
            pl.BlockSpec((points, pixels), lambda i: (0, 0)),
            pl.BlockSpec((points, pixels), lambda i: (0, 0)),
            pl.BlockSpec((block, pixels), lambda i: (i, 0)),
        ],
        out_specs=(pl.BlockSpec((1, points), lambda i: (0, 0)),) * 2,
        compiler_params=params(56),
        name="best_scores",
    )(indexed, scored, panels)
    returned = lax.ppermute(other_best, EVERY, trade)
    other_best, group_total = lax.optimization_barrier((other_best, group_total))
    group_totals = lax.all_gather(group_total, DICT, axis=0, tiled=False)
    returned, group_totals = lax.optimization_barrier((returned, group_totals))
    zs = lax.axis_size("z")
    group_totals = group_totals.reshape((zs, 2) + group_total.shape).astype(f32)
    grain_total = jnp.sum(group_totals, axis=0).reshape(-1, pixels)
    mean_square = jnp.mean(grain_total * grain_total, axis=-1, keepdims=True)
    grain_patterns = grain_total * lax.rsqrt(mean_square + EPS)
    best = jnp.maximum(own_best, returned)
    max_score = (best * (1.0 / math.sqrt(pixels))).reshape(tile_rows, tile_cols)
    return (max_score, grain_patterns)


def solution(mesh):
    groups, lines = mesh.shape["dict"], mesh.shape["scan"]
    fine = Mesh(mesh.devices.reshape(groups // 2, 2, lines // 8, 8), EVERY)
    return jax.shard_map(
        shards,
        mesh=fine,
        in_specs=(
            P(SCAN, DICT, None),
            P(),
            P(DICT, None),
            P(SCAN, DICT),
            P(SCAN, DICT),
            P(),
        ),
        out_specs=(P(SCAN, DICT), P(SCAN, None)),
        check_vma=False,
    )
```

time: 134 us -> 132 us (0.985)
  Pallas kernels: 0 us -> 24 us
  other arithmetic: 21.8 us -> 2.77 us
  matrix products: 10.1 us -> 0 us
  starting transfers between devices: 14.6 us -> 22.6 us
  waiting for transfers between devices: 7.86 us -> 4.03 us
  blocking collectives: 60.4 us -> 57.7 us
  local copies, waits for them, and re-layouts: 4.43 us -> 6.3 us
    pallas_call x0 -> x4, Pallas kernels: none -> 24 us  [the longest x1 13 us: shards(): pl.pallas_call(best_scores, grid=(panels.shape[0] // block,), out_shape=(...]
    reduce_sum x8 -> x4, other arithmetic: 13.2 us -> 1.08 us  [the longest x1 0.39 us: shards(): group_total = jnp.sum(parts.astype(f32), axis=0).astype(bf16)]
    dot_general x2 -> x0, matrix products: 10.1 us -> none  [the longest x1 8.24 us: shards(): lax.dot_general(indexed, panels, (((1,), (1,)), ((), ())), preferred_elem...]
    ppermute x4 -> x6, starting transfers between devices: 14.6 us -> 22.6 us  [the longest x1 5.38 us: shards(): low = lax.ppermute(high_edge, DICT, forward)]
    convert_element_type x3 -> x0, other arithmetic: 4.35 us -> none  [the longest x1 2.36 us: shards(): unit_panel = unit_rows(centered_panel).astype(jnp.bfloat16)]
    all_gather x1, blocking collectives: 25.1 us -> 21.6 us  [shards(): group_totals = lax.all_gather(group_total, DICT, axis=0, tiled=False)]
    concatenate x1 -> x2, other arithmetic: 2.87 us -> 0.09 us  [strip(): jnp.concatenate([filtered[row], low[row:row + 1], high[row:row + 1]], axi...]
    unnamed x10 -> x12, local copies, waits for them, and re-layouts: 0.03 us -> 2.77 us
  transfers between devices with their start and end apart: 5 -> 7, of which waited for: 4 -> 3; matrix products, arithmetic and copies ran while one was open for 16% -> 3% of each run, Pallas kernels for 0% -> 7%
where the time goes in v2:
time: 132 us
  blocking collectives  57.7 us (44%)
  Pallas kernels  24 us (18%)
  starting transfers between devices  22.6 us (17%)
  between operations  14.2 us (11%)
  local copies, waits for them, and re-layouts  6.3 us (5%)
  waiting for transfers between devices  4.03 us (3%)
  other arithmetic  2.77 us (2%)
    all_to_all x1, blocking collectives, shards(): lax.all_to_all(chip_sums.reshape(lines, -1, pixels), SCAN, 0, 0, tiled=True)  29.9 us
    all_gather x1, blocking collectives, shards(): group_totals = lax.all_gather(group_total, DICT, axis=0, tiled=False)  21.6 us
    pallas_call x1, Pallas kernels, shards(): pl.pallas_call(best_scores, grid=(panels.shape[0] // block,), out_shape=(...  13 us
    all_to_all x1, blocking collectives, shards(): lax.all_to_all(sums.reshape(2, grain_count // 2, pixels), 'core', 0, 0, t...  6.24 us
    ppermute x1, starting transfers between devices, shards(): low = lax.ppermute(high_edge, DICT, forward)  5.38 us
    ppermute x1, starting transfers between devices, shards(): high = lax.ppermute(low_edge, DICT, backward)  4.69 us
    pallas_call x1, Pallas kernels, shards(): pl.pallas_call(neighbour_sums, out_shape=(jax.ShapeDtypeStruct((points, p...  4.49 us
    pallas_call x1, Pallas kernels, shards(): pl.pallas_call(filter_tile, grid=(tile_rows // block,), out_shape=(jax.Sh...  4.29 us
  transfers between devices with their start and end apart: 7, of which 3 were waited for; matrix products, arithmetic and copies ran while one was open for 3% of the time, Pallas kernels for 7%

profile of v2, /device:TPU:1, one launch (start us, length us, event | category | flops | bytes accessed | tf_op | source)
XLA Modules:
  0.0 131.6 jit_solution(17544266505276667380)
XLA Ops:
  7.2 1.2 copy-done.2
  8.4 2.2 %normalise_templates.1 = bf16[64,3600]{1,0:T(8,128)(2,1)} custom-call(bf16[3600,128]{1,0:T(8,128)(2,1)S(1)} %bitcast.14), custom_call_target="tpu_custom_call" | custom-call | tf_op jit(solution)/shard_map/normalise_templates/pallas_call | solution.py:123
  10.7 1.3 %reshape.68.background_ref = f32[1,3600]{1,0:T(1,128)} reshape(f32[3600]{0:T(1024)} %param.7) | data formatting | bytes 28800 | tf_op jit(solution)/shard_map/reshape | solution.py:156
  12.0 4.3 %filter_tile.1 = (bf16[16,16,3600]{2,1,0:T(8,128)(2,1)}, bf16[16,3600]{1,0:T(8,128)(2,1)}, bf16[16,3600]{1,0:T(8,128)(2,1)}) custom-call(f32[1,3600]{1,0:T(1,128)} %reshape.68.background_ref, f32[16,16,3600]{2,1,0:T(8,128)} %tile_ref.1), custom_call_target="tpu_custom_call" | custom-call | tf_op jit(solution)/shard_map/filter_tile/pallas_call | solution.py:136
  16.3 5.4 %collective-permute-start = (bf16[16,3600]{1,0:T(8,128)(2,1)}, bf16[16,3600]{1,0:T(8,128)(2,1)S(1)}, u32[]{:S(2)}, u32[]{:S(2)}) collective-permute-start(bf16[16,3600]{1,0:T(8,128)(2,1)} %get-tuple-element.17), channel_id=1, source_target_pairs={{0,32},{32,64},{64,96},{96,128},{128,160},{160,192},{192,224},{224... | collective-permute-start | bytes 345608 | tf_op jit(solution)/shard_map/ppermute | solution.py:160
  21.7 4.7 %collective-permute-start.1 = (bf16[16,3600]{1,0:T(8,128)(2,1)}, bf16[16,3600]{1,0:T(8,128)(2,1)S(1)}, u32[]{:S(2)}, u32[]{:S(2)}) collective-permute-start(bf16[16,3600]{1,0:T(8,128)(2,1)} %get-tuple-element.18), channel_id=1, source_target_pairs={{32,0},{64,32},{96,64},{128,96},{160,128},{192,160},{224,192},{256... | collective-permute-start | bytes 345608 | tf_op jit(solution)/shard_map/ppermute | solution.py:161
  26.6 1.0 slice_bitcast_fusion
  28.1 1.3 collective-permute-start.3
  29.5 4.0 %collective-permute-start.2 = (bf16[18,3600]{1,0:T(8,128)(2,1)S(1)}, bf16[18,3600]{1,0:T(8,128)(2,1)S(1)}, u32[]{:S(2)}, u32[]{:S(2)}) collective-permute-start(bf16[18,3600]{1,0:T(8,128)(2,1)S(1)} %pad_maximum_fusion), channel_id=1, source_target_pairs={{0,1},{1,2},{2,3},{3,4},{4,5},{5,6},{6,7},{7,8},{8,9},{9,10},{10,1... | collective-permute-start | bytes 388808 | tf_op jit(solution)/shard_map/ppermute | solution.py:169
  33.5 2.8 %collective-permute-done.3.below_ref = bf16[18,3600]{1,0:T(8,128)(2,1)S(1)} collective-permute-done((bf16[18,3600]{1,0:T(8,128)(2,1)S(1)}, bf16[18,3600]{1,0:T(8,128)(2,1)S(1)}, u32[]{:S(2)}, u32[]{:S(2)}) %collective-permute-start.3) | collective-permute-done | bytes 129632 | tf_op jit(solution)/shard_map/ppermute | solution.py:170
  36.3 0.9 collective-permute-done.2.above_ref
  37.2 1.6 %copy-done = bf16[16,16,3600]{2,1,0:T(8,128)(2,1)S(1)} copy-done((bf16[16,16,3600]{2,1,0:T(8,128)(2,1)S(1)}, bf16[16,16,3600]{2,1,0:T(8,128)(2,1)}, u32[]{:S(2)}) %copy-start) | copy-done | bytes 1843224
  38.8 4.5 %neighbour_sums.1 = (bf16[256,3600]{1,0:T(8,128)(2,1)S(1)}, bf16[128,3600]{1,0:T(8,128)(2,1)S(1)}) custom-call(s32[1,256]{1,0:T(1,128)S(1)} %broadcast_select_fusion.point_row_ref, bf16[16,16,3600]{2,1,0:T(8,128)(2,1)S(1)} %copy-done, bf16[16,3600]{1,0:T(8,128)(2,1)S(1)} %collective-permute-done.low_ref, ...), custom_call_target="tpu_custom_call" | custom-call | tf_op jit(solution)/shard_map/neighbour_sums/pallas_call | solution.py:178
  43.3 4.2 %collective-permute-start.4 = (bf16[16,16,3600]{2,1,0:T(8,128)(2,1)S(1)}, bf16[16,16,3600]{2,1,0:T(8,128)(2,1)}, u32[]{:S(2)}, u32[]{:S(2)}) collective-permute-start(bf16[16,16,3600]{2,1,0:T(8,128)(2,1)S(1)} %bitcast.12), channel_id=1, source_target_pairs={{0,8},{32,33},{1,9},{33,32},{2,10},{34,35},{3,11},{35,34},{4,12},{... | collective-permute-start | bytes 5529608 | tf_op jit(solution)/shard_map/ppermute | solution.py:200
  47.5 6.2 %all_to_all.10 = bf16[2,64,3600]{2,1,0:T(8,128)(2,1)S(1)} all-to-all(bf16[2,64,3600]{2,1,0:T(8,128)(2,1)S(1)} %bitcast.13), channel_id=1, replica_groups=mesh['z'=8,'core'=2,'x'=4,'y'=8] {'core'}, dimensions={0} | all-to-all | bytes 1843200 | tf_op jit(solution)/shard_map/all_to_all | solution.py:202
  53.7 0.3 reduce_sum.55
  54.3 29.9 %all_to_all.11 = bf16[32,2,3600]{2,1,0:T(2,128)(2,1)S(1)} all-to-all(bf16[32,2,3600]{2,1,0:T(2,128)(2,1)S(1)} %reshape.72), channel_id=1, replica_groups=mesh['z'=8,'core'=2,'x'=4,'y'=8] {'x','y'}, dimensions={0} | all-to-all | bytes 921600 | tf_op jit(solution)/shard_map/all_to_all | solution.py:206
  84.2 0.4 reduce_sum.56
  84.6 13.0 %best_scores.1 = (f32[1,256]{1,0:T(1,128)}, f32[1,256]{1,0:T(1,128)}) custom-call(bf16[256,3600]{1,0:T(8,128)(2,1)} %copy-done.1, bf16[256,3600]{1,0:T(8,128)(2,1)} %bitcast.5.other_ref, bf16[1024,3600]{1,0:T(8,128)(2,1)} %all-gather.4.cloned.1.call-done.panel_ref), custom_call_target="tpu_custom_call" | custom-call | tf_op jit(solution)/shard_map/best_scores/pallas_call | solution.py:211
  97.6 3.0 %collective-permute-start.5 = (f32[1,256]{1,0:T(1,128)}, f32[1,256]{1,0:T(1,128)S(1)}, u32[]{:S(2)}, u32[]{:S(2)}) collective-permute-start(f32[1,256]{1,0:T(1,128)} %get-tuple-element.23), channel_id=1, source_target_pairs={{0,8},{32,33},{1,9},{33,32},{2,10},{34,35},{3,11},{35,34},{4,12},{... | collective-permute-start | bytes 3080 | tf_op jit(solution)/shard_map/ppermute | solution.py:224
  100.6 21.6 %all-gather.1 = bf16[16,2,3600]{2,1,0:T(2,128)(2,1)S(1)} all-gather(bf16[1,2,3600]{2,1,0:T(2,128)(2,1)S(1)} %bitcast.16), channel_id=2, replica_groups=mesh['z'=8,'core'=2,'x'=4,'y'=8] {'z','core'}, dimensions={0}, use_global_device_ids=true | all-gather | bytes 244800 | tf_op jit(solution)/shard_map/all_gather | solution.py:226
  122.7 0.7 multiply_reduce_fusion.1
  123.4 0.7 reshape.73
  124.1 0.7 broadcast_multiply_fusion
  (32 shorter events, 1.5 us)
Async XLA Ops:
  7.2 77.4 %all-gather.4.cloned.1.call-start = ((), (), s32[]{:S(2)}) async-start(), calls=%async_computation.2 | async-start | bytes 8077312 | tf_op jit(solution)/shard_map/all_gather | solution.py:132
  7.2 1.2 copy-start.2
  12.0 14.4 %copy-start.3 = (s32[16,16]{1,0:T(8,128)S(1)}, s32[16,16]{1,0:T(8,128)}, u32[]{:S(2)}) copy-start(s32[16,16]{1,0:T(8,128)} %param.10) | copy-start | bytes 3076
  12.0 14.5 %copy-start.4 = (s32[16,16]{1,0:T(8,128)S(1)}, s32[16,16]{1,0:T(8,128)}, u32[]{:S(2)}) copy-start(s32[16,16]{1,0:T(8,128)} %param.9) | copy-start | bytes 3076
  12.0 15.6 %copy-start.5 = (s32[128]{0:T(128)S(1)}, s32[128]{0:T(128)}, u32[]{:S(2)}) copy-start(s32[128]{0:T(128)} %param.11) | copy-start | bytes 1540
  16.3 11.5 %collective-permute-start = (bf16[16,3600]{1,0:T(8,128)(2,1)}, bf16[16,3600]{1,0:T(8,128)(2,1)S(1)}, u32[]{:S(2)}, u32[]{:S(2)}) collective-permute-start(bf16[16,3600]{1,0:T(8,128)(2,1)} %get-tuple-element.17), channel_id=1, source_target_pairs={{0,32},{32,64},{64,96},{96,128},{128,160},{160,192},{192,224},{224... | collective-permute-start | bytes 345608 | tf_op jit(solution)/shard_map/ppermute | solution.py:160
  21.7 6.4 %collective-permute-start.1 = (bf16[16,3600]{1,0:T(8,128)(2,1)}, bf16[16,3600]{1,0:T(8,128)(2,1)S(1)}, u32[]{:S(2)}, u32[]{:S(2)}) collective-permute-start(bf16[16,3600]{1,0:T(8,128)(2,1)} %get-tuple-element.18), channel_id=1, source_target_pairs={{32,0},{64,32},{96,64},{128,96},{160,128},{192,160},{224,192},{256... | collective-permute-start | bytes 345608 | tf_op jit(solution)/shard_map/ppermute | solution.py:161
  28.1 8.2 %collective-permute-start.3 = (bf16[18,3600]{1,0:T(8,128)(2,1)S(1)}, bf16[18,3600]{1,0:T(8,128)(2,1)S(1)}, u32[]{:S(2)}, u32[]{:S(2)}) collective-permute-start(bf16[18,3600]{1,0:T(8,128)(2,1)S(1)} %pad_maximum_fusion.1), channel_id=1, source_target_pairs={{1,0},{2,1},{3,2},{4,3},{5,4},{6,5},{7,6},{8,7},{9,8},{10,9},{11,1... | collective-permute-start | bytes 388808 | tf_op jit(solution)/shard_map/ppermute | solution.py:170
  29.5 7.7 %collective-permute-start.2 = (bf16[18,3600]{1,0:T(8,128)(2,1)S(1)}, bf16[18,3600]{1,0:T(8,128)(2,1)S(1)}, u32[]{:S(2)}, u32[]{:S(2)}) collective-permute-start(bf16[18,3600]{1,0:T(8,128)(2,1)S(1)} %pad_maximum_fusion), channel_id=1, source_target_pairs={{0,1},{1,2},{2,3},{3,4},{4,5},{5,6},{6,7},{7,8},{8,9},{9,10},{10,1... | collective-permute-start | bytes 388808 | tf_op jit(solution)/shard_map/ppermute | solution.py:169
  37.2 1.6 %copy-start = (bf16[16,16,3600]{2,1,0:T(8,128)(2,1)S(1)}, bf16[16,16,3600]{2,1,0:T(8,128)(2,1)}, u32[]{:S(2)}) copy-start(bf16[16,16,3600]{2,1,0:T(8,128)(2,1)} %get-tuple-element.16.tile_ref) | copy-start | bytes 5529604
  43.3 11.0 %copy-start.1 = (bf16[256,3600]{1,0:T(8,128)(2,1)}, bf16[256,3600]{1,0:T(8,128)(2,1)S(1)}, u32[]{:S(2)}) copy-start(bf16[256,3600]{1,0:T(8,128)(2,1)S(1)} %get-tuple-element.19.own_ref) | copy-start | bytes 5529604
  43.3 41.3 %collective-permute-start.4 = (bf16[16,16,3600]{2,1,0:T(8,128)(2,1)S(1)}, bf16[16,16,3600]{2,1,0:T(8,128)(2,1)}, u32[]{:S(2)}, u32[]{:S(2)}) collective-permute-start(bf16[16,16,3600]{2,1,0:T(8,128)(2,1)S(1)} %bitcast.12), channel_id=1, source_target_pairs={{0,8},{32,33},{1,9},{33,32},{2,10},{34,35},{3,11},{35,34},{4,12},{... | collective-permute-start | bytes 5529608 | tf_op jit(solution)/shard_map/ppermute | solution.py:200
  97.6 24.6 %collective-permute-start.5 = (f32[1,256]{1,0:T(1,128)}, f32[1,256]{1,0:T(1,128)S(1)}, u32[]{:S(2)}, u32[]{:S(2)}) collective-permute-start(f32[1,256]{1,0:T(1,128)} %get-tuple-element.23), channel_id=1, source_target_pairs={{0,8},{32,33},{1,9},{33,32},{2,10},{34,35},{3,11},{35,34},{4,12},{... | collective-permute-start | bytes 3080 | tf_op jit(solution)/shard_map/ppermute | solution.py:224
Sparse Core Ops, SparseCore 0:
  10.8 61.5 all-gather.3

commit v3 on v2

--- a/solution.py
+++ b/solution.py
@@ -23,12 +23,12 @@
     panel = panel * lax.rsqrt(mean_square + EPS)
     whole_ref[...] = panel.T.astype(jnp.bfloat16)
     held = out_ref.shape[0]
-    parity = (lax.axis_index("x") + lax.axis_index("y")) & 1
+    parity = lax.axis_index("x") & 1
     out_ref[...] = whole_ref[pl.ds(pl.multiple_of(parity * held, held), held), :]
 
 
 def filter_tile(background_ref, tile_ref, out_ref, low_ref, high_ref, low, high):
-    background = background_ref[...]
+    background = background_ref[...].reshape(1, -1)
     rows, _, pixels = tile_ref.shape
     for row in range(rows):
         values = tile_ref[row] - background
@@ -90,24 +90,45 @@
         ).astype(jnp.bfloat16)
 
 
-def best_scores(own_ref, other_ref, panel_ref, own_best_ref, other_best_ref):
-    first = pl.program_id(0) == 0
-    for points_ref, best_ref in ((own_ref, own_best_ref), (other_ref, other_best_ref)):
-        scores = lax.dot_general(
-            panel_ref[...],
-            points_ref[...],
-            (((1,), (1,)), ((), ())),
-            preferred_element_type=jnp.float32,
-        )
-        best = jnp.max(scores, axis=0, keepdims=True)
-
-        @pl.when(first)
-        def _(best=best, best_ref=best_ref):
-            best_ref[...] = best
-
-        @pl.when(jnp.logical_not(first))
-        def _(best=best, best_ref=best_ref):
-            best_ref[...] = jnp.maximum(best_ref[...], best)
+def best_scores(own_ref, other_ref, panel_ref, own_best_ref, other_best_ref, points_ref, best_ref):
+    points = own_ref.shape[0]
+    step = pl.program_id(0)
+
+    @pl.when(step == 0)
+    def _():
+        points_ref[:points, :] = own_ref[...]
+        points_ref[points:, :] = other_ref[...]
+        best_ref[...] = jnp.full(best_ref.shape, -jnp.inf, jnp.float32)
+
+    scores = lax.dot_general(
+        points_ref[...], panel_ref[...], (((1,), (1,)), ((), ())), preferred_element_type=jnp.float32
+    )
+    lanes = best_ref.shape[1]
+    best = best_ref[...]
+    for start in range(0, scores.shape[1], lanes):
+        best = jnp.maximum(best, scores[:, start : start + lanes])
+    best_ref[...] = best
+
+    @pl.when(step == pl.num_programs(0) - 1)
+    def _():
+        best = jnp.max(best_ref[...].T, axis=0, keepdims=True)
+        own_best_ref[...] = best[:, :points]
+        other_best_ref[...] = best[:, points:]
+
+
+def finish(own_best_ref, returned_ref, totals_ref, max_score_ref, patterns_ref):
+    pixels = patterns_ref.shape[1]
+    rows, cols = max_score_ref.shape
+    best = jnp.maximum(own_best_ref[...], returned_ref[...]) * (1.0 / math.sqrt(pixels))
+    for row in range(rows):
+        max_score_ref[row : row + 1, :] = best[:, row * cols : (row + 1) * cols]
+    groups = totals_ref.shape[0] // 2
+    for core in range(2):
+        total = totals_ref[core].astype(jnp.float32)
+        for group in range(1, groups):
+            total = total + totals_ref[2 * group + core].astype(jnp.float32)
+        mean_square = jnp.sum(total * total, axis=-1, keepdims=True) * (1.0 / pixels)
+        patterns_ref[2 * core : 2 * core + 2, :] = total * lax.rsqrt(mean_square + EPS)
 
 
 def params(mebibytes):
@@ -131,7 +152,7 @@
     )(templates.T)
     panels = lax.all_gather(panel, DICT, axis=0, tiled=True)
 
-    background, panel = lax.optimization_barrier((background, panel))
+    patterns, panel = lax.optimization_barrier((patterns, panel))
     block = 8
     filtered, low_edge, high_edge = pl.pallas_call(
         filter_tile,
@@ -142,7 +163,7 @@
             jax.ShapeDtypeStruct((tile_rows, pixels), bf16),
         ),
         in_specs=[
-            pl.BlockSpec((1, pixels), lambda i: (0, 0)),
+            pl.BlockSpec((pixels,), lambda i: (0,)),
             pl.BlockSpec((block, tile_cols, pixels), lambda i: (i, 0, 0)),
         ],
         out_specs=(
@@ -151,9 +172,9 @@
             pl.BlockSpec((block, pixels), lambda i: (i, 0)),
         ),
         scratch_shapes=[VMEM((block, pixels), f32)] * 2,
-        compiler_params=params(56),
+        compiler_params=params(16),
         name="filter_tile",
-    )(background.reshape(1, pixels), patterns)
+    )(background, pltpu.with_memory_space_constraint(patterns, pltpu.HBM))
     columns = lax.axis_size(DICT)
     forward = [(i, i + 1) for i in range(columns - 1)]
     backward = [(i + 1, i) for i in range(columns - 1)]
@@ -194,9 +215,10 @@
     for z in range(lax.axis_size("z")):
         for x in range(xs):
             for y in range(ys):
-                at = z * 2 * xs * ys
-                trade.append((at + x * ys + y, at + (x ^ 1) * ys + y))
-                trade.append((at + xs * ys + x * ys + y, at + xs * ys + x * ys + (y ^ 1)))
+                for core in range(2):
+                    at = (z * 2 + core) * xs
+                    partner = (((x + core) ^ 1) - core) % xs
+                    trade.append(((at + x) * ys + y, (at + partner) * ys + y))
     other = lax.ppermute(indexed.reshape(patterns.shape), EVERY, trade).reshape(points, pixels)
 
     halves = lax.all_to_all(
@@ -206,7 +228,7 @@
     parts = lax.all_to_all(chip_sums.reshape(lines, -1, pixels), SCAN, 0, 0, tiled=True)
     group_total = jnp.sum(parts.astype(f32), axis=0).astype(bf16)
 
-    block = 256
+    block = 512
     scored, group_total = lax.optimization_barrier((other, group_total))
     own_best, other_best = pl.pallas_call(
         best_scores,
@@ -218,21 +240,25 @@
             pl.BlockSpec((block, pixels), lambda i: (i, 0)),
         ],
         out_specs=(pl.BlockSpec((1, points), lambda i: (0, 0)),) * 2,
-        compiler_params=params(56),
+        scratch_shapes=[VMEM((2 * points, pixels), bf16), VMEM((2 * points, 128), f32)],
+        compiler_params=params(40),
         name="best_scores",
-    )(indexed, scored, panels)
+    )(indexed, scored, pltpu.with_memory_space_constraint(panels, pltpu.HBM))
     returned = lax.ppermute(other_best, EVERY, trade)
     other_best, group_total = lax.optimization_barrier((other_best, group_total))
     group_totals = lax.all_gather(group_total, DICT, axis=0, tiled=False)
     returned, group_totals = lax.optimization_barrier((returned, group_totals))
-    zs = lax.axis_size("z")
-    group_totals = group_totals.reshape((zs, 2) + group_total.shape).astype(f32)
-    grain_total = jnp.sum(group_totals, axis=0).reshape(-1, pixels)
-    mean_square = jnp.mean(grain_total * grain_total, axis=-1, keepdims=True)
-    grain_patterns = grain_total * lax.rsqrt(mean_square + EPS)
-    best = jnp.maximum(own_best, returned)
-    max_score = (best * (1.0 / math.sqrt(pixels))).reshape(tile_rows, tile_cols)
-    return (max_score, grain_patterns)
+    return pl.pallas_call(
+        finish,
+        out_shape=(
+            jax.ShapeDtypeStruct((tile_rows, tile_cols), f32),
+            jax.ShapeDtypeStruct((2 * group_total.shape[0], pixels), f32),
+        ),
+        in_specs=[pl.BlockSpec(memory_space=VMEM)] * 3,
+        out_specs=[pl.BlockSpec(memory_space=VMEM)] * 2,
+        compiler_params=params(8),
+        name="finish",
+    )(own_best, returned, group_totals)
 
 
 def solution(mesh):

time: 132 us -> 120 us (0.909)
  blocking collectives: 57.7 us -> 48.8 us
  starting transfers between devices: 22.6 us -> 28.9 us
  Pallas kernels: 24 us -> 19.2 us
  local copies, waits for them, and re-layouts: 6.3 us -> 2.32 us
  other arithmetic: 2.77 us -> 1.02 us
    all_to_all x1, blocking collectives: 29.9 us -> 21.9 us  [shards(): lax.all_to_all(chip_sums.reshape(lines, -1, pixels), SCAN, 0, 0, tiled=True)]
    pallas_call x1, Pallas kernels: 13 us -> 7.58 us  [shards(): pl.pallas_call(best_scores, grid=(panels.shape[0] // block,), out_shape=(...]
    ppermute x1, starting transfers between devices: 4.16 us -> 9.07 us  [shards(): lax.ppermute(indexed.reshape(patterns.shape), EVERY, trade)]
    reshape x3 -> x0, local copies, waits for them, and re-layouts: 2.07 us -> none  [the longest x1 1.33 us: shards(): background.reshape(1, pixels)]
    all_to_all x1, blocking collectives: 6.24 us -> 4.28 us  [shards(): lax.all_to_all(sums.reshape(2, grain_count // 2, pixels), 'core', 0, 0, t...]
    mul x2 -> x0, other arithmetic: 1.4 us -> none  [the longest x1 0.7 us: shards(): max_score = (best * (1.0 / math.sqrt(pixels))).reshape(tile_rows, tile_cols)]
    ppermute x1, starting transfers between devices: 3.03 us -> 4.43 us  [shards(): returned = lax.ppermute(other_best, EVERY, trade)]
    unnamed x12 -> x10, local copies, waits for them, and re-layouts: 2.77 us -> 1.9 us
  transfers between devices with their start and end apart: 7 -> 7, of which waited for: 3 -> 3; matrix products, arithmetic and copies ran while one was open for 3% -> 1% of each run, Pallas kernels for 7% -> 7%
where the time goes in v3:
time: 120 us; the launch traced here: 119 us
  blocking collectives  48.8 us (41%)
  starting transfers between devices  28.9 us (24%)
  Pallas kernels  19.2 us (16%)
  between operations  14.2 us (12%)
  waiting for transfers between devices  4.78 us (4%)
  local copies, waits for them, and re-layouts  2.32 us (2%)
    all_gather x1, blocking collectives, shards(): group_totals = lax.all_gather(group_total, DICT, axis=0, tiled=False)  22.6 us
    all_to_all x1, blocking collectives, shards(): lax.all_to_all(chip_sums.reshape(lines, -1, pixels), SCAN, 0, 0, tiled=True)  21.9 us
    ppermute x1, starting transfers between devices, shards(): lax.ppermute(indexed.reshape(patterns.shape), EVERY, trade)  9.07 us
    pallas_call x1, Pallas kernels, shards(): pl.pallas_call(best_scores, grid=(panels.shape[0] // block,), out_shape=(...  7.58 us
    pallas_call x1, Pallas kernels, shards(): pl.pallas_call(neighbour_sums, out_shape=(jax.ShapeDtypeStruct((points, p...  5.44 us
    ppermute x1, starting transfers between devices, shards(): low = lax.ppermute(high_edge, DICT, forward)  5.39 us
    ppermute x1, starting transfers between devices, shards(): high = lax.ppermute(low_edge, DICT, backward)  4.69 us
    ppermute x1, starting transfers between devices, shards(): returned = lax.ppermute(other_best, EVERY, trade)  4.43 us
  transfers between devices with their start and end apart: 7, of which 3 were waited for; matrix products, arithmetic and copies ran while one was open for 1% of the time, Pallas kernels for 7%

profile of v3, /device:TPU:1, one launch (start us, length us, event | category | flops | bytes accessed | tf_op | source)
XLA Modules:
  0.0 119.2 jit_solution(7282670404272233416)
XLA Ops:
  7.2 1.2 copy-done
  8.4 2.3 %normalise_templates.1 = bf16[64,3600]{1,0:T(8,128)(2,1)} custom-call(bf16[3600,128]{1,0:T(8,128)(2,1)S(1)} %bitcast.12), custom_call_target="tpu_custom_call" | custom-call | tf_op jit(solution)/shard_map/normalise_templates/pallas_call | solution.py:144
  10.7 0.7 copy-done.1
  11.4 3.1 %filter_tile.1 = (bf16[16,16,3600]{2,1,0:T(8,128)(2,1)S(1)}, bf16[16,3600]{1,0:T(8,128)(2,1)S(1)}, bf16[16,3600]{1,0:T(8,128)(2,1)S(1)}) custom-call(f32[3600]{0:T(1024)S(1)} %copy-done.1, f32[16,16,3600]{2,1,0:T(8,128)} %tile_ref), custom_call_target="tpu_custom_call" | custom-call | tf_op jit(solution)/shard_map/filter_tile/pallas_call | solution.py:157
  14.5 5.4 %collective-permute-start = (bf16[16,3600]{1,0:T(8,128)(2,1)S(1)}, bf16[16,3600]{1,0:T(8,128)(2,1)S(1)}, u32[]{:S(2)}, u32[]{:S(2)}) collective-permute-start(bf16[16,3600]{1,0:T(8,128)(2,1)S(1)} %get-tuple-element.17), channel_id=1, source_target_pairs={{0,32},{32,64},{64,96},{96,128},{128,160},{160,192},{192,224},{224... | collective-permute-start | bytes 345608 | tf_op jit(solution)/shard_map/ppermute | solution.py:181
  19.9 4.7 %collective-permute-start.1 = (bf16[16,3600]{1,0:T(8,128)(2,1)S(1)}, bf16[16,3600]{1,0:T(8,128)(2,1)S(1)}, u32[]{:S(2)}, u32[]{:S(2)}) collective-permute-start(bf16[16,3600]{1,0:T(8,128)(2,1)S(1)} %get-tuple-element.18), channel_id=1, source_target_pairs={{32,0},{64,32},{96,64},{128,96},{160,128},{192,160},{224,192},{256... | collective-permute-start | bytes 345608 | tf_op jit(solution)/shard_map/ppermute | solution.py:182
  24.7 0.1 eq.33
  24.9 0.2 select_reduce_fusion
  25.1 1.0 collective-permute-done.1.high_ref
  26.2 1.3 %collective-permute-start.3 = (bf16[18,3600]{1,0:T(8,128)(2,1)S(1)}, bf16[18,3600]{1,0:T(8,128)(2,1)S(1)}, u32[]{:S(2)}, u32[]{:S(2)}) collective-permute-start(bf16[18,3600]{1,0:T(8,128)(2,1)S(1)} %pad_maximum_fusion.1), channel_id=1, source_target_pairs={{1,0},{2,1},{3,2},{4,3},{5,4},{6,5},{7,6},{8,7},{9,8},{10,9},{11,1... | collective-permute-start | bytes 388808 | tf_op jit(solution)/shard_map/ppermute | solution.py:191
  27.5 4.0 %collective-permute-start.2 = (bf16[18,3600]{1,0:T(8,128)(2,1)S(1)}, bf16[18,3600]{1,0:T(8,128)(2,1)S(1)}, u32[]{:S(2)}, u32[]{:S(2)}) collective-permute-start(bf16[18,3600]{1,0:T(8,128)(2,1)S(1)} %pad_maximum_fusion), channel_id=1, source_target_pairs={{0,1},{1,2},{2,3},{3,4},{4,5},{5,6},{6,7},{7,8},{8,9},{9,10},{10,1... | collective-permute-start | bytes 388808 | tf_op jit(solution)/shard_map/ppermute | solution.py:190
  31.5 2.8 %collective-permute-done.3.below_ref = bf16[18,3600]{1,0:T(8,128)(2,1)S(1)} collective-permute-done((bf16[18,3600]{1,0:T(8,128)(2,1)S(1)}, bf16[18,3600]{1,0:T(8,128)(2,1)S(1)}, u32[]{:S(2)}, u32[]{:S(2)}) %collective-permute-start.3) | collective-permute-done | bytes 129632 | tf_op jit(solution)/shard_map/ppermute | solution.py:191
  34.4 0.9 collective-permute-done.2.above_ref
  35.3 5.4 %neighbour_sums.1 = (bf16[256,3600]{1,0:T(8,128)(2,1)}, bf16[128,3600]{1,0:T(8,128)(2,1)S(1)}) custom-call(s32[1,256]{1,0:T(1,128)S(1)} %broadcast_select_fusion.point_row_ref, bf16[16,16,3600]{2,1,0:T(8,128)(2,1)S(1)} %get-tuple-element.16.tile_ref, bf16[16,3600]{1,0:T(8,128)(2,1)S(1)} %collective-permute-done.low_ref, ...), custom_call_target="tpu_custom_call" | custom-call | tf_op jit(solution)/shard_map/neighbour_sums/pallas_call | solution.py:199
  40.7 9.1 %collective-permute-start.4 = (bf16[16,16,3600]{2,1,0:T(8,128)(2,1)}, bf16[16,16,3600]{2,1,0:T(8,128)(2,1)S(1)}, u32[]{:S(2)}, u32[]{:S(2)}) collective-permute-start(bf16[16,16,3600]{2,1,0:T(8,128)(2,1)} %bitcast.4), channel_id=1, source_target_pairs={{0,8},{32,56},{1,9},{33,57},{2,10},{34,58},{3,11},{35,59},{4,12},{... | collective-permute-start | bytes 5529608 | tf_op jit(solution)/shard_map/ppermute | solution.py:222
  49.8 4.3 %all_to_all.10 = bf16[2,64,3600]{2,1,0:T(8,128)(2,1)S(1)} all-to-all(bf16[2,64,3600]{2,1,0:T(8,128)(2,1)S(1)} %bitcast.11), channel_id=1, replica_groups=mesh['z'=8,'core'=2,'x'=4,'y'=8] {'core'}, dimensions={0} | all-to-all | bytes 1843200 | tf_op jit(solution)/shard_map/all_to_all | solution.py:224
  54.1 0.3 reduce_sum.37
  54.4 0.2 reshape.42
  54.6 21.9 %all_to_all.11 = bf16[32,2,3600]{2,1,0:T(2,128)(2,1)S(1)} all-to-all(bf16[32,2,3600]{2,1,0:T(2,128)(2,1)S(1)} %reshape.42), channel_id=1, replica_groups=mesh['z'=8,'core'=2,'x'=4,'y'=8] {'x','y'}, dimensions={0} | all-to-all | bytes 921600 | tf_op jit(solution)/shard_map/all_to_all | solution.py:228
  76.5 0.4 reduce_sum.38
  77.0 7.6 %best_scores.1 = (f32[1,256]{1,0:T(1,128)S(1)}, f32[1,256]{1,0:T(1,128)S(1)}) custom-call(bf16[256,3600]{1,0:T(8,128)(2,1)} %get-tuple-element.19.own_ref, bf16[256,3600]{1,0:T(8,128)(2,1)S(1)} %bitcast.10, bf16[1024,3600]{1,0:T(8,128)(2,1)} %all-gather.4.cloned.1.call-done.panel_ref), custom_call_target="tpu_custom_call" | custom-call | tf_op jit(solution)/shard_map/best_scores/pallas_call | solution.py:233
  84.5 4.4 %collective-permute-start.5 = (f32[1,256]{1,0:T(1,128)S(1)}, f32[1,256]{1,0:T(1,128)S(1)}, u32[]{:S(2)}, u32[]{:S(2)}) collective-permute-start(f32[1,256]{1,0:T(1,128)S(1)} %get-tuple-element.23), channel_id=1, source_target_pairs={{0,8},{32,56},{1,9},{33,57},{2,10},{34,58},{3,11},{35,59},{4,12},{... | collective-permute-start | bytes 3080 | tf_op jit(solution)/shard_map/ppermute | solution.py:247
  89.0 22.6 %all-gather.1.totals_ref = bf16[16,2,3600]{2,1,0:T(2,128)(2,1)S(1)} all-gather(bf16[1,2,3600]{2,1,0:T(2,128)(2,1)S(1)} %bitcast.13), channel_id=2, replica_groups=mesh['z'=8,'core'=2,'x'=4,'y'=8] {'z','core'}, dimensions={0}, use_global_device_ids=true | all-gather | bytes 244800 | tf_op jit(solution)/shard_map/all_gather | solution.py:249
  111.6 0.8 finish.1
  (22 shorter events, 0.4 us)
Async XLA Ops:
  7.2 69.8 %all-gather.4.cloned.1.call-start = ((), (), s32[]{:S(2)}) async-start(), calls=%async_computation.2 | async-start | bytes 8077312 | tf_op jit(solution)/shard_map/all_gather | solution.py:153
  7.2 1.2 copy-start
  10.7 0.7 copy-start.1
  11.4 13.2 %copy-start.2 = (s32[16,16]{1,0:T(8,128)S(1)}, s32[16,16]{1,0:T(8,128)}, u32[]{:S(2)}) copy-start(s32[16,16]{1,0:T(8,128)} %param.10) | copy-start | bytes 3076
  11.4 13.3 %copy-start.3 = (s32[16,16]{1,0:T(8,128)S(1)}, s32[16,16]{1,0:T(8,128)}, u32[]{:S(2)}) copy-start(s32[16,16]{1,0:T(8,128)} %param.9) | copy-start | bytes 3076
  11.4 13.5 %copy-start.4 = (s32[128]{0:T(128)S(1)}, s32[128]{0:T(128)}, u32[]{:S(2)}) copy-start(s32[128]{0:T(128)} %param.11) | copy-start | bytes 1540
  14.5 10.5 %collective-permute-start = (bf16[16,3600]{1,0:T(8,128)(2,1)S(1)}, bf16[16,3600]{1,0:T(8,128)(2,1)S(1)}, u32[]{:S(2)}, u32[]{:S(2)}) collective-permute-start(bf16[16,3600]{1,0:T(8,128)(2,1)S(1)} %get-tuple-element.17), channel_id=1, source_target_pairs={{0,32},{32,64},{64,96},{96,128},{128,160},{160,192},{192,224},{224... | collective-permute-start | bytes 345608 | tf_op jit(solution)/shard_map/ppermute | solution.py:181
  19.9 6.2 %collective-permute-start.1 = (bf16[16,3600]{1,0:T(8,128)(2,1)S(1)}, bf16[16,3600]{1,0:T(8,128)(2,1)S(1)}, u32[]{:S(2)}, u32[]{:S(2)}) collective-permute-start(bf16[16,3600]{1,0:T(8,128)(2,1)S(1)} %get-tuple-element.18), channel_id=1, source_target_pairs={{32,0},{64,32},{96,64},{128,96},{160,128},{192,160},{224,192},{256... | collective-permute-start | bytes 345608 | tf_op jit(solution)/shard_map/ppermute | solution.py:182
  26.2 8.2 %collective-permute-start.3 = (bf16[18,3600]{1,0:T(8,128)(2,1)S(1)}, bf16[18,3600]{1,0:T(8,128)(2,1)S(1)}, u32[]{:S(2)}, u32[]{:S(2)}) collective-permute-start(bf16[18,3600]{1,0:T(8,128)(2,1)S(1)} %pad_maximum_fusion.1), channel_id=1, source_target_pairs={{1,0},{2,1},{3,2},{4,3},{5,4},{6,5},{7,6},{8,7},{9,8},{10,9},{11,1... | collective-permute-start | bytes 388808 | tf_op jit(solution)/shard_map/ppermute | solution.py:191
  27.5 7.7 %collective-permute-start.2 = (bf16[18,3600]{1,0:T(8,128)(2,1)S(1)}, bf16[18,3600]{1,0:T(8,128)(2,1)S(1)}, u32[]{:S(2)}, u32[]{:S(2)}) collective-permute-start(bf16[18,3600]{1,0:T(8,128)(2,1)S(1)} %pad_maximum_fusion), channel_id=1, source_target_pairs={{0,1},{1,2},{2,3},{3,4},{4,5},{5,6},{6,7},{7,8},{8,9},{9,10},{10,1... | collective-permute-start | bytes 388808 | tf_op jit(solution)/shard_map/ppermute | solution.py:190
  40.7 36.2 %collective-permute-start.4 = (bf16[16,16,3600]{2,1,0:T(8,128)(2,1)}, bf16[16,16,3600]{2,1,0:T(8,128)(2,1)S(1)}, u32[]{:S(2)}, u32[]{:S(2)}) collective-permute-start(bf16[16,16,3600]{2,1,0:T(8,128)(2,1)} %bitcast.4), channel_id=1, source_target_pairs={{0,8},{32,56},{1,9},{33,57},{2,10},{34,58},{3,11},{35,59},{4,12},{... | collective-permute-start | bytes 5529608 | tf_op jit(solution)/shard_map/ppermute | solution.py:222
  84.5 27.0 %collective-permute-start.5 = (f32[1,256]{1,0:T(1,128)S(1)}, f32[1,256]{1,0:T(1,128)S(1)}, u32[]{:S(2)}, u32[]{:S(2)}) collective-permute-start(f32[1,256]{1,0:T(1,128)S(1)} %get-tuple-element.23), channel_id=1, source_target_pairs={{0,8},{32,56},{1,9},{33,57},{2,10},{34,58},{3,11},{35,59},{4,12},{... | collective-permute-start | bytes 3080 | tf_op jit(solution)/shard_map/ppermute | solution.py:247
Sparse Core Ops, SparseCore 0:
  10.8 61.5 all-gather.3

commit v4 on v3

--- a/solution.py
+++ b/solution.py
@@ -15,22 +15,55 @@
 VMEM = pltpu.VMEM
 
 
-def normalise_templates(panel_ref, out_ref, whole_ref):
-    panel = panel_ref[...].astype(jnp.float32)
-    pixels = panel.shape[0]
-    panel = panel - jnp.sum(panel, axis=0, keepdims=True) * (1.0 / pixels)
-    mean_square = jnp.sum(panel * panel, axis=0, keepdims=True) * (1.0 / pixels)
-    panel = panel * lax.rsqrt(mean_square + EPS)
-    whole_ref[...] = panel.T.astype(jnp.bfloat16)
+def normalise_templates(panel_hbm, out_ref, panel_ref, arrived):
+    pixels, lanes = panel_ref.shape
     held = out_ref.shape[0]
-    parity = lax.axis_index("x") & 1
-    out_ref[...] = whole_ref[pl.ds(pl.multiple_of(parity * held, held), held), :]
-
-
-def filter_tile(background_ref, tile_ref, out_ref, low_ref, high_ref, low, high):
+    step = pixels // arrived.shape[0]
+    copies = []
+    for part in range(arrived.shape[0]):
+        rows = pl.ds(part * step, step)
+        copies.append(pltpu.make_async_copy(panel_hbm.at[rows], panel_ref.at[rows], arrived.at[part]))
+        copies[-1].start()
+    total = jnp.zeros((1, lanes), jnp.float32)
+    for part, copy in enumerate(copies):
+        copy.wait()
+        values = panel_ref[part * step : (part + 1) * step, :].astype(jnp.float32)
+        total = total + jnp.sum(values, axis=0, keepdims=True)
+    mean = total * (1.0 / pixels)
+    total = jnp.zeros((1, lanes), jnp.float32)
+    for start in range(0, pixels, step):
+        values = panel_ref[start : start + step, :].astype(jnp.float32) - mean
+        total = total + jnp.sum(values * values, axis=0, keepdims=True)
+    scale = lax.rsqrt(total * (1.0 / pixels) + EPS)
+    first = (lax.axis_index("x") & 1) * held
+    lane = lax.broadcasted_iota(jnp.int32, (held, lanes), 1)
+    place = lax.broadcasted_iota(jnp.int32, (held, lanes), 0)
+    chosen = jnp.where(lane == place + first, 1.0, 0.0).astype(jnp.bfloat16)
+    step = 768
+    for start in range(0, pixels, step):
+        stop = min(start + step, pixels)
+        values = (panel_ref[start:stop, :].astype(jnp.float32) - mean) * scale
+        out_ref[:, start:stop] = lax.dot_general(
+            chosen,
+            values.astype(jnp.bfloat16),
+            (((1,), (1,)), ((), ())),
+            preferred_element_type=jnp.float32,
+        ).astype(jnp.bfloat16)
+
+
+def filter_tile(background_ref, tile_hbm, out_ref, low_ref, high_ref, tile_ref, low, high, arrived):
+    rows, cols, pixels = tile_ref.shape
+    parts = arrived.shape[0]
+    step = rows // parts
+    copies = []
+    for part in range(parts):
+        lines = pl.ds(part * step, step)
+        copies.append(pltpu.make_async_copy(tile_hbm.at[lines], tile_ref.at[lines], arrived.at[part]))
+        copies[-1].start()
     background = background_ref[...].reshape(1, -1)
-    rows, _, pixels = tile_ref.shape
     for row in range(rows):
+        if row % step == 0:
+            copies[row // step].wait()
         values = tile_ref[row] - background
         values = values - jnp.sum(values, axis=-1, keepdims=True) * (1.0 / pixels)
         mean_square = jnp.sum(values * values, axis=-1, keepdims=True) * (1.0 / pixels)
@@ -42,43 +75,64 @@
     high_ref[...] = high[...].astype(jnp.bfloat16)
 
 
-def neighbour_sums(
-    point_row_ref, tile_ref, low_ref, high_ref, above_ref, below_ref, out_ref, sums_ref, low_pad, high_pad, shift, ends
-):
+def index_points(column, low, high, shift):
+    cols, pixels = column.shape
+    shift[7:8, :] = low
+    shift[8 : 8 + cols, :] = column
+    shift[8 + cols : 9 + cols, :] = high
+    total = column + shift[7 : 7 + cols, :] + shift[9 : 9 + cols, :]
+    mean_square = jnp.sum(total * total, axis=-1, keepdims=True) * (1.0 / pixels)
+    return (total * lax.rsqrt(mean_square + EPS)).astype(jnp.bfloat16)
+
+
+def inner_rows(tile_ref, low_ref, high_ref, out_ref, low_pad, high_pad, shift, ends):
     rows, cols, pixels = tile_ref.shape
-    above, below = above_ref[...].astype(jnp.float32), below_ref[...].astype(jnp.float32)
-    for pad, side_ref, corner in ((low_pad, low_ref, cols), (high_pad, high_ref, cols + 1)):
-        pad[0:1, :] = above[corner : corner + 1]
-        pad[1 : rows + 1, :] = side_ref[...].astype(jnp.float32)
-        pad[rows + 1 : rows + 2, :] = below[corner : corner + 1]
-
-    for row in range(rows):
-        for side, pad in enumerate((low_pad, high_pad)):
-            ends[row, side : side + 1, :] = pad[row : row + 1, :] + pad[row + 1 : row + 2, :] + pad[row + 2 : row + 3, :]
-
-    def one_row(row, before, middle, after):
-        column = before + middle + after
-        shift[7:8, :] = ends[row, 0:1, :]
-        shift[8 : 8 + cols, :] = column
-        shift[8 + cols : 9 + cols, :] = ends[row, 1:2, :]
-        total = column + shift[7 : 7 + cols, :] + shift[9 : 9 + cols, :]
-        mean_square = jnp.sum(total * total, axis=-1, keepdims=True) * (1.0 / pixels)
-        values = (total * lax.rsqrt(mean_square + EPS)).astype(jnp.bfloat16)
-        out_ref[pl.ds(pl.multiple_of(row * cols, cols), cols), :] = values
+    for side, (pad, side_ref) in enumerate(((low_pad, low_ref), (high_pad, high_ref))):
+        pad[...] = side_ref[...].astype(jnp.float32)
+        for row in range(1, rows - 1):
+            ends[row, side : side + 1, :] = (
+                pad[row - 1 : row, :] + pad[row : row + 1, :] + pad[row + 1 : row + 2, :]
+            )
 
     def line(row):
         return tile_ref[row].astype(jnp.float32)
 
-    one_row(0, above[:cols], line(0), line(1))
-
-    def inner(row, carry):
-        one_row(row, line(row - 1), line(row), line(row + 1))
+    def one_row(row, carry):
+        column = line(row - 1) + line(row) + line(row + 1)
+        start = pl.multiple_of((row - 1) * cols, cols)
+        out_ref[pl.ds(start, cols), :] = index_points(
+            column, ends[row, 0:1, :], ends[row, 1:2, :], shift
+        )
         return carry
 
-    lax.fori_loop(1, rows - 1, inner, 0)
-    one_row(rows - 1, line(rows - 2), line(rows - 1), below[:cols])
+    lax.fori_loop(1, rows - 1, one_row, 0)
+
+
+def outer_rows(
+    point_row_ref, first_ref, second_ref, third_ref, fourth_ref, low_ref, high_ref, above_ref, below_ref,
+    inner_ref, out_ref, sums_ref, shift,
+):
+    points, pixels = out_ref.shape
+    cols = first_ref.shape[0]
+    rows = points // cols
+    out_ref[cols : points - cols, :] = inner_ref[...]
+    low, high = low_ref[...].astype(jnp.float32), high_ref[...].astype(jnp.float32)
+    above, below = above_ref[...].astype(jnp.float32), below_ref[...].astype(jnp.float32)
+    for halo, near_ref, next_ref, row, inward in (
+        (above, first_ref, second_ref, 0, 1),
+        (below, fourth_ref, third_ref, rows - 1, -1),
+    ):
+        column = halo[:cols] + near_ref[...].astype(jnp.float32) + next_ref[...].astype(jnp.float32)
+        edges = []
+        for side, values in enumerate((low, high)):
+            edges.append(
+                halo[cols + side : cols + side + 1]
+                + values[row : row + 1]
+                + values[row + inward : row + inward + 1]
+            )
+        out_ref[row * cols : (row + 1) * cols, :] = index_points(column, edges[0], edges[1], shift)
     grains = sums_ref.shape[0]
-    k = lax.broadcasted_iota(jnp.int32, (grains, rows * cols), 0)
+    k = lax.broadcasted_iota(jnp.int32, (grains, points), 0)
     half = grains // 2
     grain = (k % half) // 2 * 4 + k // half * 2 + k % 2
     selector = jnp.where(grain == point_row_ref[...], 1.0, 0.0).astype(jnp.bfloat16)
@@ -144,37 +198,36 @@
     panel = pl.pallas_call(
         normalise_templates,
         out_shape=jax.ShapeDtypeStruct((held, pixels), bf16),
-        in_specs=[pl.BlockSpec(memory_space=VMEM)],
+        in_specs=[pl.BlockSpec(memory_space=pl.ANY)],
         out_specs=pl.BlockSpec(memory_space=VMEM),
-        scratch_shapes=[VMEM((2 * held, pixels), bf16)],
+        scratch_shapes=[VMEM((pixels, 2 * held), bf16), pltpu.SemaphoreType.DMA((5,))],
         compiler_params=params(10),
         name="normalise_templates",
-    )(templates.T)
+    )(pltpu.with_memory_space_constraint(templates.T, pltpu.HBM))
     panels = lax.all_gather(panel, DICT, axis=0, tiled=True)
 
     patterns, panel = lax.optimization_barrier((patterns, panel))
-    block = 8
     filtered, low_edge, high_edge = pl.pallas_call(
         filter_tile,
-        grid=(tile_rows // block,),
         out_shape=(
             jax.ShapeDtypeStruct((tile_rows, tile_cols, pixels), bf16),
             jax.ShapeDtypeStruct((tile_rows, pixels), bf16),
             jax.ShapeDtypeStruct((tile_rows, pixels), bf16),
         ),
-        in_specs=[
-            pl.BlockSpec((pixels,), lambda i: (0,)),
-            pl.BlockSpec((block, tile_cols, pixels), lambda i: (i, 0, 0)),
+        in_specs=[pl.BlockSpec(memory_space=VMEM), pl.BlockSpec(memory_space=pl.ANY)],
+        out_specs=(pl.BlockSpec(memory_space=VMEM),) * 3,
+        scratch_shapes=[
+            VMEM((tile_rows, tile_cols, pixels), f32),
+            VMEM((tile_rows, pixels), f32),
+            VMEM((tile_rows, pixels), f32),
+            pltpu.SemaphoreType.DMA((8,)),
         ],
-        out_specs=(
-            pl.BlockSpec((block, tile_cols, pixels), lambda i: (i, 0, 0)),
-            pl.BlockSpec((block, pixels), lambda i: (i, 0)),
-            pl.BlockSpec((block, pixels), lambda i: (i, 0)),
-        ),
-        scratch_shapes=[VMEM((block, pixels), f32)] * 2,
         compiler_params=params(16),
         name="filter_tile",
-    )(background, pltpu.with_memory_space_constraint(patterns, pltpu.HBM))
+    )(
+        pltpu.with_memory_space_constraint(background, pltpu.HBM),
+        pltpu.with_memory_space_constraint(patterns, pltpu.HBM),
+    )
     columns = lax.axis_size(DICT)
     forward = [(i, i + 1) for i in range(columns - 1)]
     backward = [(i + 1, i) for i in range(columns - 1)]
@@ -196,19 +249,32 @@
     point_row = jnp.sum(jnp.where(matches, grain_row[None, :], 0), axis=1)
     point_row = jnp.where(keep_mask.reshape(-1) == 1, point_row, -1).reshape(1, points)
 
+    inner_points = points - 2 * tile_cols
+    inner = pl.pallas_call(
+        inner_rows,
+        out_shape=jax.ShapeDtypeStruct((inner_points, pixels), bf16),
+        in_specs=[pl.BlockSpec(memory_space=VMEM)] * 3,
+        out_specs=pl.BlockSpec(memory_space=VMEM),
+        scratch_shapes=[VMEM((tile_rows, pixels), f32)] * 2
+        + [VMEM((32, pixels), f32), VMEM((tile_rows, 2, pixels), f32)],
+        compiler_params=params(10),
+        cost_estimate=pl.CostEstimate(
+            flops=12 * inner_points * pixels, bytes_accessed=16 * inner_points * pixels, transcendentals=0
+        ),
+        name="inner_rows",
+    )(filtered, low, high)
     indexed, sums = pl.pallas_call(
-        neighbour_sums,
+        outer_rows,
         out_shape=(
             jax.ShapeDtypeStruct((points, pixels), bf16),
             jax.ShapeDtypeStruct((grain_count, pixels), bf16),
         ),
-        in_specs=[pl.BlockSpec(memory_space=VMEM)] * 6,
+        in_specs=[pl.BlockSpec(memory_space=VMEM)] * 10,
         out_specs=[pl.BlockSpec(memory_space=VMEM)] * 2,
-        scratch_shapes=[VMEM((24, pixels), f32)] * 2
-        + [VMEM((32, pixels), f32), VMEM((tile_rows, 2, pixels), f32)],
-        compiler_params=params(12),
-        name="neighbour_sums",
-    )(point_row, filtered, low, high, above, below)
+        scratch_shapes=[VMEM((32, pixels), f32)],
+        compiler_params=params(10),
+        name="outer_rows",
+    )(point_row, filtered[0], filtered[1], filtered[-2], filtered[-1], low, high, above, below, inner)
 
     xs, ys = lax.axis_size("x"), lax.axis_size("y")
     trade = []
@@ -241,7 +307,7 @@
         ],
         out_specs=(pl.BlockSpec((1, points), lambda i: (0, 0)),) * 2,
         scratch_shapes=[VMEM((2 * points, pixels), bf16), VMEM((2 * points, 128), f32)],
-        compiler_params=params(40),
+        compiler_params=params(28),
         name="best_scores",
     )(indexed, scored, pltpu.with_memory_space_constraint(panels, pltpu.HBM))
     returned = lax.ppermute(other_best, EVERY, trade)

time: 120 us -> 115 us (0.958)
  waiting for transfers between devices: 4.78 us -> 1.29 us
  local copies, waits for them, and re-layouts: 2.32 us -> 0.46 us
    ppermute x1, waiting for transfers between devices: 2.84 us -> 0.01 us  [shards(): below = lax.ppermute(strip(0), SCAN, backward)]
    unnamed x10 -> x6, local copies, waits for them, and re-layouts: 1.9 us -> 0.02 us
    pallas_call x2 -> x3, Pallas kernels: 8.57 us -> 8.9 us  [the longest x1 4.47 us: shards(): pl.pallas_call(filter_tile, out_shape=(jax.ShapeDtypeStruct((tile_rows, t...]
  transfers between devices with their start and end apart: 7 -> 7, of which waited for: 3 -> 2; matrix products, arithmetic and copies ran while one was open for 1% -> 1% of each run, Pallas kernels for 7% -> 8%
where the time goes in v4:
time: 115 us
  blocking collectives  48.6 us (42%)
  starting transfers between devices  28.9 us (25%)
  Pallas kernels  20.3 us (18%)
  between operations  14.2 us (12%)
  waiting for transfers between devices  1.29 us (1%)
    all_gather x1, blocking collectives, shards(): group_totals = lax.all_gather(group_total, DICT, axis=0, tiled=False)  22.6 us
    all_to_all x1, blocking collectives, shards(): lax.all_to_all(chip_sums.reshape(lines, -1, pixels), SCAN, 0, 0, tiled=True)  21.7 us
    ppermute x1, starting transfers between devices, shards(): lax.ppermute(indexed.reshape(patterns.shape), EVERY, trade)  9.04 us
    pallas_call x1, Pallas kernels, shards(): pl.pallas_call(best_scores, grid=(panels.shape[0] // block,), out_shape=(...  7.57 us
    ppermute x1, starting transfers between devices, shards(): low = lax.ppermute(high_edge, DICT, forward)  5.39 us
    ppermute x1, starting transfers between devices, shards(): high = lax.ppermute(low_edge, DICT, backward)  4.69 us
    pallas_call x1, Pallas kernels, shards(): pl.pallas_call(filter_tile, out_shape=(jax.ShapeDtypeStruct((tile_rows, t...  4.47 us
    ppermute x1, starting transfers between devices, shards(): returned = lax.ppermute(other_best, EVERY, trade)  4.44 us
  transfers between devices with their start and end apart: 7, of which 2 were waited for; matrix products, arithmetic and copies ran while one was open for 1% of the time, Pallas kernels for 8%

profile of v4, /device:TPU:1, one launch (start us, length us, event | category | flops | bytes accessed | tf_op | source)
XLA Modules:
  0.0 114.9 jit_solution(16222363460004446123)
XLA Ops:
  7.2 0.0 all-gather.4.cloned.1.call-start
  7.2 3.1 %normalise_templates.1 = bf16[64,3600]{1,0:T(8,128)(2,1)} custom-call(bf16[3600,128]{1,0:T(8,128)(2,1)} %bitcast.16), custom_call_target="tpu_custom_call" | custom-call | tf_op jit(solution)/shard_map/normalise_templates/pallas_call | solution.py:198
  10.3 4.5 %filter_tile.1 = (bf16[16,16,3600]{2,1,0:T(8,128)(2,1)S(1)}, bf16[16,3600]{1,0:T(8,128)(2,1)S(1)}, bf16[16,3600]{1,0:T(8,128)(2,1)S(1)}) custom-call(f32[3600]{0:T(1024)} %background_ref.1, f32[16,16,3600]{2,1,0:T(8,128)} %tile_hbm), custom_call_target="tpu_custom_call" | custom-call | tf_op jit(solution)/shard_map/filter_tile/pallas_call | solution.py:210
  14.8 5.4 %collective-permute-start = (bf16[16,3600]{1,0:T(8,128)(2,1)S(1)}, bf16[16,3600]{1,0:T(8,128)(2,1)S(1)}, u32[]{:S(2)}, u32[]{:S(2)}) collective-permute-start(bf16[16,3600]{1,0:T(8,128)(2,1)S(1)} %get-tuple-element.17), channel_id=1, source_target_pairs={{0,32},{32,64},{64,96},{96,128},{128,160},{160,192},{192,224},{224... | collective-permute-start | bytes 345608 | tf_op jit(solution)/shard_map/ppermute | solution.py:234
  20.2 4.7 %collective-permute-start.1 = (bf16[16,3600]{1,0:T(8,128)(2,1)S(1)}, bf16[16,3600]{1,0:T(8,128)(2,1)S(1)}, u32[]{:S(2)}, u32[]{:S(2)}) collective-permute-start(bf16[16,3600]{1,0:T(8,128)(2,1)S(1)} %get-tuple-element.18), channel_id=1, source_target_pairs={{32,0},{64,32},{96,64},{128,96},{160,128},{192,160},{224,192},{256... | collective-permute-start | bytes 345608 | tf_op jit(solution)/shard_map/ppermute | solution.py:235
  24.9 0.1 eq.33
  25.0 0.1 eq.34
  25.2 0.2 select_reduce_fusion
  25.4 1.0 collective-permute-done.1.high_ref
  26.5 1.3 %collective-permute-start.3 = (bf16[18,3600]{1,0:T(8,128)(2,1)S(1)}, bf16[18,3600]{1,0:T(8,128)(2,1)S(1)}, u32[]{:S(2)}, u32[]{:S(2)}) collective-permute-start(bf16[18,3600]{1,0:T(8,128)(2,1)S(1)} %pad_maximum_fusion.1), channel_id=1, source_target_pairs={{1,0},{2,1},{3,2},{4,3},{5,4},{6,5},{7,6},{8,7},{9,8},{10,9},{11,1... | collective-permute-start | bytes 388808 | tf_op jit(solution)/shard_map/ppermute | solution.py:244
  27.8 4.0 %collective-permute-start.2 = (bf16[18,3600]{1,0:T(8,128)(2,1)S(1)}, bf16[18,3600]{1,0:T(8,128)(2,1)S(1)}, u32[]{:S(2)}, u32[]{:S(2)}) collective-permute-start(bf16[18,3600]{1,0:T(8,128)(2,1)S(1)} %pad_maximum_fusion), channel_id=1, source_target_pairs={{0,1},{1,2},{2,3},{3,4},{4,5},{5,6},{6,7},{7,8},{8,9},{9,10},{10,1... | collective-permute-start | bytes 388808 | tf_op jit(solution)/shard_map/ppermute | solution.py:243
  31.8 3.5 %inner_rows.1.inner_ref = bf16[224,3600]{1,0:T(8,128)(2,1)S(1)} custom-call(bf16[16,16,3600]{2,1,0:T(8,128)(2,1)S(1)} %get-tuple-element.16.tile_ref, bf16[16,3600]{1,0:T(8,128)(2,1)S(1)} %collective-permute-done.low_ref, bf16[16,3600]{1,0:T(8,128)(2,1)S(1)} %collective-permute-done.1.high_ref), custom_call_target="tpu_custom_call" | custom-call | flops 9676800 | bytes 12902400 | tf_op jit(solution)/shard_map/inner_rows/pallas_call | solution.py:253
  35.3 0.3 collective-permute-done.2.above_ref
  35.6 1.0 outer_rows.1
  36.5 9.0 %collective-permute-start.4 = (bf16[16,16,3600]{2,1,0:T(8,128)(2,1)S(1)}, bf16[16,16,3600]{2,1,0:T(8,128)(2,1)}, u32[]{:S(2)}, u32[]{:S(2)}) collective-permute-start(bf16[16,16,3600]{2,1,0:T(8,128)(2,1)S(1)} %bitcast.14), channel_id=1, source_target_pairs={{0,8},{32,56},{1,9},{33,57},{2,10},{34,58},{3,11},{35,59},{4,12},{... | collective-permute-start | bytes 5529608 | tf_op jit(solution)/shard_map/ppermute | solution.py:288
  45.6 4.3 %all_to_all.10 = bf16[2,64,3600]{2,1,0:T(8,128)(2,1)S(1)} all-to-all(bf16[2,64,3600]{2,1,0:T(8,128)(2,1)S(1)} %bitcast.15), channel_id=1, replica_groups=mesh['z'=8,'core'=2,'x'=4,'y'=8] {'core'}, dimensions={0} | all-to-all | bytes 1843200 | tf_op jit(solution)/shard_map/all_to_all | solution.py:290
  49.9 0.3 reduce_sum.37
  50.2 0.2 reshape.42
  50.4 21.7 %all_to_all.11 = bf16[32,2,3600]{2,1,0:T(2,128)(2,1)S(1)} all-to-all(bf16[32,2,3600]{2,1,0:T(2,128)(2,1)S(1)} %reshape.42), channel_id=1, replica_groups=mesh['z'=8,'core'=2,'x'=4,'y'=8] {'x','y'}, dimensions={0} | all-to-all | bytes 921600 | tf_op jit(solution)/shard_map/all_to_all | solution.py:294
  72.1 0.4 reduce_sum.38
  72.5 7.6 %best_scores.1 = (f32[1,256]{1,0:T(1,128)S(1)}, f32[1,256]{1,0:T(1,128)S(1)}) custom-call(bf16[256,3600]{1,0:T(8,128)(2,1)S(1)} %get-tuple-element.19.own_ref, bf16[256,3600]{1,0:T(8,128)(2,1)} %bitcast.7.other_ref, bf16[1024,3600]{1,0:T(8,128)(2,1)} %all-gather.4.cloned.1.call-done.panel_ref), custom_call_target="tpu_custom_call" | custom-call | tf_op jit(solution)/shard_map/best_scores/pallas_call | solution.py:299
  80.1 4.4 %collective-permute-start.5 = (f32[1,256]{1,0:T(1,128)S(1)}, f32[1,256]{1,0:T(1,128)S(1)}, u32[]{:S(2)}, u32[]{:S(2)}) collective-permute-start(f32[1,256]{1,0:T(1,128)S(1)} %get-tuple-element.23), channel_id=1, source_target_pairs={{0,8},{32,56},{1,9},{33,57},{2,10},{34,58},{3,11},{35,59},{4,12},{... | collective-permute-start | bytes 3080 | tf_op jit(solution)/shard_map/ppermute | solution.py:313
  84.6 22.6 %all-gather.1.totals_ref = bf16[16,2,3600]{2,1,0:T(2,128)(2,1)S(1)} all-gather(bf16[1,2,3600]{2,1,0:T(2,128)(2,1)S(1)} %bitcast.17), channel_id=2, replica_groups=mesh['z'=8,'core'=2,'x'=4,'y'=8] {'z','core'}, dimensions={0}, use_global_device_ids=true | all-gather | bytes 244800 | tf_op jit(solution)/shard_map/all_gather | solution.py:315
  107.2 0.8 finish.1
  (19 shorter events, 0.3 us)
Async XLA Ops:
  7.2 65.4 %all-gather.4.cloned.1.call-start = ((), (), s32[]{:S(2)}) async-start(), calls=%async_computation.2 | async-start | bytes 8077312 | tf_op jit(solution)/shard_map/all_gather | solution.py:207
  10.3 14.6 %copy-start = (s32[16,16]{1,0:T(8,128)S(1)}, s32[16,16]{1,0:T(8,128)}, u32[]{:S(2)}) copy-start(s32[16,16]{1,0:T(8,128)} %param.10) | copy-start | bytes 3076
  10.3 14.7 %copy-start.1 = (s32[16,16]{1,0:T(8,128)S(1)}, s32[16,16]{1,0:T(8,128)}, u32[]{:S(2)}) copy-start(s32[16,16]{1,0:T(8,128)} %param.9) | copy-start | bytes 3076
  10.3 14.8 %copy-start.2 = (s32[128]{0:T(128)S(1)}, s32[128]{0:T(128)}, u32[]{:S(2)}) copy-start(s32[128]{0:T(128)} %param.11) | copy-start | bytes 1540
  14.8 10.5 %collective-permute-start = (bf16[16,3600]{1,0:T(8,128)(2,1)S(1)}, bf16[16,3600]{1,0:T(8,128)(2,1)S(1)}, u32[]{:S(2)}, u32[]{:S(2)}) collective-permute-start(bf16[16,3600]{1,0:T(8,128)(2,1)S(1)} %get-tuple-element.17), channel_id=1, source_target_pairs={{0,32},{32,64},{64,96},{96,128},{128,160},{160,192},{192,224},{224... | collective-permute-start | bytes 345608 | tf_op jit(solution)/shard_map/ppermute | solution.py:234
  20.2 6.2 %collective-permute-start.1 = (bf16[16,3600]{1,0:T(8,128)(2,1)S(1)}, bf16[16,3600]{1,0:T(8,128)(2,1)S(1)}, u32[]{:S(2)}, u32[]{:S(2)}) collective-permute-start(bf16[16,3600]{1,0:T(8,128)(2,1)S(1)} %get-tuple-element.18), channel_id=1, source_target_pairs={{32,0},{64,32},{96,64},{128,96},{160,128},{192,160},{224,192},{256... | collective-permute-start | bytes 345608 | tf_op jit(solution)/shard_map/ppermute | solution.py:235
  26.5 8.8 %collective-permute-start.3 = (bf16[18,3600]{1,0:T(8,128)(2,1)S(1)}, bf16[18,3600]{1,0:T(8,128)(2,1)S(1)}, u32[]{:S(2)}, u32[]{:S(2)}) collective-permute-start(bf16[18,3600]{1,0:T(8,128)(2,1)S(1)} %pad_maximum_fusion.1), channel_id=1, source_target_pairs={{1,0},{2,1},{3,2},{4,3},{5,4},{6,5},{7,6},{8,7},{9,8},{10,9},{11,1... | collective-permute-start | bytes 388808 | tf_op jit(solution)/shard_map/ppermute | solution.py:244
  27.8 7.7 %collective-permute-start.2 = (bf16[18,3600]{1,0:T(8,128)(2,1)S(1)}, bf16[18,3600]{1,0:T(8,128)(2,1)S(1)}, u32[]{:S(2)}, u32[]{:S(2)}) collective-permute-start(bf16[18,3600]{1,0:T(8,128)(2,1)S(1)} %pad_maximum_fusion), channel_id=1, source_target_pairs={{0,1},{1,2},{2,3},{3,4},{4,5},{5,6},{6,7},{7,8},{8,9},{9,10},{10,1... | collective-permute-start | bytes 388808 | tf_op jit(solution)/shard_map/ppermute | solution.py:243
  36.5 36.0 %collective-permute-start.4 = (bf16[16,16,3600]{2,1,0:T(8,128)(2,1)S(1)}, bf16[16,16,3600]{2,1,0:T(8,128)(2,1)}, u32[]{:S(2)}, u32[]{:S(2)}) collective-permute-start(bf16[16,16,3600]{2,1,0:T(8,128)(2,1)S(1)} %bitcast.14), channel_id=1, source_target_pairs={{0,8},{32,56},{1,9},{33,57},{2,10},{34,58},{3,11},{35,59},{4,12},{... | collective-permute-start | bytes 5529608 | tf_op jit(solution)/shard_map/ppermute | solution.py:288
  80.1 27.1 %collective-permute-start.5 = (f32[1,256]{1,0:T(1,128)S(1)}, f32[1,256]{1,0:T(1,128)S(1)}, u32[]{:S(2)}, u32[]{:S(2)}) collective-permute-start(f32[1,256]{1,0:T(1,128)S(1)} %get-tuple-element.23), channel_id=1, source_target_pairs={{0,8},{32,56},{1,9},{33,57},{2,10},{34,58},{3,11},{35,59},{4,12},{... | collective-permute-start | bytes 3080 | tf_op jit(solution)/shard_map/ppermute | solution.py:313
Sparse Core Ops, SparseCore 0:
  10.4 61.5 all-gather.3

commit v5 on v4

--- a/solution.py
+++ b/solution.py
@@ -51,19 +51,10 @@
         ).astype(jnp.bfloat16)
 
 
-def filter_tile(background_ref, tile_hbm, out_ref, low_ref, high_ref, tile_ref, low, high, arrived):
-    rows, cols, pixels = tile_ref.shape
-    parts = arrived.shape[0]
-    step = rows // parts
-    copies = []
-    for part in range(parts):
-        lines = pl.ds(part * step, step)
-        copies.append(pltpu.make_async_copy(tile_hbm.at[lines], tile_ref.at[lines], arrived.at[part]))
-        copies[-1].start()
+def filter_tile(background_ref, tile_ref, out_ref, low_ref, high_ref, low, high):
     background = background_ref[...].reshape(1, -1)
+    rows, _, pixels = tile_ref.shape
     for row in range(rows):
-        if row % step == 0:
-            copies[row // step].wait()
         values = tile_ref[row] - background
         values = values - jnp.sum(values, axis=-1, keepdims=True) * (1.0 / pixels)
         mean_square = jnp.sum(values * values, axis=-1, keepdims=True) * (1.0 / pixels)
@@ -110,7 +101,7 @@
 
 def outer_rows(
     point_row_ref, first_ref, second_ref, third_ref, fourth_ref, low_ref, high_ref, above_ref, below_ref,
-    inner_ref, out_ref, sums_ref, shift,
+    inner_ref, out_ref, kept_ref, sent_ref, shift,
 ):
     points, pixels = out_ref.shape
     cols = first_ref.shape[0]
@@ -131,17 +122,17 @@
                 + values[row + inward : row + inward + 1]
             )
         out_ref[row * cols : (row + 1) * cols, :] = index_points(column, edges[0], edges[1], shift)
-    grains = sums_ref.shape[0]
-    k = lax.broadcasted_iota(jnp.int32, (grains, points), 0)
-    half = grains // 2
-    grain = (k % half) // 2 * 4 + k // half * 2 + k % 2
+    half = kept_ref.shape[0]
+    k = lax.broadcasted_iota(jnp.int32, (2 * half, points), 0)
+    core = lax.axis_index("core") ^ (k // half)
+    grain = (k % half) // 2 * 4 + core * 2 + k % 2
     selector = jnp.where(grain == point_row_ref[...], 1.0, 0.0).astype(jnp.bfloat16)
     step = 1024
     for start in range(0, pixels, step):
         stop = min(start + step, pixels)
-        sums_ref[:, start:stop] = jnp.dot(
-            selector, out_ref[:, start:stop], preferred_element_type=jnp.float32
-        ).astype(jnp.bfloat16)
+        sums = jnp.dot(selector, out_ref[:, start:stop], preferred_element_type=jnp.float32)
+        kept_ref[:, start:stop] = sums[:half]
+        sent_ref[:, start:stop] = sums[half:].astype(jnp.bfloat16)
 
 
 def best_scores(own_ref, other_ref, panel_ref, own_best_ref, other_best_ref, points_ref, best_ref):
@@ -207,21 +198,25 @@
     panels = lax.all_gather(panel, DICT, axis=0, tiled=True)
 
     patterns, panel = lax.optimization_barrier((patterns, panel))
+    block = tile_rows // 2
     filtered, low_edge, high_edge = pl.pallas_call(
         filter_tile,
+        grid=(tile_rows // block,),
         out_shape=(
             jax.ShapeDtypeStruct((tile_rows, tile_cols, pixels), bf16),
             jax.ShapeDtypeStruct((tile_rows, pixels), bf16),
             jax.ShapeDtypeStruct((tile_rows, pixels), bf16),
         ),
-        in_specs=[pl.BlockSpec(memory_space=VMEM), pl.BlockSpec(memory_space=pl.ANY)],
-        out_specs=(pl.BlockSpec(memory_space=VMEM),) * 3,
-        scratch_shapes=[
-            VMEM((tile_rows, tile_cols, pixels), f32),
-            VMEM((tile_rows, pixels), f32),
-            VMEM((tile_rows, pixels), f32),
-            pltpu.SemaphoreType.DMA((8,)),
+        in_specs=[
+            pl.BlockSpec((pixels,), lambda i: (0,)),
+            pl.BlockSpec((block, tile_cols, pixels), lambda i: (i, 0, 0)),
         ],
+        out_specs=(
+            pl.BlockSpec((block, tile_cols, pixels), lambda i: (i, 0, 0)),
+            pl.BlockSpec((block, pixels), lambda i: (i, 0)),
+            pl.BlockSpec((block, pixels), lambda i: (i, 0)),
+        ),
+        scratch_shapes=[VMEM((block, pixels), f32)] * 2,
         compiler_params=params(16),
         name="filter_tile",
     )(
@@ -263,14 +258,15 @@
         ),
         name="inner_rows",
     )(filtered, low, high)
-    indexed, sums = pl.pallas_call(
+    indexed, kept, sent = pl.pallas_call(
         outer_rows,
         out_shape=(
             jax.ShapeDtypeStruct((points, pixels), bf16),
-            jax.ShapeDtypeStruct((grain_count, pixels), bf16),
+            jax.ShapeDtypeStruct((grain_count // 2, pixels), f32),
+            jax.ShapeDtypeStruct((grain_count // 2, pixels), bf16),
         ),
         in_specs=[pl.BlockSpec(memory_space=VMEM)] * 10,
-        out_specs=[pl.BlockSpec(memory_space=VMEM)] * 2,
+        out_specs=[pl.BlockSpec(memory_space=VMEM)] * 3,
         scratch_shapes=[VMEM((32, pixels), f32)],
         compiler_params=params(10),
         name="outer_rows",
@@ -285,12 +281,10 @@
                     at = (z * 2 + core) * xs
                     partner = (((x + core) ^ 1) - core) % xs
                     trade.append(((at + x) * ys + y, (at + partner) * ys + y))
+    swapped = lax.ppermute(sent, "core", [(0, 1), (1, 0)])
     other = lax.ppermute(indexed.reshape(patterns.shape), EVERY, trade).reshape(points, pixels)
 
-    halves = lax.all_to_all(
-        sums.reshape(2, grain_count // 2, pixels), "core", 0, 0, tiled=True
-    )
-    chip_sums = jnp.sum(halves.astype(f32), axis=0).astype(bf16)
+    chip_sums = (kept + swapped.astype(f32)).astype(bf16)
     parts = lax.all_to_all(chip_sums.reshape(lines, -1, pixels), SCAN, 0, 0, tiled=True)
     group_total = jnp.sum(parts.astype(f32), axis=0).astype(bf16)
 

time: 115 us -> 116 us (level)
  starting transfers between devices: 28.9 us -> 31.1 us
  Pallas kernels: 20.3 us -> 19 us
    all_to_all x1 -> x0, blocking collectives: 4.28 us -> none  [shards(): lax.all_to_all(sums.reshape(2, grain_count // 2, pixels), 'core', 0, 0, t...]
    all_to_all x1, blocking collectives: 21.7 us -> 25.9 us  [shards(): lax.all_to_all(chip_sums.reshape(lines, -1, pixels), SCAN, 0, 0, tiled=True)]
    ppermute x0 -> x1, starting transfers between devices: none -> 2.85 us  [shards(): swapped = lax.ppermute(sent, 'core', [(0, 1), (1, 0)])]
    pallas_call x1, Pallas kernels: 4.47 us -> 3.1 us  [shards(): pl.pallas_call(filter_tile, grid=(tile_rows // block,), out_shape=(jax.Sh...]
  transfers between devices with their start and end apart: 7 -> 8, of which waited for: 2 -> 2; matrix products, arithmetic and copies ran while one was open for 1% -> 1% of each run, Pallas kernels for 8% -> 7%
where the time goes in v5:
time: 116 us; the launch traced here: 115 us
  blocking collectives  48.6 us (42%)
  starting transfers between devices  31.1 us (27%)
  Pallas kernels  19 us (16%)
  between operations  14.3 us (12%)
  waiting for transfers between devices  1.3 us (1%)
    all_to_all x1, blocking collectives, shards(): lax.all_to_all(chip_sums.reshape(lines, -1, pixels), SCAN, 0, 0, tiled=True)  25.9 us
    all_gather x1, blocking collectives, shards(): group_totals = lax.all_gather(group_total, DICT, axis=0, tiled=False)  22.6 us
    ppermute x1, starting transfers between devices, shards(): lax.ppermute(indexed.reshape(patterns.shape), EVERY, trade)  8.15 us
    pallas_call x1, Pallas kernels, shards(): pl.pallas_call(best_scores, grid=(panels.shape[0] // block,), out_shape=(...  7.57 us
    ppermute x1, starting transfers between devices, shards(): low = lax.ppermute(high_edge, DICT, forward)  5.39 us
    ppermute x1, starting transfers between devices, shards(): returned = lax.ppermute(other_best, EVERY, trade)  4.73 us
    ppermute x1, starting transfers between devices, shards(): high = lax.ppermute(low_edge, DICT, backward)  4.69 us
    ppermute x1, starting transfers between devices, shards(): above = lax.ppermute(strip(tile_rows - 1), SCAN, forward)  4 us
  transfers between devices with their start and end apart: 8, of which 2 were waited for; matrix products, arithmetic and copies ran while one was open for 1% of the time, Pallas kernels for 7%

profile of v5, /device:TPU:1, one launch (start us, length us, event | category | flops | bytes accessed | tf_op | source)
XLA Modules:
  0.0 115.4 jit_solution(18140671480526266587)
XLA Ops:
  7.2 0.0 all-gather.4.cloned.1.call-start
  7.2 3.1 %normalise_templates.1 = bf16[64,3600]{1,0:T(8,128)(2,1)} custom-call(bf16[3600,128]{1,0:T(8,128)(2,1)} %bitcast.14), custom_call_target="tpu_custom_call" | custom-call | tf_op jit(solution)/shard_map/normalise_templates/pallas_call | solution.py:189
  10.3 3.1 %filter_tile.1 = (bf16[16,16,3600]{2,1,0:T(8,128)(2,1)S(1)}, bf16[16,3600]{1,0:T(8,128)(2,1)S(1)}, bf16[16,3600]{1,0:T(8,128)(2,1)S(1)}) custom-call(f32[3600]{0:T(1024)} %background_ref.1, f32[16,16,3600]{2,1,0:T(8,128)} %tile_ref), custom_call_target="tpu_custom_call" | custom-call | tf_op jit(solution)/shard_map/filter_tile/pallas_call | solution.py:202
  13.4 5.4 %collective-permute-start = (bf16[16,3600]{1,0:T(8,128)(2,1)S(1)}, bf16[16,3600]{1,0:T(8,128)(2,1)S(1)}, u32[]{:S(2)}, u32[]{:S(2)}) collective-permute-start(bf16[16,3600]{1,0:T(8,128)(2,1)S(1)} %get-tuple-element.18), channel_id=1, source_target_pairs={{0,32},{32,64},{64,96},{96,128},{128,160},{160,192},{192,224},{224... | collective-permute-start | bytes 345608 | tf_op jit(solution)/shard_map/ppermute | solution.py:229
  18.8 4.7 %collective-permute-start.1 = (bf16[16,3600]{1,0:T(8,128)(2,1)S(1)}, bf16[16,3600]{1,0:T(8,128)(2,1)S(1)}, u32[]{:S(2)}, u32[]{:S(2)}) collective-permute-start(bf16[16,3600]{1,0:T(8,128)(2,1)S(1)} %get-tuple-element.19), channel_id=1, source_target_pairs={{32,0},{64,32},{96,64},{128,96},{160,128},{192,160},{224,192},{256... | collective-permute-start | bytes 345608 | tf_op jit(solution)/shard_map/ppermute | solution.py:230
  23.6 0.1 eq.33
  23.7 0.1 eq.34
  23.8 0.2 select_reduce_fusion
  24.0 1.0 collective-permute-done.1.high_ref
  25.1 1.3 %collective-permute-start.3 = (bf16[18,3600]{1,0:T(8,128)(2,1)S(1)}, bf16[18,3600]{1,0:T(8,128)(2,1)S(1)}, u32[]{:S(2)}, u32[]{:S(2)}) collective-permute-start(bf16[18,3600]{1,0:T(8,128)(2,1)S(1)} %pad_maximum_fusion.1), channel_id=1, source_target_pairs={{1,0},{2,1},{3,2},{4,3},{5,4},{6,5},{7,6},{8,7},{9,8},{10,9},{11,1... | collective-permute-start | bytes 388808 | tf_op jit(solution)/shard_map/ppermute | solution.py:239
  26.4 4.0 %collective-permute-start.2 = (bf16[18,3600]{1,0:T(8,128)(2,1)S(1)}, bf16[18,3600]{1,0:T(8,128)(2,1)S(1)}, u32[]{:S(2)}, u32[]{:S(2)}) collective-permute-start(bf16[18,3600]{1,0:T(8,128)(2,1)S(1)} %pad_maximum_fusion), channel_id=1, source_target_pairs={{0,1},{1,2},{2,3},{3,4},{4,5},{5,6},{6,7},{7,8},{8,9},{9,10},{10,1... | collective-permute-start | bytes 388808 | tf_op jit(solution)/shard_map/ppermute | solution.py:238
  30.4 3.5 %inner_rows.1.inner_ref = bf16[224,3600]{1,0:T(8,128)(2,1)S(1)} custom-call(bf16[16,16,3600]{2,1,0:T(8,128)(2,1)S(1)} %get-tuple-element.17.tile_ref, bf16[16,3600]{1,0:T(8,128)(2,1)S(1)} %collective-permute-done.low_ref, bf16[16,3600]{1,0:T(8,128)(2,1)S(1)} %collective-permute-done.1.high_ref), custom_call_target="tpu_custom_call" | custom-call | flops 9676800 | bytes 12902400 | tf_op jit(solution)/shard_map/inner_rows/pallas_call | solution.py:248
  33.9 0.3 collective-permute-done.2.above_ref
  34.2 1.0 outer_rows.1
  35.2 2.9 %collective-permute-start.5 = (bf16[64,3600]{1,0:T(8,128)(2,1)S(1)}, bf16[64,3600]{1,0:T(8,128)(2,1)S(1)}, u32[]{:S(2)}, u32[]{:S(2)}) collective-permute-start(bf16[64,3600]{1,0:T(8,128)(2,1)S(1)} %get-tuple-element.22), channel_id=1, source_target_pairs={{0,32},{32,0},{1,33},{33,1},{2,34},{34,2},{3,35},{35,3},{4,36},{36... | collective-permute-start | bytes 1382408 | tf_op jit(solution)/shard_map/ppermute | solution.py:284
  38.0 8.1 %collective-permute-start.4 = (bf16[16,16,3600]{2,1,0:T(8,128)(2,1)S(1)}, bf16[16,16,3600]{2,1,0:T(8,128)(2,1)}, u32[]{:S(2)}, u32[]{:S(2)}) collective-permute-start(bf16[16,16,3600]{2,1,0:T(8,128)(2,1)S(1)} %bitcast.13), channel_id=1, source_target_pairs={{0,8},{32,56},{1,9},{33,57},{2,10},{34,58},{3,11},{35,59},{4,12},{... | collective-permute-start | bytes 5529608 | tf_op jit(solution)/shard_map/ppermute | solution.py:285
  46.2 0.1 add_convert_fusion
  46.3 0.2 reshape.38
  46.5 25.9 %all_to_all.5 = bf16[32,2,3600]{2,1,0:T(2,128)(2,1)S(1)} all-to-all(bf16[32,2,3600]{2,1,0:T(2,128)(2,1)S(1)} %reshape.38), channel_id=1, replica_groups=mesh['z'=8,'core'=2,'x'=4,'y'=8] {'x','y'}, dimensions={0} | all-to-all | bytes 921600 | tf_op jit(solution)/shard_map/all_to_all | solution.py:288
  72.4 0.4 reduce_sum.25
  72.9 7.6 %best_scores.1 = (f32[1,256]{1,0:T(1,128)S(1)}, f32[1,256]{1,0:T(1,128)S(1)}) custom-call(bf16[256,3600]{1,0:T(8,128)(2,1)S(1)} %get-tuple-element.20.own_ref, bf16[256,3600]{1,0:T(8,128)(2,1)} %bitcast.7.other_ref, bf16[1024,3600]{1,0:T(8,128)(2,1)} %all-gather.4.cloned.1.call-done.panel_ref), custom_call_target="tpu_custom_call" | custom-call | tf_op jit(solution)/shard_map/best_scores/pallas_call | solution.py:293
  80.4 4.7 %collective-permute-start.6 = (f32[1,256]{1,0:T(1,128)S(1)}, f32[1,256]{1,0:T(1,128)S(1)}, u32[]{:S(2)}, u32[]{:S(2)}) collective-permute-start(f32[1,256]{1,0:T(1,128)S(1)} %get-tuple-element.25), channel_id=1, source_target_pairs={{0,8},{32,56},{1,9},{33,57},{2,10},{34,58},{3,11},{35,59},{4,12},{... | collective-permute-start | bytes 3080 | tf_op jit(solution)/shard_map/ppermute | solution.py:307
  85.2 22.6 %all-gather.1.totals_ref = bf16[16,2,3600]{2,1,0:T(2,128)(2,1)S(1)} all-gather(bf16[1,2,3600]{2,1,0:T(2,128)(2,1)S(1)} %bitcast.15), channel_id=2, replica_groups=mesh['z'=8,'core'=2,'x'=4,'y'=8] {'z','core'}, dimensions={0}, use_global_device_ids=true | all-gather | bytes 244800 | tf_op jit(solution)/shard_map/all_gather | solution.py:309
  107.8 0.8 finish.1
  (20 shorter events, 0.3 us)
Async XLA Ops:
  7.2 65.7 %all-gather.4.cloned.1.call-start = ((), (), s32[]{:S(2)}) async-start(), calls=%async_computation.1 | async-start | bytes 8077312 | tf_op jit(solution)/shard_map/all_gather | solution.py:198
  10.3 13.2 %copy-start = (s32[16,16]{1,0:T(8,128)S(1)}, s32[16,16]{1,0:T(8,128)}, u32[]{:S(2)}) copy-start(s32[16,16]{1,0:T(8,128)} %param.10) | copy-start | bytes 3076
  10.3 13.3 %copy-start.1 = (s32[16,16]{1,0:T(8,128)S(1)}, s32[16,16]{1,0:T(8,128)}, u32[]{:S(2)}) copy-start(s32[16,16]{1,0:T(8,128)} %param.9) | copy-start | bytes 3076
  10.3 13.5 %copy-start.2 = (s32[128]{0:T(128)S(1)}, s32[128]{0:T(128)}, u32[]{:S(2)}) copy-start(s32[128]{0:T(128)} %param.11) | copy-start | bytes 1540
  13.4 10.5 %collective-permute-start = (bf16[16,3600]{1,0:T(8,128)(2,1)S(1)}, bf16[16,3600]{1,0:T(8,128)(2,1)S(1)}, u32[]{:S(2)}, u32[]{:S(2)}) collective-permute-start(bf16[16,3600]{1,0:T(8,128)(2,1)S(1)} %get-tuple-element.18), channel_id=1, source_target_pairs={{0,32},{32,64},{64,96},{96,128},{128,160},{160,192},{192,224},{224... | collective-permute-start | bytes 345608 | tf_op jit(solution)/shard_map/ppermute | solution.py:229
  18.8 6.2 %collective-permute-start.1 = (bf16[16,3600]{1,0:T(8,128)(2,1)S(1)}, bf16[16,3600]{1,0:T(8,128)(2,1)S(1)}, u32[]{:S(2)}, u32[]{:S(2)}) collective-permute-start(bf16[16,3600]{1,0:T(8,128)(2,1)S(1)} %get-tuple-element.19), channel_id=1, source_target_pairs={{32,0},{64,32},{96,64},{128,96},{160,128},{192,160},{224,192},{256... | collective-permute-start | bytes 345608 | tf_op jit(solution)/shard_map/ppermute | solution.py:230
  25.1 8.8 %collective-permute-start.3 = (bf16[18,3600]{1,0:T(8,128)(2,1)S(1)}, bf16[18,3600]{1,0:T(8,128)(2,1)S(1)}, u32[]{:S(2)}, u32[]{:S(2)}) collective-permute-start(bf16[18,3600]{1,0:T(8,128)(2,1)S(1)} %pad_maximum_fusion.1), channel_id=1, source_target_pairs={{1,0},{2,1},{3,2},{4,3},{5,4},{6,5},{7,6},{8,7},{9,8},{10,9},{11,1... | collective-permute-start | bytes 388808 | tf_op jit(solution)/shard_map/ppermute | solution.py:239
  26.4 7.7 %collective-permute-start.2 = (bf16[18,3600]{1,0:T(8,128)(2,1)S(1)}, bf16[18,3600]{1,0:T(8,128)(2,1)S(1)}, u32[]{:S(2)}, u32[]{:S(2)}) collective-permute-start(bf16[18,3600]{1,0:T(8,128)(2,1)S(1)} %pad_maximum_fusion), channel_id=1, source_target_pairs={{0,1},{1,2},{2,3},{3,4},{4,5},{5,6},{6,7},{7,8},{8,9},{9,10},{10,1... | collective-permute-start | bytes 388808 | tf_op jit(solution)/shard_map/ppermute | solution.py:238
  35.2 11.0 %collective-permute-start.5 = (bf16[64,3600]{1,0:T(8,128)(2,1)S(1)}, bf16[64,3600]{1,0:T(8,128)(2,1)S(1)}, u32[]{:S(2)}, u32[]{:S(2)}) collective-permute-start(bf16[64,3600]{1,0:T(8,128)(2,1)S(1)} %get-tuple-element.22), channel_id=1, source_target_pairs={{0,32},{32,0},{1,33},{33,1},{2,34},{34,2},{3,35},{35,3},{4,36},{36... | collective-permute-start | bytes 1382408 | tf_op jit(solution)/shard_map/ppermute | solution.py:284
  38.0 34.8 %collective-permute-start.4 = (bf16[16,16,3600]{2,1,0:T(8,128)(2,1)S(1)}, bf16[16,16,3600]{2,1,0:T(8,128)(2,1)}, u32[]{:S(2)}, u32[]{:S(2)}) collective-permute-start(bf16[16,16,3600]{2,1,0:T(8,128)(2,1)S(1)} %bitcast.13), channel_id=1, source_target_pairs={{0,8},{32,56},{1,9},{33,57},{2,10},{34,58},{3,11},{35,59},{4,12},{... | collective-permute-start | bytes 5529608 | tf_op jit(solution)/shard_map/ppermute | solution.py:285
  80.4 27.4 %collective-permute-start.6 = (f32[1,256]{1,0:T(1,128)S(1)}, f32[1,256]{1,0:T(1,128)S(1)}, u32[]{:S(2)}, u32[]{:S(2)}) collective-permute-start(f32[1,256]{1,0:T(1,128)S(1)} %get-tuple-element.25), channel_id=1, source_target_pairs={{0,8},{32,56},{1,9},{33,57},{2,10},{34,58},{3,11},{35,59},{4,12},{... | collective-permute-start | bytes 3080 | tf_op jit(solution)/shard_map/ppermute | solution.py:307
Sparse Core Ops, SparseCore 0:
  10.4 61.5 all-gather.3

commit v6 on v5

--- a/solution.py
+++ b/solution.py
@@ -1,3 +1,4 @@
+import functools
 import math
 
 import jax
@@ -135,38 +136,50 @@
         sent_ref[:, start:stop] = sums[half:].astype(jnp.bfloat16)
 
 
-def best_scores(own_ref, other_ref, panel_ref, own_best_ref, other_best_ref, points_ref, best_ref):
-    points = own_ref.shape[0]
+def lane_best(best, scores):
+    lanes = best.shape[1]
+    for start in range(0, scores.shape[1], lanes):
+        best = jnp.maximum(best, scores[:, start : start + lanes])
+    return best
+
+
+def products(points, panel):
+    return lax.dot_general(points, panel, (((1,), (1,)), ((), ())), preferred_element_type=jnp.float32)
+
+
+def own_scores(points_ref, panel_ref, out_ref, best_ref):
     step = pl.program_id(0)
 
     @pl.when(step == 0)
     def _():
-        points_ref[:points, :] = own_ref[...]
-        points_ref[points:, :] = other_ref[...]
         best_ref[...] = jnp.full(best_ref.shape, -jnp.inf, jnp.float32)
 
-    scores = lax.dot_general(
-        points_ref[...], panel_ref[...], (((1,), (1,)), ((), ())), preferred_element_type=jnp.float32
-    )
-    lanes = best_ref.shape[1]
-    best = best_ref[...]
-    for start in range(0, scores.shape[1], lanes):
-        best = jnp.maximum(best, scores[:, start : start + lanes])
+    best = lane_best(best_ref[...], products(points_ref[...], panel_ref[...]))
     best_ref[...] = best
 
     @pl.when(step == pl.num_programs(0) - 1)
     def _():
-        best = jnp.max(best_ref[...].T, axis=0, keepdims=True)
-        own_best_ref[...] = best[:, :points]
-        other_best_ref[...] = best[:, points:]
-
-
-def finish(own_best_ref, returned_ref, totals_ref, max_score_ref, patterns_ref):
-    pixels = patterns_ref.shape[1]
+        out_ref[...] = jnp.max(best.T, axis=0, keepdims=True)
+
+
+def other_scores(points_ref, panel_ref, out_ref):
+    points = points_ref[...]
+    best = jnp.full((points.shape[0], 128), -jnp.inf, jnp.float32)
+    block = 512
+    for start in range(0, panel_ref.shape[0], block):
+        best = lane_best(best, products(points, panel_ref[start : start + block, :]))
+    out_ref[...] = jnp.max(best.T, axis=0, keepdims=True)
+
+
+def finish_scores(own_best_ref, returned_ref, max_score_ref, pixels):
     rows, cols = max_score_ref.shape
     best = jnp.maximum(own_best_ref[...], returned_ref[...]) * (1.0 / math.sqrt(pixels))
     for row in range(rows):
         max_score_ref[row : row + 1, :] = best[:, row * cols : (row + 1) * cols]
+
+
+def finish_patterns(totals_ref, patterns_ref):
+    pixels = patterns_ref.shape[1]
     groups = totals_ref.shape[0] // 2
     for core in range(2):
         total = totals_ref[core].astype(jnp.float32)
@@ -282,43 +295,66 @@
                     partner = (((x + core) ^ 1) - core) % xs
                     trade.append(((at + x) * ys + y, (at + partner) * ys + y))
     swapped = lax.ppermute(sent, "core", [(0, 1), (1, 0)])
-    other = lax.ppermute(indexed.reshape(patterns.shape), EVERY, trade).reshape(points, pixels)
-
     chip_sums = (kept + swapped.astype(f32)).astype(bf16)
     parts = lax.all_to_all(chip_sums.reshape(lines, -1, pixels), SCAN, 0, 0, tiled=True)
     group_total = jnp.sum(parts.astype(f32), axis=0).astype(bf16)
 
+    ready, group_total = lax.optimization_barrier((indexed, group_total))
+    other = lax.ppermute(ready.reshape(patterns.shape), EVERY, trade)
+
     block = 512
-    scored, group_total = lax.optimization_barrier((other, group_total))
-    own_best, other_best = pl.pallas_call(
-        best_scores,
+    own_best = pl.pallas_call(
+        own_scores,
         grid=(panels.shape[0] // block,),
-        out_shape=(jax.ShapeDtypeStruct((1, points), f32),) * 2,
+        out_shape=jax.ShapeDtypeStruct((1, points), f32),
         in_specs=[
-            pl.BlockSpec((points, pixels), lambda i: (0, 0)),
             pl.BlockSpec((points, pixels), lambda i: (0, 0)),
             pl.BlockSpec((block, pixels), lambda i: (i, 0)),
         ],
-        out_specs=(pl.BlockSpec((1, points), lambda i: (0, 0)),) * 2,
-        scratch_shapes=[VMEM((2 * points, pixels), bf16), VMEM((2 * points, 128), f32)],
-        compiler_params=params(28),
-        name="best_scores",
-    )(indexed, scored, pltpu.with_memory_space_constraint(panels, pltpu.HBM))
+        out_specs=pl.BlockSpec((1, points), lambda i: (0, 0)),
+        scratch_shapes=[VMEM((points, 128), f32)],
+        compiler_params=params(20),
+        cost_estimate=pl.CostEstimate(
+            flops=2 * points * pixels * panels.shape[0],
+            bytes_accessed=2 * pixels * panels.shape[0],
+            transcendentals=0,
+        ),
+        name="own_scores",
+    )(ready, pltpu.with_memory_space_constraint(panels, pltpu.HBM))
+    own_best, group_total, panels = lax.optimization_barrier((own_best, group_total, panels))
+    group_totals = lax.all_gather(group_total, DICT, axis=0, tiled=False)
+    other, group_totals = lax.optimization_barrier((other, group_totals))
+    grain_patterns = pl.pallas_call(
+        finish_patterns,
+        out_shape=jax.ShapeDtypeStruct((2 * group_total.shape[0], pixels), f32),
+        in_specs=[pl.BlockSpec(memory_space=VMEM)],
+        out_specs=pl.BlockSpec(memory_space=VMEM),
+        compiler_params=params(4),
+        name="finish_patterns",
+    )(group_totals)
+    other_best = pl.pallas_call(
+        other_scores,
+        out_shape=jax.ShapeDtypeStruct((1, points), f32),
+        in_specs=[pl.BlockSpec(memory_space=VMEM)] * 2,
+        out_specs=pl.BlockSpec(memory_space=VMEM),
+        compiler_params=params(12),
+        cost_estimate=pl.CostEstimate(
+            flops=2 * points * pixels * panels.shape[0],
+            bytes_accessed=2 * pixels * panels.shape[0],
+            transcendentals=0,
+        ),
+        name="other_scores",
+    )(other.reshape(points, pixels), panels)
     returned = lax.ppermute(other_best, EVERY, trade)
-    other_best, group_total = lax.optimization_barrier((other_best, group_total))
-    group_totals = lax.all_gather(group_total, DICT, axis=0, tiled=False)
-    returned, group_totals = lax.optimization_barrier((returned, group_totals))
-    return pl.pallas_call(
-        finish,
-        out_shape=(
-            jax.ShapeDtypeStruct((tile_rows, tile_cols), f32),
-            jax.ShapeDtypeStruct((2 * group_total.shape[0], pixels), f32),
-        ),
-        in_specs=[pl.BlockSpec(memory_space=VMEM)] * 3,
-        out_specs=[pl.BlockSpec(memory_space=VMEM)] * 2,
-        compiler_params=params(8),
-        name="finish",
-    )(own_best, returned, group_totals)
+    max_score = pl.pallas_call(
+        functools.partial(finish_scores, pixels=pixels),
+        out_shape=jax.ShapeDtypeStruct((tile_rows, tile_cols), f32),
+        in_specs=[pl.BlockSpec(memory_space=VMEM)] * 2,
+        out_specs=pl.BlockSpec(memory_space=VMEM),
+        compiler_params=params(4),
+        name="finish_scores",
+    )(own_best, returned)
+    return (max_score, grain_patterns)
 
 
 def solution(mesh):

time: 116 us -> 114 us (0.983)
  waiting for transfers between devices: 1.3 us -> 10.6 us
  starting transfers between devices: 31.1 us -> 24.4 us
  blocking collectives: 48.6 us -> 42.1 us
  Pallas kernels: 19 us -> 21.2 us
    all_gather x1, waiting for transfers between devices: 0.02 us -> 4.36 us  [shards(): panels = lax.all_gather(panel, DICT, axis=0, tiled=True)]
    ppermute x1, starting transfers between devices: 8.15 us -> 4.28 us  [shards(): other = lax.ppermute(ready.reshape(patterns.shape), EVERY, trade)]
    all_to_all x1, blocking collectives: 25.9 us -> 22.7 us  [shards(): lax.all_to_all(chip_sums.reshape(lines, -1, pixels), SCAN, 0, 0, tiled=True)]
    all_gather x1, blocking collectives: 22.6 us -> 19.4 us  [shards(): group_totals = lax.all_gather(group_total, DICT, axis=0, tiled=False)]
    pallas_call x2 -> x4, Pallas kernels: 8.36 us -> 10.6 us  [the longest x1 5.27 us: shards(): pl.pallas_call(own_scores, grid=(panels.shape[0] // block,), out_shape=ja...]
    ppermute x1, waiting for transfers between devices: 0.01 us -> 2.15 us  [shards(): below = lax.ppermute(strip(0), SCAN, backward)]
    ppermute x1, waiting for transfers between devices: 0.01 us -> 1.81 us  [shards(): swapped = lax.ppermute(sent, 'core', [(0, 1), (1, 0)])]
    ppermute x1, starting transfers between devices: 4.73 us -> 3.53 us  [shards(): returned = lax.ppermute(other_best, EVERY, trade)]
  transfers between devices with their start and end apart: 8 -> 8, of which waited for: 2 -> 5; matrix products, arithmetic and copies ran while one was open for 1% -> 1% of each run, Pallas kernels for 7% -> 12%
where the time goes in v6:
time: 114 us
  blocking collectives  42.1 us (37%)
  starting transfers between devices  24.4 us (21%)
  Pallas kernels  21.2 us (19%)
  between operations  14.2 us (12%)
  waiting for transfers between devices  10.6 us (9%)
    all_to_all x1, blocking collectives, shards(): lax.all_to_all(chip_sums.reshape(lines, -1, pixels), SCAN, 0, 0, tiled=True)  22.7 us
    all_gather x1, blocking collectives, shards(): group_totals = lax.all_gather(group_total, DICT, axis=0, tiled=False)  19.4 us
    ppermute x1, starting transfers between devices, shards(): low = lax.ppermute(high_edge, DICT, forward)  5.39 us
    pallas_call x1, Pallas kernels, shards(): pl.pallas_call(own_scores, grid=(panels.shape[0] // block,), out_shape=ja...  5.27 us
    ppermute x1, starting transfers between devices, shards(): high = lax.ppermute(low_edge, DICT, backward)  4.69 us
    all_gather x1, waiting for transfers between devices, shards(): panels = lax.all_gather(panel, DICT, axis=0, tiled=True)  4.36 us
    ppermute x1, starting transfers between devices, shards(): other = lax.ppermute(ready.reshape(patterns.shape), EVERY, trade)  4.28 us
    pallas_call x1, Pallas kernels, shards(): pl.pallas_call(other_scores, out_shape=jax.ShapeDtypeStruct((1, points),...  3.82 us
  transfers between devices with their start and end apart: 8, of which 5 were waited for; matrix products, arithmetic and copies ran while one was open for 1% of the time, Pallas kernels for 12%

profile of v6, /device:TPU:1, one launch (start us, length us, event | category | flops | bytes accessed | tf_op | source)
XLA Modules:
  0.0 113.6 jit_solution(6219893150986768144)
XLA Ops:
  7.2 3.1 %normalise_templates.1 = bf16[64,3600]{1,0:T(8,128)(2,1)} custom-call(bf16[3600,128]{1,0:T(8,128)(2,1)} %bitcast.14), custom_call_target="tpu_custom_call" | custom-call | tf_op jit(solution)/shard_map/normalise_templates/pallas_call | solution.py:202
  10.3 3.1 %filter_tile.1 = (bf16[16,16,3600]{2,1,0:T(8,128)(2,1)S(1)}, bf16[16,3600]{1,0:T(8,128)(2,1)S(1)}, bf16[16,3600]{1,0:T(8,128)(2,1)S(1)}) custom-call(f32[3600]{0:T(1024)} %background_ref.1, f32[16,16,3600]{2,1,0:T(8,128)} %tile_ref), custom_call_target="tpu_custom_call" | custom-call | tf_op jit(solution)/shard_map/filter_tile/pallas_call | solution.py:215
  13.4 5.4 %collective-permute-start = (bf16[16,3600]{1,0:T(8,128)(2,1)S(1)}, bf16[16,3600]{1,0:T(8,128)(2,1)S(1)}, u32[]{:S(2)}, u32[]{:S(2)}) collective-permute-start(bf16[16,3600]{1,0:T(8,128)(2,1)S(1)} %get-tuple-element.18), channel_id=1, source_target_pairs={{0,32},{32,64},{64,96},{96,128},{128,160},{160,192},{192,224},{224... | collective-permute-start | bytes 345608 | tf_op jit(solution)/shard_map/ppermute | solution.py:242
  18.8 4.7 %collective-permute-start.1 = (bf16[16,3600]{1,0:T(8,128)(2,1)S(1)}, bf16[16,3600]{1,0:T(8,128)(2,1)S(1)}, u32[]{:S(2)}, u32[]{:S(2)}) collective-permute-start(bf16[16,3600]{1,0:T(8,128)(2,1)S(1)} %get-tuple-element.19), channel_id=1, source_target_pairs={{32,0},{64,32},{96,64},{128,96},{160,128},{192,160},{224,192},{256... | collective-permute-start | bytes 345608 | tf_op jit(solution)/shard_map/ppermute | solution.py:243
  24.0 1.0 collective-permute-done.1.high_ref
  25.1 3.2 %collective-permute-start.2 = (bf16[18,3600]{1,0:T(8,128)(2,1)S(1)}, bf16[18,3600]{1,0:T(8,128)(2,1)S(1)}, u32[]{:S(2)}, u32[]{:S(2)}) collective-permute-start(bf16[18,3600]{1,0:T(8,128)(2,1)S(1)} %pad_maximum_fusion), channel_id=1, source_target_pairs={{0,1},{1,2},{2,3},{3,4},{4,5},{5,6},{6,7},{7,8},{8,9},{9,10},{10,1... | collective-permute-start | bytes 388808 | tf_op jit(solution)/shard_map/ppermute | solution.py:251
  28.4 1.3 %collective-permute-start.3 = (bf16[18,3600]{1,0:T(8,128)(2,1)S(1)}, bf16[18,3600]{1,0:T(8,128)(2,1)S(1)}, u32[]{:S(2)}, u32[]{:S(2)}) collective-permute-start(bf16[18,3600]{1,0:T(8,128)(2,1)S(1)} %pad_maximum_fusion.1), channel_id=1, source_target_pairs={{1,0},{2,1},{3,2},{4,3},{5,4},{6,5},{7,6},{8,7},{9,8},{10,9},{11,1... | collective-permute-start | bytes 388808 | tf_op jit(solution)/shard_map/ppermute | solution.py:252
  29.7 3.5 %inner_rows.1.inner_ref = bf16[224,3600]{1,0:T(8,128)(2,1)S(1)} custom-call(bf16[16,16,3600]{2,1,0:T(8,128)(2,1)S(1)} %get-tuple-element.17.tile_ref, bf16[16,3600]{1,0:T(8,128)(2,1)S(1)} %collective-permute-done.low_ref, bf16[16,3600]{1,0:T(8,128)(2,1)S(1)} %collective-permute-done.1.high_ref), custom_call_target="tpu_custom_call" | custom-call | flops 9676800 | bytes 12902400 | tf_op jit(solution)/shard_map/inner_rows/pallas_call | solution.py:261
  33.2 2.1 %collective-permute-done.3.below_ref = bf16[18,3600]{1,0:T(8,128)(2,1)S(1)} collective-permute-done((bf16[18,3600]{1,0:T(8,128)(2,1)S(1)}, bf16[18,3600]{1,0:T(8,128)(2,1)S(1)}, u32[]{:S(2)}, u32[]{:S(2)}) %collective-permute-start.3) | collective-permute-done | bytes 129632 | tf_op jit(solution)/shard_map/ppermute | solution.py:252
  35.3 1.0 outer_rows.1
  36.3 1.9 %collective-permute-start.4 = (bf16[64,3600]{1,0:T(8,128)(2,1)S(1)}, bf16[64,3600]{1,0:T(8,128)(2,1)S(1)}, u32[]{:S(2)}, u32[]{:S(2)}) collective-permute-start(bf16[64,3600]{1,0:T(8,128)(2,1)S(1)} %get-tuple-element.22), channel_id=1, source_target_pairs={{0,32},{32,0},{1,33},{33,1},{2,34},{34,2},{3,35},{35,3},{4,36},{36... | collective-permute-start | bytes 1382408 | tf_op jit(solution)/shard_map/ppermute | solution.py:297
  38.2 1.8 %collective-permute-done.4 = bf16[64,3600]{1,0:T(8,128)(2,1)S(1)} collective-permute-done((bf16[64,3600]{1,0:T(8,128)(2,1)S(1)}, bf16[64,3600]{1,0:T(8,128)(2,1)S(1)}, u32[]{:S(2)}, u32[]{:S(2)}) %collective-permute-start.4) | collective-permute-done | bytes 460832 | tf_op jit(solution)/shard_map/ppermute | solution.py:297
  40.1 0.2 reshape.36
  40.3 22.7 %all_to_all.5 = bf16[32,2,3600]{2,1,0:T(2,128)(2,1)S(1)} all-to-all(bf16[32,2,3600]{2,1,0:T(2,128)(2,1)S(1)} %reshape.36), channel_id=1, replica_groups=mesh['z'=8,'core'=2,'x'=4,'y'=8] {'x','y'}, dimensions={0} | all-to-all | bytes 921600 | tf_op jit(solution)/shard_map/all_to_all | solution.py:299
  63.0 0.4 reduce_sum.25
  63.4 4.3 %collective-permute-start.5 = (bf16[16,16,3600]{2,1,0:T(8,128)(2,1)S(1)}, bf16[16,16,3600]{2,1,0:T(8,128)(2,1)}, u32[]{:S(2)}, u32[]{:S(2)}) collective-permute-start(bf16[16,16,3600]{2,1,0:T(8,128)(2,1)S(1)} %bitcast.13), channel_id=1, source_target_pairs={{0,8},{32,56},{1,9},{33,57},{2,10},{34,58},{3,11},{35,59},{4,12},{... | collective-permute-start | bytes 5529608 | tf_op jit(solution)/shard_map/ppermute | solution.py:303
  67.7 4.4 %all-gather.4.cloned.1.call-done.panel_ref = bf16[1024,3600]{1,0:T(8,128)(2,1)} async-done(((bf16[64,3600]{1,0:T(8,128)(2,1)}), bf16[1024,3600]{1,0:T(8,128)(2,1)}) %all-gather.4.cloned.1.call-update) | async-done | bytes 7372816 | tf_op jit(solution)/shard_map/all_gather | solution.py:211
  72.0 5.3 %own_scores.1.own_best_ref = f32[1,256]{1,0:T(1,128)S(1)} custom-call(bf16[256,3600]{1,0:T(8,128)(2,1)S(1)} %get-tuple-element.23.points_ref, bf16[1024,3600]{1,0:T(8,128)(2,1)} %all-gather.4.cloned.1.call-done.panel_ref), custom_call_target="tpu_custom_call" | custom-call | flops 1887436800 | bytes 7372800 | tf_op jit(solution)/shard_map/own_scores/pallas_call | solution.py:306
  77.3 19.4 %all-gather.1.totals_ref = bf16[16,2,3600]{2,1,0:T(2,128)(2,1)S(1)} all-gather(bf16[1,2,3600]{2,1,0:T(2,128)(2,1)S(1)} %bitcast.15), channel_id=2, replica_groups=mesh['z'=8,'core'=2,'x'=4,'y'=8] {'z','core'}, dimensions={0}, use_global_device_ids=true | all-gather | bytes 244800 | tf_op jit(solution)/shard_map/all_gather | solution.py:325
  96.8 3.8 %other_scores.1 = f32[1,256]{1,0:T(1,128)S(1)} custom-call(bf16[256,3600]{1,0:T(8,128)(2,1)} %bitcast.8.points_ref, bf16[1024,3600]{1,0:T(8,128)(2,1)S(1)} %copy-done), custom_call_target="tpu_custom_call" | custom-call | flops 1887436800 | bytes 7372800 | tf_op jit(solution)/shard_map/other_scores/pallas_call | solution.py:335
  100.6 3.5 %collective-permute-start.6 = (f32[1,256]{1,0:T(1,128)S(1)}, f32[1,256]{1,0:T(1,128)S(1)}, u32[]{:S(2)}, u32[]{:S(2)}) collective-permute-start(f32[1,256]{1,0:T(1,128)S(1)} %other_scores.1), channel_id=1, source_target_pairs={{0,8},{32,56},{1,9},{33,57},{2,10},{34,58},{3,11},{35,59},{4,12},{... | collective-permute-start | bytes 3080 | tf_op jit(solution)/shard_map/ppermute | solution.py:348
  104.1 0.8 finish_patterns.1
  104.9 1.2 %collective-permute-done.6.returned_ref = f32[1,256]{1,0:T(1,128)S(1)} collective-permute-done((f32[1,256]{1,0:T(1,128)S(1)}, f32[1,256]{1,0:T(1,128)S(1)}, u32[]{:S(2)}, u32[]{:S(2)}) %collective-permute-start.6) | collective-permute-done | bytes 1056 | tf_op jit(solution)/shard_map/ppermute | solution.py:348
  106.1 0.7 finish_scores.1
  (24 shorter events, 0.7 us)
Async XLA Ops:
  7.2 64.9 %all-gather.4.cloned.1.call-start = ((), (), s32[]{:S(2)}) async-start(), calls=%async_computation.1 | async-start | bytes 8077312 | tf_op jit(solution)/shard_map/all_gather | solution.py:211
  10.3 13.2 %copy-start.1 = (s32[16,16]{1,0:T(8,128)S(1)}, s32[16,16]{1,0:T(8,128)}, u32[]{:S(2)}) copy-start(s32[16,16]{1,0:T(8,128)} %param.10) | copy-start | bytes 3076
  10.3 13.3 %copy-start.2 = (s32[16,16]{1,0:T(8,128)S(1)}, s32[16,16]{1,0:T(8,128)}, u32[]{:S(2)}) copy-start(s32[16,16]{1,0:T(8,128)} %param.9) | copy-start | bytes 3076
  10.3 13.5 %copy-start.3 = (s32[128]{0:T(128)S(1)}, s32[128]{0:T(128)}, u32[]{:S(2)}) copy-start(s32[128]{0:T(128)} %param.11) | copy-start | bytes 1540
  13.4 11.6 %collective-permute-start = (bf16[16,3600]{1,0:T(8,128)(2,1)S(1)}, bf16[16,3600]{1,0:T(8,128)(2,1)S(1)}, u32[]{:S(2)}, u32[]{:S(2)}) collective-permute-start(bf16[16,3600]{1,0:T(8,128)(2,1)S(1)} %get-tuple-element.18), channel_id=1, source_target_pairs={{0,32},{32,64},{64,96},{96,128},{128,160},{160,192},{192,224},{224... | collective-permute-start | bytes 345608 | tf_op jit(solution)/shard_map/ppermute | solution.py:242
  18.8 6.2 %collective-permute-start.1 = (bf16[16,3600]{1,0:T(8,128)(2,1)S(1)}, bf16[16,3600]{1,0:T(8,128)(2,1)S(1)}, u32[]{:S(2)}, u32[]{:S(2)}) collective-permute-start(bf16[16,3600]{1,0:T(8,128)(2,1)S(1)} %get-tuple-element.19), channel_id=1, source_target_pairs={{32,0},{64,32},{96,64},{128,96},{160,128},{192,160},{224,192},{256... | collective-permute-start | bytes 345608 | tf_op jit(solution)/shard_map/ppermute | solution.py:243
  25.1 8.0 %collective-permute-start.2 = (bf16[18,3600]{1,0:T(8,128)(2,1)S(1)}, bf16[18,3600]{1,0:T(8,128)(2,1)S(1)}, u32[]{:S(2)}, u32[]{:S(2)}) collective-permute-start(bf16[18,3600]{1,0:T(8,128)(2,1)S(1)} %pad_maximum_fusion), channel_id=1, source_target_pairs={{0,1},{1,2},{2,3},{3,4},{4,5},{5,6},{6,7},{7,8},{8,9},{9,10},{10,1... | collective-permute-start | bytes 388808 | tf_op jit(solution)/shard_map/ppermute | solution.py:251
  28.4 6.9 %collective-permute-start.3 = (bf16[18,3600]{1,0:T(8,128)(2,1)S(1)}, bf16[18,3600]{1,0:T(8,128)(2,1)S(1)}, u32[]{:S(2)}, u32[]{:S(2)}) collective-permute-start(bf16[18,3600]{1,0:T(8,128)(2,1)S(1)} %pad_maximum_fusion.1), channel_id=1, source_target_pairs={{1,0},{2,1},{3,2},{4,3},{5,4},{6,5},{7,6},{8,7},{9,8},{10,9},{11,1... | collective-permute-start | bytes 388808 | tf_op jit(solution)/shard_map/ppermute | solution.py:252
  36.3 3.7 %collective-permute-start.4 = (bf16[64,3600]{1,0:T(8,128)(2,1)S(1)}, bf16[64,3600]{1,0:T(8,128)(2,1)S(1)}, u32[]{:S(2)}, u32[]{:S(2)}) collective-permute-start(bf16[64,3600]{1,0:T(8,128)(2,1)S(1)} %get-tuple-element.22), channel_id=1, source_target_pairs={{0,32},{32,0},{1,33},{33,1},{2,34},{34,2},{3,35},{35,3},{4,36},{36... | collective-permute-start | bytes 1382408 | tf_op jit(solution)/shard_map/ppermute | solution.py:297
  63.4 33.4 %collective-permute-start.5 = (bf16[16,16,3600]{2,1,0:T(8,128)(2,1)S(1)}, bf16[16,16,3600]{2,1,0:T(8,128)(2,1)}, u32[]{:S(2)}, u32[]{:S(2)}) collective-permute-start(bf16[16,16,3600]{2,1,0:T(8,128)(2,1)S(1)} %bitcast.13), channel_id=1, source_target_pairs={{0,8},{32,56},{1,9},{33,57},{2,10},{34,58},{3,11},{35,59},{4,12},{... | collective-permute-start | bytes 5529608 | tf_op jit(solution)/shard_map/ppermute | solution.py:303
  72.0 24.7 %copy-start = (bf16[1024,3600]{1,0:T(8,128)(2,1)S(1)}, bf16[1024,3600]{1,0:T(8,128)(2,1)}, u32[]{:S(2)}) copy-start(bf16[1024,3600]{1,0:T(8,128)(2,1)} %all-gather.4.cloned.1.call-done.panel_ref) | copy-start | bytes 22118404
  100.6 5.5 %collective-permute-start.6 = (f32[1,256]{1,0:T(1,128)S(1)}, f32[1,256]{1,0:T(1,128)S(1)}, u32[]{:S(2)}, u32[]{:S(2)}) collective-permute-start(f32[1,256]{1,0:T(1,128)S(1)} %other_scores.1), channel_id=1, source_target_pairs={{0,8},{32,56},{1,9},{33,57},{2,10},{34,58},{3,11},{35,59},{4,12},{... | collective-permute-start | bytes 3080 | tf_op jit(solution)/shard_map/ppermute | solution.py:348
Sparse Core Ops, SparseCore 0:
  10.4 61.5 all-gather.3

commit v7 on v5

--- a/solution.py
+++ b/solution.py
@@ -285,11 +285,13 @@
     other = lax.ppermute(indexed.reshape(patterns.shape), EVERY, trade).reshape(points, pixels)
 
     chip_sums = (kept + swapped.astype(f32)).astype(bf16)
-    parts = lax.all_to_all(chip_sums.reshape(lines, -1, pixels), SCAN, 0, 0, tiled=True)
+    chip_sums = chip_sums.reshape(lines, -1, pixels)
+    parts = lax.all_to_all(chip_sums, SCAN, 0, 0, tiled=True)
     group_total = jnp.sum(parts.astype(f32), axis=0).astype(bf16)
 
     block = 512
-    scored, group_total = lax.optimization_barrier((other, group_total))
+    copies = jnp.broadcast_to(group_total, (columns,) + group_total.shape)
+    group_totals = lax.all_to_all(copies, DICT, 0, 0, tiled=True)
     own_best, other_best = pl.pallas_call(
         best_scores,
         grid=(panels.shape[0] // block,),
@@ -302,11 +304,14 @@
         out_specs=(pl.BlockSpec((1, points), lambda i: (0, 0)),) * 2,
         scratch_shapes=[VMEM((2 * points, pixels), bf16), VMEM((2 * points, 128), f32)],
         compiler_params=params(28),
+        cost_estimate=pl.CostEstimate(
+            flops=4 * points * pixels * panels.shape[0],
+            bytes_accessed=2 * pixels * panels.shape[0],
+            transcendentals=0,
+        ),
         name="best_scores",
-    )(indexed, scored, pltpu.with_memory_space_constraint(panels, pltpu.HBM))
+    )(indexed, other, pltpu.with_memory_space_constraint(panels, pltpu.HBM))
     returned = lax.ppermute(other_best, EVERY, trade)
-    other_best, group_total = lax.optimization_barrier((other_best, group_total))
-    group_totals = lax.all_gather(group_total, DICT, axis=0, tiled=False)
     returned, group_totals = lax.optimization_barrier((returned, group_totals))
     return pl.pallas_call(
         finish,

time: 116 us -> 111 us (0.957)
  blocking collectives: 48.6 us -> 26.1 us
  starting transfers between devices: 31.1 us -> 43.2 us
  waiting for transfers between devices: 1.3 us -> 4.45 us
    all_gather x1 -> x0, blocking collectives: 22.6 us -> none  [shards(): group_totals = lax.all_gather(group_total, DICT, axis=0, tiled=False)]
    all_to_all x0 -> x1, starting transfers between devices: none -> 14.4 us  [shards(): group_totals = lax.all_to_all(copies, DICT, 0, 0, tiled=True)]
    ppermute x1, starting transfers between devices: 4.73 us -> 2.36 us  [shards(): returned = lax.ppermute(other_best, EVERY, trade)]
    ppermute x1, waiting for transfers between devices: 0.01 us -> 1.92 us  [shards(): returned = lax.ppermute(other_best, EVERY, trade)]
    all_to_all x0 -> x1, waiting for transfers between devices: none -> 1.24 us  [shards(): group_totals = lax.all_to_all(copies, DICT, 0, 0, tiled=True)]
  transfers between devices with their start and end apart: 8 -> 9, of which waited for: 2 -> 4; matrix products, arithmetic and copies ran while one was open for 1% -> 2% of each run, Pallas kernels for 7% -> 15%
where the time goes in v7:
time: 111 us; the launch traced here: 110 us
  starting transfers between devices  43.2 us (39%)
  blocking collectives  26.1 us (24%)
  Pallas kernels  20.1 us (18%)
  between operations  14.2 us (13%)
  waiting for transfers between devices  4.45 us (4%)
  local copies, waits for them, and re-layouts  1.29 us (1%)
    all_to_all x1, blocking collectives, shards(): parts = lax.all_to_all(chip_sums, SCAN, 0, 0, tiled=True)  26.1 us
    all_to_all x1, starting transfers between devices, shards(): group_totals = lax.all_to_all(copies, DICT, 0, 0, tiled=True)  14.4 us
    ppermute x1, starting transfers between devices, shards(): lax.ppermute(indexed.reshape(patterns.shape), EVERY, trade)  8.15 us
    pallas_call x1, Pallas kernels, shards(): pl.pallas_call(best_scores, grid=(panels.shape[0] // block,), out_shape=(...  7.57 us
    ppermute x1, starting transfers between devices, shards(): low = lax.ppermute(high_edge, DICT, forward)  5.39 us
    ppermute x1, starting transfers between devices, shards(): high = lax.ppermute(low_edge, DICT, backward)  4.69 us
    ppermute x1, starting transfers between devices, shards(): above = lax.ppermute(strip(tile_rows - 1), SCAN, forward)  4 us
    pallas_call x1, Pallas kernels, shards(): pl.pallas_call(inner_rows, out_shape=jax.ShapeDtypeStruct((inner_points,...  3.45 us
  transfers between devices with their start and end apart: 9, of which 4 were waited for; matrix products, arithmetic and copies ran while one was open for 2% of the time, Pallas kernels for 15%

profile of v7, /device:TPU:1, one launch (start us, length us, event | category | flops | bytes accessed | tf_op | source)
XLA Modules:
  0.0 110.2 jit_solution(2913758559179610680)
XLA Ops:
  7.2 3.1 %normalise_templates.1 = bf16[64,3600]{1,0:T(8,128)(2,1)} custom-call(bf16[3600,128]{1,0:T(8,128)(2,1)} %bitcast.13), custom_call_target="tpu_custom_call" | custom-call | tf_op jit(solution)/shard_map/normalise_templates/pallas_call | solution.py:189
  10.3 3.1 %filter_tile.1 = (bf16[16,16,3600]{2,1,0:T(8,128)(2,1)S(1)}, bf16[16,3600]{1,0:T(8,128)(2,1)S(1)}, bf16[16,3600]{1,0:T(8,128)(2,1)S(1)}) custom-call(f32[3600]{0:T(1024)} %background_ref.1, f32[16,16,3600]{2,1,0:T(8,128)} %tile_ref), custom_call_target="tpu_custom_call" | custom-call | tf_op jit(solution)/shard_map/filter_tile/pallas_call | solution.py:202
  13.5 5.4 %collective-permute-start = (bf16[16,3600]{1,0:T(8,128)(2,1)S(1)}, bf16[16,3600]{1,0:T(8,128)(2,1)S(1)}, u32[]{:S(2)}, u32[]{:S(2)}) collective-permute-start(bf16[16,3600]{1,0:T(8,128)(2,1)S(1)} %get-tuple-element.15), channel_id=1, source_target_pairs={{0,32},{32,64},{64,96},{96,128},{128,160},{160,192},{192,224},{224... | collective-permute-start | bytes 345608 | tf_op jit(solution)/shard_map/ppermute | solution.py:229
  18.9 4.7 %collective-permute-start.1 = (bf16[16,3600]{1,0:T(8,128)(2,1)S(1)}, bf16[16,3600]{1,0:T(8,128)(2,1)S(1)}, u32[]{:S(2)}, u32[]{:S(2)}) collective-permute-start(bf16[16,3600]{1,0:T(8,128)(2,1)S(1)} %get-tuple-element.16), channel_id=1, source_target_pairs={{32,0},{64,32},{96,64},{128,96},{160,128},{192,160},{224,192},{256... | collective-permute-start | bytes 345608 | tf_op jit(solution)/shard_map/ppermute | solution.py:230
  23.8 0.2 select_reduce_fusion
  24.0 1.0 collective-permute-done.1.high_ref
  25.1 1.3 %collective-permute-start.3 = (bf16[18,3600]{1,0:T(8,128)(2,1)S(1)}, bf16[18,3600]{1,0:T(8,128)(2,1)S(1)}, u32[]{:S(2)}, u32[]{:S(2)}) collective-permute-start(bf16[18,3600]{1,0:T(8,128)(2,1)S(1)} %pad_maximum_fusion.1), channel_id=1, source_target_pairs={{1,0},{2,1},{3,2},{4,3},{5,4},{6,5},{7,6},{8,7},{9,8},{10,9},{11,1... | collective-permute-start | bytes 388808 | tf_op jit(solution)/shard_map/ppermute | solution.py:239
  26.4 4.0 %collective-permute-start.2 = (bf16[18,3600]{1,0:T(8,128)(2,1)S(1)}, bf16[18,3600]{1,0:T(8,128)(2,1)S(1)}, u32[]{:S(2)}, u32[]{:S(2)}) collective-permute-start(bf16[18,3600]{1,0:T(8,128)(2,1)S(1)} %pad_maximum_fusion), channel_id=1, source_target_pairs={{0,1},{1,2},{2,3},{3,4},{4,5},{5,6},{6,7},{7,8},{8,9},{9,10},{10,1... | collective-permute-start | bytes 388808 | tf_op jit(solution)/shard_map/ppermute | solution.py:238
  30.5 3.5 %inner_rows.1.inner_ref = bf16[224,3600]{1,0:T(8,128)(2,1)S(1)} custom-call(bf16[16,16,3600]{2,1,0:T(8,128)(2,1)S(1)} %get-tuple-element.14.tile_ref, bf16[16,3600]{1,0:T(8,128)(2,1)S(1)} %collective-permute-done.low_ref, bf16[16,3600]{1,0:T(8,128)(2,1)S(1)} %collective-permute-done.1.high_ref), custom_call_target="tpu_custom_call" | custom-call | flops 9676800 | bytes 12902400 | tf_op jit(solution)/shard_map/inner_rows/pallas_call | solution.py:248
  33.9 0.3 collective-permute-done.2.above_ref
  34.2 2.1 %outer_rows.1 = (bf16[256,3600]{1,0:T(8,128)(2,1)}, f32[64,3600]{1,0:T(8,128)S(1)}, bf16[64,3600]{1,0:T(8,128)(2,1)S(1)}) custom-call(s32[1,256]{1,0:T(1,128)S(1)} %broadcast_select_fusion.point_row_ref, bf16[16,3600]{1,0:T(8,128)(2,1)S(1)} %get-tuple-element.27.first_ref, bf16[16,3600]{1,0:T(8,128)(2,1)S(1)} %get-tuple-element.26.second_ref, ...), custom_call_target="tpu_custom_call" | custom-call | tf_op jit(solution)/shard_map/outer_rows/pallas_call | solution.py:261
  36.3 2.8 %collective-permute-start.6 = (bf16[64,3600]{1,0:T(8,128)(2,1)S(1)}, bf16[64,3600]{1,0:T(8,128)(2,1)S(1)}, u32[]{:S(2)}, u32[]{:S(2)}) collective-permute-start(bf16[64,3600]{1,0:T(8,128)(2,1)S(1)} %get-tuple-element.21), channel_id=1, source_target_pairs={{0,32},{32,0},{1,33},{33,1},{2,34},{34,2},{3,35},{35,3},{4,36},{36... | collective-permute-start | bytes 1382408 | tf_op jit(solution)/shard_map/ppermute | solution.py:284
  39.2 8.1 %collective-permute-start.4 = (bf16[16,16,3600]{2,1,0:T(8,128)(2,1)}, bf16[16,16,3600]{2,1,0:T(8,128)(2,1)S(1)}, u32[]{:S(2)}, u32[]{:S(2)}) collective-permute-start(bf16[16,16,3600]{2,1,0:T(8,128)(2,1)} %bitcast.6), channel_id=1, source_target_pairs={{0,8},{32,56},{1,9},{33,57},{2,10},{34,58},{3,11},{35,59},{4,12},{... | collective-permute-start | bytes 5529608 | tf_op jit(solution)/shard_map/ppermute | solution.py:285
  47.3 0.1 add_convert_fusion
  47.4 0.2 reshape.38
  47.6 26.1 %all_to_all.10 = bf16[32,2,3600]{2,1,0:T(2,128)(2,1)S(1)} all-to-all(bf16[32,2,3600]{2,1,0:T(2,128)(2,1)S(1)} %reshape.38), channel_id=1, replica_groups=mesh['z'=8,'core'=2,'x'=4,'y'=8] {'x','y'}, dimensions={0} | all-to-all | bytes 921600 | tf_op jit(solution)/shard_map/all_to_all | solution.py:289
  73.8 0.4 reduce_sum.25
  74.2 0.8 broadcast_in_dim.24
  75.0 14.4 %all-to-all-start.1 = ((bf16[16,2,3600]{2,1,0:T(2,128)(2,1)}), bf16[16,2,3600]{2,1,0:T(2,128)(2,1)S(1)}, u32[]{:S(2)}, u32[]{:S(2)}) async-start(bf16[16,2,3600]{2,1,0:T(2,128)(2,1)} %broadcast_in_dim.24), calls=%async_computation.1 | async-start | bytes 475136 | tf_op jit(solution)/shard_map/all_to_all | solution.py:294
  89.4 7.6 %best_scores.1 = (f32[1,256]{1,0:T(1,128)S(1)}, f32[1,256]{1,0:T(1,128)S(1)}) custom-call(bf16[256,3600]{1,0:T(8,128)(2,1)} %get-tuple-element.17.own_ref, bf16[256,3600]{1,0:T(8,128)(2,1)S(1)} %bitcast.12, bf16[1024,3600]{1,0:T(8,128)(2,1)} %all-gather.2.cloned.1.call-done.panel_ref), custom_call_target="tpu_custom_call" | custom-call | flops 3774873600 | bytes 7372800 | tf_op jit(solution)/shard_map/best_scores/pallas_call | solution.py:295
  97.0 2.4 %collective-permute-start.5 = (f32[1,256]{1,0:T(1,128)S(1)}, f32[1,256]{1,0:T(1,128)S(1)}, u32[]{:S(2)}, u32[]{:S(2)}) collective-permute-start(f32[1,256]{1,0:T(1,128)S(1)} %get-tuple-element.19), channel_id=1, source_target_pairs={{0,8},{32,56},{1,9},{33,57},{2,10},{34,58},{3,11},{35,59},{4,12},{... | collective-permute-start | bytes 3080 | tf_op jit(solution)/shard_map/ppermute | solution.py:314
  99.4 1.2 %all-to-all-done.1.totals_ref = bf16[16,2,3600]{2,1,0:T(2,128)(2,1)S(1)} async-done(((bf16[16,2,3600]{2,1,0:T(2,128)(2,1)}), bf16[16,2,3600]{2,1,0:T(2,128)(2,1)S(1)}, u32[]{:S(2)}, u32[]{:S(2)}) %all-to-all-start.1) | async-done | bytes 230432 | tf_op jit(solution)/shard_map/all_to_all | solution.py:294
  100.6 1.9 %collective-permute-done.5.returned_ref = f32[1,256]{1,0:T(1,128)S(1)} collective-permute-done((f32[1,256]{1,0:T(1,128)S(1)}, f32[1,256]{1,0:T(1,128)S(1)}, u32[]{:S(2)}, u32[]{:S(2)}) %collective-permute-start.5) | collective-permute-done | bytes 1056 | tf_op jit(solution)/shard_map/ppermute | solution.py:314
  102.5 0.8 finish.1
  (22 shorter events, 0.5 us)
Async XLA Ops:
  7.2 82.3 %all-gather.2.cloned.1.call-start = ((), (), s32[]{:S(2)}) async-start(), calls=%async_computation.2 | async-start | bytes 8077312 | tf_op jit(solution)/shard_map/all_gather | solution.py:198
  10.3 13.2 %copy-start = (s32[16,16]{1,0:T(8,128)S(1)}, s32[16,16]{1,0:T(8,128)}, u32[]{:S(2)}) copy-start(s32[16,16]{1,0:T(8,128)} %param.10) | copy-start | bytes 3076
  10.3 13.3 %copy-start.1 = (s32[16,16]{1,0:T(8,128)S(1)}, s32[16,16]{1,0:T(8,128)}, u32[]{:S(2)}) copy-start(s32[16,16]{1,0:T(8,128)} %param.9) | copy-start | bytes 3076
  10.3 13.5 %copy-start.2 = (s32[128]{0:T(128)S(1)}, s32[128]{0:T(128)}, u32[]{:S(2)}) copy-start(s32[128]{0:T(128)} %param.11) | copy-start | bytes 1540
  13.5 10.5 %collective-permute-start = (bf16[16,3600]{1,0:T(8,128)(2,1)S(1)}, bf16[16,3600]{1,0:T(8,128)(2,1)S(1)}, u32[]{:S(2)}, u32[]{:S(2)}) collective-permute-start(bf16[16,3600]{1,0:T(8,128)(2,1)S(1)} %get-tuple-element.15), channel_id=1, source_target_pairs={{0,32},{32,64},{64,96},{96,128},{128,160},{160,192},{192,224},{224... | collective-permute-start | bytes 345608 | tf_op jit(solution)/shard_map/ppermute | solution.py:229
  18.9 6.2 %collective-permute-start.1 = (bf16[16,3600]{1,0:T(8,128)(2,1)S(1)}, bf16[16,3600]{1,0:T(8,128)(2,1)S(1)}, u32[]{:S(2)}, u32[]{:S(2)}) collective-permute-start(bf16[16,3600]{1,0:T(8,128)(2,1)S(1)} %get-tuple-element.16), channel_id=1, source_target_pairs={{32,0},{64,32},{96,64},{128,96},{160,128},{192,160},{224,192},{256... | collective-permute-start | bytes 345608 | tf_op jit(solution)/shard_map/ppermute | solution.py:230
  25.1 8.8 %collective-permute-start.3 = (bf16[18,3600]{1,0:T(8,128)(2,1)S(1)}, bf16[18,3600]{1,0:T(8,128)(2,1)S(1)}, u32[]{:S(2)}, u32[]{:S(2)}) collective-permute-start(bf16[18,3600]{1,0:T(8,128)(2,1)S(1)} %pad_maximum_fusion.1), channel_id=1, source_target_pairs={{1,0},{2,1},{3,2},{4,3},{5,4},{6,5},{7,6},{8,7},{9,8},{10,9},{11,1... | collective-permute-start | bytes 388808 | tf_op jit(solution)/shard_map/ppermute | solution.py:239
  26.4 7.7 %collective-permute-start.2 = (bf16[18,3600]{1,0:T(8,128)(2,1)S(1)}, bf16[18,3600]{1,0:T(8,128)(2,1)S(1)}, u32[]{:S(2)}, u32[]{:S(2)}) collective-permute-start(bf16[18,3600]{1,0:T(8,128)(2,1)S(1)} %pad_maximum_fusion), channel_id=1, source_target_pairs={{0,1},{1,2},{2,3},{3,4},{4,5},{5,6},{6,7},{7,8},{8,9},{9,10},{10,1... | collective-permute-start | bytes 388808 | tf_op jit(solution)/shard_map/ppermute | solution.py:238
  36.3 11.0 %collective-permute-start.6 = (bf16[64,3600]{1,0:T(8,128)(2,1)S(1)}, bf16[64,3600]{1,0:T(8,128)(2,1)S(1)}, u32[]{:S(2)}, u32[]{:S(2)}) collective-permute-start(bf16[64,3600]{1,0:T(8,128)(2,1)S(1)} %get-tuple-element.21), channel_id=1, source_target_pairs={{0,32},{32,0},{1,33},{33,1},{2,34},{34,2},{3,35},{35,3},{4,36},{36... | collective-permute-start | bytes 1382408 | tf_op jit(solution)/shard_map/ppermute | solution.py:284
  39.2 50.3 %collective-permute-start.4 = (bf16[16,16,3600]{2,1,0:T(8,128)(2,1)}, bf16[16,16,3600]{2,1,0:T(8,128)(2,1)S(1)}, u32[]{:S(2)}, u32[]{:S(2)}) collective-permute-start(bf16[16,16,3600]{2,1,0:T(8,128)(2,1)} %bitcast.6), channel_id=1, source_target_pairs={{0,8},{32,56},{1,9},{33,57},{2,10},{34,58},{3,11},{35,59},{4,12},{... | collective-permute-start | bytes 5529608 | tf_op jit(solution)/shard_map/ppermute | solution.py:285
  75.0 25.6 %all-to-all-start.1 = ((bf16[16,2,3600]{2,1,0:T(2,128)(2,1)}), bf16[16,2,3600]{2,1,0:T(2,128)(2,1)S(1)}, u32[]{:S(2)}, u32[]{:S(2)}) async-start(bf16[16,2,3600]{2,1,0:T(2,128)(2,1)} %broadcast_in_dim.24), calls=%async_computation.1 | async-start | bytes 475136 | tf_op jit(solution)/shard_map/all_to_all | solution.py:294
  97.0 5.5 %collective-permute-start.5 = (f32[1,256]{1,0:T(1,128)S(1)}, f32[1,256]{1,0:T(1,128)S(1)}, u32[]{:S(2)}, u32[]{:S(2)}) collective-permute-start(f32[1,256]{1,0:T(1,128)S(1)} %get-tuple-element.19), channel_id=1, source_target_pairs={{0,8},{32,56},{1,9},{33,57},{2,10},{34,58},{3,11},{35,59},{4,12},{... | collective-permute-start | bytes 3080 | tf_op jit(solution)/shard_map/ppermute | solution.py:314
Sparse Core Ops, SparseCore 0:
  10.4 61.5 all-gather.1

commit v8 on v7

--- a/solution.py
+++ b/solution.py
@@ -1,3 +1,4 @@
+import functools
 import math
 
 import jax
@@ -135,30 +136,30 @@
         sent_ref[:, start:stop] = sums[half:].astype(jnp.bfloat16)
 
 
-def best_scores(own_ref, other_ref, panel_ref, own_best_ref, other_best_ref, points_ref, best_ref):
-    points = own_ref.shape[0]
+def lane_best(best, scores):
+    lanes = best.shape[1]
+    for start in range(0, scores.shape[1], lanes):
+        best = jnp.maximum(best, scores[:, start : start + lanes])
+    return best
+
+
+def products(points, panel):
+    return lax.dot_general(points, panel, (((1,), (1,)), ((), ())), preferred_element_type=jnp.float32)
+
+
+def best_scores(panel_ref, points_ref, out_ref, best_ref):
     step = pl.program_id(0)
 
     @pl.when(step == 0)
     def _():
-        points_ref[:points, :] = own_ref[...]
-        points_ref[points:, :] = other_ref[...]
         best_ref[...] = jnp.full(best_ref.shape, -jnp.inf, jnp.float32)
 
-    scores = lax.dot_general(
-        points_ref[...], panel_ref[...], (((1,), (1,)), ((), ())), preferred_element_type=jnp.float32
-    )
-    lanes = best_ref.shape[1]
-    best = best_ref[...]
-    for start in range(0, scores.shape[1], lanes):
-        best = jnp.maximum(best, scores[:, start : start + lanes])
+    best = lane_best(best_ref[...], products(points_ref[...], panel_ref[...]))
     best_ref[...] = best
 
     @pl.when(step == pl.num_programs(0) - 1)
     def _():
-        best = jnp.max(best_ref[...].T, axis=0, keepdims=True)
-        own_best_ref[...] = best[:, :points]
-        other_best_ref[...] = best[:, points:]
+        out_ref[...] = jnp.max(best.T, axis=0, keepdims=True)
 
 
 def finish(own_best_ref, returned_ref, totals_ref, max_score_ref, patterns_ref):
@@ -287,30 +288,35 @@
     chip_sums = (kept + swapped.astype(f32)).astype(bf16)
     chip_sums = chip_sums.reshape(lines, -1, pixels)
     parts = lax.all_to_all(chip_sums, SCAN, 0, 0, tiled=True)
+    block = 512
+    scored = functools.partial(
+        pl.pallas_call(
+            best_scores,
+            grid=(panels.shape[0] // block,),
+            out_shape=jax.ShapeDtypeStruct((1, points), f32),
+            in_specs=[
+                pl.BlockSpec((block, pixels), lambda i: (i, 0)),
+                pl.BlockSpec((points, pixels), lambda i: (0, 0)),
+            ],
+            out_specs=pl.BlockSpec((1, points), lambda i: (0, 0)),
+            scratch_shapes=[VMEM((points, 128), f32)],
+            compiler_params=params(20),
+            cost_estimate=pl.CostEstimate(
+                flops=2 * points * pixels * panels.shape[0],
+                bytes_accessed=2 * pixels * panels.shape[0],
+                transcendentals=0,
+            ),
+            name="best_scores",
+        ),
+        pltpu.with_memory_space_constraint(panels, pltpu.HBM),
+    )
+    own_best = scored(indexed)
+    own_best, parts = lax.optimization_barrier((own_best, parts))
     group_total = jnp.sum(parts.astype(f32), axis=0).astype(bf16)
 
-    block = 512
     copies = jnp.broadcast_to(group_total, (columns,) + group_total.shape)
     group_totals = lax.all_to_all(copies, DICT, 0, 0, tiled=True)
-    own_best, other_best = pl.pallas_call(
-        best_scores,
-        grid=(panels.shape[0] // block,),
-        out_shape=(jax.ShapeDtypeStruct((1, points), f32),) * 2,
-        in_specs=[
-            pl.BlockSpec((points, pixels), lambda i: (0, 0)),
-            pl.BlockSpec((points, pixels), lambda i: (0, 0)),
-            pl.BlockSpec((block, pixels), lambda i: (i, 0)),
-        ],
-        out_specs=(pl.BlockSpec((1, points), lambda i: (0, 0)),) * 2,
-        scratch_shapes=[VMEM((2 * points, pixels), bf16), VMEM((2 * points, 128), f32)],
-        compiler_params=params(28),
-        cost_estimate=pl.CostEstimate(
-            flops=4 * points * pixels * panels.shape[0],
-            bytes_accessed=2 * pixels * panels.shape[0],
-            transcendentals=0,
-        ),
-        name="best_scores",
-    )(indexed, other, pltpu.with_memory_space_constraint(panels, pltpu.HBM))
+    other_best = scored(other)
     returned = lax.ppermute(other_best, EVERY, trade)
     returned, group_totals = lax.optimization_barrier((returned, group_totals))
     return pl.pallas_call(

time: 111 us -> 107 us (0.964)
  blocking collectives: 26.1 us -> 0 us
  waiting for transfers between devices: 4.45 us -> 25.7 us
    all_to_all x1 -> x0, blocking collectives: 26.1 us -> none  [shards(): parts = lax.all_to_all(chip_sums, SCAN, 0, 0, tiled=True)]
    all_gather x1, waiting for transfers between devices: 0.02 us -> 20.9 us  [shards(): panels = lax.all_gather(panel, DICT, axis=0, tiled=True)]
    all_to_all x1, starting transfers between devices: 14.4 us -> 10.2 us  [shards(): group_totals = lax.all_to_all(copies, DICT, 0, 0, tiled=True)]
    all_to_all x0 -> x1, starting transfers between devices: none -> 3.89 us  [shards(): parts = lax.all_to_all(chip_sums, SCAN, 0, 0, tiled=True)]
    pallas_call x1 -> x2, Pallas kernels: 7.57 us -> 9.84 us  [the longest x1 5.23 us: shards(): other_best = scored(other)]
    ppermute x1, waiting for transfers between devices: 1.92 us -> 3.16 us  [shards(): returned = lax.ppermute(other_best, EVERY, trade)]
    pallas_call x1, Pallas kernels: 2.11 us -> 0.99 us  [shards(): pl.pallas_call(outer_rows, out_shape=(jax.ShapeDtypeStruct((points, pixel...]
  transfers between devices with their start and end apart: 9 -> 10, of which waited for: 4 -> 5; matrix products, arithmetic and copies ran while one was open for 2% -> 3% of each run, Pallas kernels for 15% -> 16%
where the time goes in v8:
time: 107 us
  starting transfers between devices  42.9 us (40%)
  waiting for transfers between devices  25.7 us (24%)
  Pallas kernels  21.2 us (20%)
  between operations  14.3 us (13%)
  local copies, waits for them, and re-layouts  2.06 us (2%)
    all_gather x1, waiting for transfers between devices, shards(): panels = lax.all_gather(panel, DICT, axis=0, tiled=True)  20.9 us
    all_to_all x1, starting transfers between devices, shards(): group_totals = lax.all_to_all(copies, DICT, 0, 0, tiled=True)  10.2 us
    ppermute x1, starting transfers between devices, shards(): lax.ppermute(indexed.reshape(patterns.shape), EVERY, trade)  8.15 us
    ppermute x1, starting transfers between devices, shards(): low = lax.ppermute(high_edge, DICT, forward)  5.39 us
    pallas_call x1, Pallas kernels, shards(): other_best = scored(other)  5.23 us
    ppermute x1, starting transfers between devices, shards(): high = lax.ppermute(low_edge, DICT, backward)  4.69 us
    pallas_call x1, Pallas kernels, shards(): own_best = scored(indexed)  4.61 us
    ppermute x1, starting transfers between devices, shards(): above = lax.ppermute(strip(tile_rows - 1), SCAN, forward)  4 us
  transfers between devices with their start and end apart: 10, of which 5 were waited for; matrix products, arithmetic and copies ran while one was open for 3% of the time, Pallas kernels for 16%

profile of v8, /device:TPU:1, one launch (start us, length us, event | category | flops | bytes accessed | tf_op | source)
XLA Modules:
  0.0 106.9 jit_solution(6342136507754677622)
XLA Ops:
  7.2 3.1 %normalise_templates.1 = bf16[64,3600]{1,0:T(8,128)(2,1)} custom-call(bf16[3600,128]{1,0:T(8,128)(2,1)} %bitcast.13), custom_call_target="tpu_custom_call" | custom-call | tf_op jit(solution)/shard_map/normalise_templates/pallas_call | solution.py:190
  10.3 3.1 %filter_tile.1 = (bf16[16,16,3600]{2,1,0:T(8,128)(2,1)S(1)}, bf16[16,3600]{1,0:T(8,128)(2,1)S(1)}, bf16[16,3600]{1,0:T(8,128)(2,1)S(1)}) custom-call(f32[3600]{0:T(1024)} %background_ref.1, f32[16,16,3600]{2,1,0:T(8,128)} %tile_ref), custom_call_target="tpu_custom_call" | custom-call | tf_op jit(solution)/shard_map/filter_tile/pallas_call | solution.py:203
  13.5 5.4 %collective-permute-start = (bf16[16,3600]{1,0:T(8,128)(2,1)S(1)}, bf16[16,3600]{1,0:T(8,128)(2,1)S(1)}, u32[]{:S(2)}, u32[]{:S(2)}) collective-permute-start(bf16[16,3600]{1,0:T(8,128)(2,1)S(1)} %get-tuple-element.15), channel_id=1, source_target_pairs={{0,32},{32,64},{64,96},{96,128},{128,160},{160,192},{192,224},{224... | collective-permute-start | bytes 345608 | tf_op jit(solution)/shard_map/ppermute | solution.py:230
  18.9 4.7 %collective-permute-start.1 = (bf16[16,3600]{1,0:T(8,128)(2,1)S(1)}, bf16[16,3600]{1,0:T(8,128)(2,1)S(1)}, u32[]{:S(2)}, u32[]{:S(2)}) collective-permute-start(bf16[16,3600]{1,0:T(8,128)(2,1)S(1)} %get-tuple-element.16), channel_id=1, source_target_pairs={{32,0},{64,32},{96,64},{128,96},{160,128},{192,160},{224,192},{256... | collective-permute-start | bytes 345608 | tf_op jit(solution)/shard_map/ppermute | solution.py:231
  24.0 1.0 collective-permute-done.1.high_ref
  25.1 1.3 %collective-permute-start.3 = (bf16[18,3600]{1,0:T(8,128)(2,1)S(1)}, bf16[18,3600]{1,0:T(8,128)(2,1)S(1)}, u32[]{:S(2)}, u32[]{:S(2)}) collective-permute-start(bf16[18,3600]{1,0:T(8,128)(2,1)S(1)} %pad_maximum_fusion.1), channel_id=1, source_target_pairs={{1,0},{2,1},{3,2},{4,3},{5,4},{6,5},{7,6},{8,7},{9,8},{10,9},{11,1... | collective-permute-start | bytes 388808 | tf_op jit(solution)/shard_map/ppermute | solution.py:240
  26.4 4.0 %collective-permute-start.2 = (bf16[18,3600]{1,0:T(8,128)(2,1)S(1)}, bf16[18,3600]{1,0:T(8,128)(2,1)S(1)}, u32[]{:S(2)}, u32[]{:S(2)}) collective-permute-start(bf16[18,3600]{1,0:T(8,128)(2,1)S(1)} %pad_maximum_fusion), channel_id=1, source_target_pairs={{0,1},{1,2},{2,3},{3,4},{4,5},{5,6},{6,7},{7,8},{8,9},{9,10},{10,1... | collective-permute-start | bytes 388808 | tf_op jit(solution)/shard_map/ppermute | solution.py:239
  30.5 3.5 %inner_rows.1.inner_ref = bf16[224,3600]{1,0:T(8,128)(2,1)S(1)} custom-call(bf16[16,16,3600]{2,1,0:T(8,128)(2,1)S(1)} %get-tuple-element.14.tile_ref, bf16[16,3600]{1,0:T(8,128)(2,1)S(1)} %collective-permute-done.low_ref, bf16[16,3600]{1,0:T(8,128)(2,1)S(1)} %collective-permute-done.1.high_ref), custom_call_target="tpu_custom_call" | custom-call | flops 9676800 | bytes 12902400 | tf_op jit(solution)/shard_map/inner_rows/pallas_call | solution.py:249
  33.9 0.3 collective-permute-done.2.above_ref
  34.2 1.0 outer_rows.1
  35.2 2.9 %collective-permute-start.4 = (bf16[64,3600]{1,0:T(8,128)(2,1)S(1)}, bf16[64,3600]{1,0:T(8,128)(2,1)S(1)}, u32[]{:S(2)}, u32[]{:S(2)}) collective-permute-start(bf16[64,3600]{1,0:T(8,128)(2,1)S(1)} %get-tuple-element.19), channel_id=1, source_target_pairs={{0,32},{32,0},{1,33},{33,1},{2,34},{34,2},{3,35},{35,3},{4,36},{36... | collective-permute-start | bytes 1382408 | tf_op jit(solution)/shard_map/ppermute | solution.py:285
  38.0 8.1 %collective-permute-start.5 = (bf16[16,16,3600]{2,1,0:T(8,128)(2,1)S(1)}, bf16[16,16,3600]{2,1,0:T(8,128)(2,1)}, u32[]{:S(2)}, u32[]{:S(2)}) collective-permute-start(bf16[16,16,3600]{2,1,0:T(8,128)(2,1)S(1)} %bitcast.12), channel_id=1, source_target_pairs={{0,8},{32,56},{1,9},{33,57},{2,10},{34,58},{3,11},{35,59},{4,12},{... | collective-permute-start | bytes 5529608 | tf_op jit(solution)/shard_map/ppermute | solution.py:286
  46.3 1.0 reshape.36
  47.3 3.9 %all-to-all-start = ((bf16[32,2,3600]{2,1,0:T(2,128)(2,1)}), bf16[32,2,3600]{2,1,0:T(2,128)(2,1)S(1)}, u32[]{:S(2)}, u32[]{:S(2)}) async-start(bf16[32,2,3600]{2,1,0:T(2,128)(2,1)} %reshape.36), calls=%async_computation | async-start | bytes 950272 | tf_op jit(solution)/shard_map/all_to_all | solution.py:290
  51.2 20.9 %all-gather.2.cloned.1.call-done.panel_ref = bf16[1024,3600]{1,0:T(8,128)(2,1)} async-done(((bf16[64,3600]{1,0:T(8,128)(2,1)}), bf16[1024,3600]{1,0:T(8,128)(2,1)}) %all-gather.2.cloned.1.call-update) | async-done | bytes 7372816 | tf_op jit(solution)/shard_map/all_gather | solution.py:199
  72.0 4.6 %best_scores.2.own_best_ref = f32[1,256]{1,0:T(1,128)S(1)} custom-call(bf16[1024,3600]{1,0:T(8,128)(2,1)} %all-gather.2.cloned.1.call-done.panel_ref, bf16[256,3600]{1,0:T(8,128)(2,1)S(1)} %get-tuple-element.17.points_ref), custom_call_target="tpu_custom_call" | custom-call | flops 1887436800 | bytes 7372800 | tf_op jit(solution)/shard_map/best_scores/pallas_call | solution.py:313
  76.6 0.4 reduce_sum.25
  77.0 0.8 broadcast_in_dim.24
  77.9 10.2 %all-to-all-start.1 = ((bf16[16,2,3600]{2,1,0:T(2,128)(2,1)}), bf16[16,2,3600]{2,1,0:T(2,128)(2,1)S(1)}, u32[]{:S(2)}, u32[]{:S(2)}) async-start(bf16[16,2,3600]{2,1,0:T(2,128)(2,1)} %broadcast_in_dim.24), calls=%async_computation.1 | async-start | bytes 475136 | tf_op jit(solution)/shard_map/all_to_all | solution.py:318
  88.1 5.2 %best_scores.3 = f32[1,256]{1,0:T(1,128)S(1)} custom-call(bf16[1024,3600]{1,0:T(8,128)(2,1)} %all-gather.2.cloned.1.call-done.panel_ref, bf16[256,3600]{1,0:T(8,128)(2,1)} %bitcast.7.points_ref), custom_call_target="tpu_custom_call" | custom-call | flops 1887436800 | bytes 7372800 | tf_op jit(solution)/shard_map/best_scores/pallas_call | solution.py:319
  93.3 2.4 %collective-permute-start.6 = (f32[1,256]{1,0:T(1,128)S(1)}, f32[1,256]{1,0:T(1,128)S(1)}, u32[]{:S(2)}, u32[]{:S(2)}) collective-permute-start(f32[1,256]{1,0:T(1,128)S(1)} %best_scores.3), channel_id=1, source_target_pairs={{0,8},{32,56},{1,9},{33,57},{2,10},{34,58},{3,11},{35,59},{4,12},{... | collective-permute-start | bytes 3080 | tf_op jit(solution)/shard_map/ppermute | solution.py:320
  95.7 3.2 %collective-permute-done.6.returned_ref = f32[1,256]{1,0:T(1,128)S(1)} collective-permute-done((f32[1,256]{1,0:T(1,128)S(1)}, f32[1,256]{1,0:T(1,128)S(1)}, u32[]{:S(2)}, u32[]{:S(2)}) %collective-permute-start.6) | collective-permute-done | bytes 1056 | tf_op jit(solution)/shard_map/ppermute | solution.py:320
  98.8 0.4 all-to-all-done.1.totals_ref
  99.3 0.8 finish.1
  (24 shorter events, 0.7 us)
Async XLA Ops:
  7.2 64.9 %all-gather.2.cloned.1.call-start = ((), (), s32[]{:S(2)}) async-start(), calls=%async_computation.2 | async-start | bytes 8077312 | tf_op jit(solution)/shard_map/all_gather | solution.py:199
  10.3 13.2 %copy-start = (s32[16,16]{1,0:T(8,128)S(1)}, s32[16,16]{1,0:T(8,128)}, u32[]{:S(2)}) copy-start(s32[16,16]{1,0:T(8,128)} %param.10) | copy-start | bytes 3076
  10.3 13.3 %copy-start.1 = (s32[16,16]{1,0:T(8,128)S(1)}, s32[16,16]{1,0:T(8,128)}, u32[]{:S(2)}) copy-start(s32[16,16]{1,0:T(8,128)} %param.9) | copy-start | bytes 3076
  10.3 13.5 %copy-start.2 = (s32[128]{0:T(128)S(1)}, s32[128]{0:T(128)}, u32[]{:S(2)}) copy-start(s32[128]{0:T(128)} %param.11) | copy-start | bytes 1540
  13.5 10.5 %collective-permute-start = (bf16[16,3600]{1,0:T(8,128)(2,1)S(1)}, bf16[16,3600]{1,0:T(8,128)(2,1)S(1)}, u32[]{:S(2)}, u32[]{:S(2)}) collective-permute-start(bf16[16,3600]{1,0:T(8,128)(2,1)S(1)} %get-tuple-element.15), channel_id=1, source_target_pairs={{0,32},{32,64},{64,96},{96,128},{128,160},{160,192},{192,224},{224... | collective-permute-start | bytes 345608 | tf_op jit(solution)/shard_map/ppermute | solution.py:230
  18.9 6.2 %collective-permute-start.1 = (bf16[16,3600]{1,0:T(8,128)(2,1)S(1)}, bf16[16,3600]{1,0:T(8,128)(2,1)S(1)}, u32[]{:S(2)}, u32[]{:S(2)}) collective-permute-start(bf16[16,3600]{1,0:T(8,128)(2,1)S(1)} %get-tuple-element.16), channel_id=1, source_target_pairs={{32,0},{64,32},{96,64},{128,96},{160,128},{192,160},{224,192},{256... | collective-permute-start | bytes 345608 | tf_op jit(solution)/shard_map/ppermute | solution.py:231
  25.1 8.8 %collective-permute-start.3 = (bf16[18,3600]{1,0:T(8,128)(2,1)S(1)}, bf16[18,3600]{1,0:T(8,128)(2,1)S(1)}, u32[]{:S(2)}, u32[]{:S(2)}) collective-permute-start(bf16[18,3600]{1,0:T(8,128)(2,1)S(1)} %pad_maximum_fusion.1), channel_id=1, source_target_pairs={{1,0},{2,1},{3,2},{4,3},{5,4},{6,5},{7,6},{8,7},{9,8},{10,9},{11,1... | collective-permute-start | bytes 388808 | tf_op jit(solution)/shard_map/ppermute | solution.py:240
  26.4 7.7 %collective-permute-start.2 = (bf16[18,3600]{1,0:T(8,128)(2,1)S(1)}, bf16[18,3600]{1,0:T(8,128)(2,1)S(1)}, u32[]{:S(2)}, u32[]{:S(2)}) collective-permute-start(bf16[18,3600]{1,0:T(8,128)(2,1)S(1)} %pad_maximum_fusion), channel_id=1, source_target_pairs={{0,1},{1,2},{2,3},{3,4},{4,5},{5,6},{6,7},{7,8},{8,9},{9,10},{10,1... | collective-permute-start | bytes 388808 | tf_op jit(solution)/shard_map/ppermute | solution.py:239
  35.2 11.0 %collective-permute-start.4 = (bf16[64,3600]{1,0:T(8,128)(2,1)S(1)}, bf16[64,3600]{1,0:T(8,128)(2,1)S(1)}, u32[]{:S(2)}, u32[]{:S(2)}) collective-permute-start(bf16[64,3600]{1,0:T(8,128)(2,1)S(1)} %get-tuple-element.19), channel_id=1, source_target_pairs={{0,32},{32,0},{1,33},{33,1},{2,34},{34,2},{3,35},{35,3},{4,36},{36... | collective-permute-start | bytes 1382408 | tf_op jit(solution)/shard_map/ppermute | solution.py:285
  38.0 50.0 %collective-permute-start.5 = (bf16[16,16,3600]{2,1,0:T(8,128)(2,1)S(1)}, bf16[16,16,3600]{2,1,0:T(8,128)(2,1)}, u32[]{:S(2)}, u32[]{:S(2)}) collective-permute-start(bf16[16,16,3600]{2,1,0:T(8,128)(2,1)S(1)} %bitcast.12), channel_id=1, source_target_pairs={{0,8},{32,56},{1,9},{33,57},{2,10},{34,58},{3,11},{35,59},{4,12},{... | collective-permute-start | bytes 5529608 | tf_op jit(solution)/shard_map/ppermute | solution.py:286
  47.3 29.4 %all-to-all-start = ((bf16[32,2,3600]{2,1,0:T(2,128)(2,1)}), bf16[32,2,3600]{2,1,0:T(2,128)(2,1)S(1)}, u32[]{:S(2)}, u32[]{:S(2)}) async-start(bf16[32,2,3600]{2,1,0:T(2,128)(2,1)} %reshape.36), calls=%async_computation | async-start | bytes 950272 | tf_op jit(solution)/shard_map/all_to_all | solution.py:290
  77.9 21.4 %all-to-all-start.1 = ((bf16[16,2,3600]{2,1,0:T(2,128)(2,1)}), bf16[16,2,3600]{2,1,0:T(2,128)(2,1)S(1)}, u32[]{:S(2)}, u32[]{:S(2)}) async-start(bf16[16,2,3600]{2,1,0:T(2,128)(2,1)} %broadcast_in_dim.24), calls=%async_computation.1 | async-start | bytes 475136 | tf_op jit(solution)/shard_map/all_to_all | solution.py:318
  93.3 5.5 %collective-permute-start.6 = (f32[1,256]{1,0:T(1,128)S(1)}, f32[1,256]{1,0:T(1,128)S(1)}, u32[]{:S(2)}, u32[]{:S(2)}) collective-permute-start(f32[1,256]{1,0:T(1,128)S(1)} %best_scores.3), channel_id=1, source_target_pairs={{0,8},{32,56},{1,9},{33,57},{2,10},{34,58},{3,11},{35,59},{4,12},{... | collective-permute-start | bytes 3080 | tf_op jit(solution)/shard_map/ppermute | solution.py:320
Sparse Core Ops, SparseCore 0:
  10.4 61.5 all-gather.1

commit v9 on v7

--- a/solution.py
+++ b/solution.py
@@ -287,11 +287,7 @@
     chip_sums = (kept + swapped.astype(f32)).astype(bf16)
     chip_sums = chip_sums.reshape(lines, -1, pixels)
     parts = lax.all_to_all(chip_sums, SCAN, 0, 0, tiled=True)
-    group_total = jnp.sum(parts.astype(f32), axis=0).astype(bf16)
-
     block = 512
-    copies = jnp.broadcast_to(group_total, (columns,) + group_total.shape)
-    group_totals = lax.all_to_all(copies, DICT, 0, 0, tiled=True)
     own_best, other_best = pl.pallas_call(
         best_scores,
         grid=(panels.shape[0] // block,),
@@ -310,8 +306,15 @@
             transcendentals=0,
         ),
         name="best_scores",
-    )(indexed, other, pltpu.with_memory_space_constraint(panels, pltpu.HBM))
+    )(
+        pltpu.with_memory_space_constraint(indexed, pltpu.HBM),
+        pltpu.with_memory_space_constraint(other, pltpu.HBM),
+        pltpu.with_memory_space_constraint(panels, pltpu.HBM),
+    )
     returned = lax.ppermute(other_best, EVERY, trade)
+    other_best, parts = lax.optimization_barrier((other_best, parts))
+    group_total = jnp.sum(parts.astype(f32), axis=0).astype(bf16)
+    group_totals = lax.all_gather(group_total, DICT, axis=0, tiled=False)
     returned, group_totals = lax.optimization_barrier((returned, group_totals))
     return pl.pallas_call(
         finish,

time: 111 us -> 116 us (1.045)
  waiting for transfers between devices: 4.45 us -> 22.5 us
  starting transfers between devices: 43.2 us -> 35 us
  blocking collectives: 26.1 us -> 22.3 us
    all_to_all x1 -> x0, blocking collectives: 26.1 us -> none  [shards(): parts = lax.all_to_all(chip_sums, SCAN, 0, 0, tiled=True)]
    all_gather x0 -> x1, blocking collectives: none -> 22.3 us  [shards(): group_totals = lax.all_gather(group_total, DICT, axis=0, tiled=False)]
    ppermute x1, waiting for transfers between devices: 0.01 us -> 21.2 us  [shards(): lax.ppermute(indexed.reshape(patterns.shape), EVERY, trade)]
    all_to_all x1, starting transfers between devices: 14.4 us -> 3.89 us  [shards(): parts = lax.all_to_all(chip_sums, SCAN, 0, 0, tiled=True)]
    ppermute x1, starting transfers between devices: 2.36 us -> 4.73 us  [shards(): returned = lax.ppermute(other_best, EVERY, trade)]
    ppermute x1, waiting for transfers between devices: 1.92 us -> 0.01 us  [shards(): returned = lax.ppermute(other_best, EVERY, trade)]
    all_to_all x1, waiting for transfers between devices: 1.24 us -> 0.01 us  [shards(): parts = lax.all_to_all(chip_sums, SCAN, 0, 0, tiled=True)]
  transfers between devices with their start and end apart: 9 -> 9, of which waited for: 4 -> 3; matrix products, arithmetic and copies ran while one was open for 2% -> 2% of each run, Pallas kernels for 15% -> 14%
where the time goes in v9:
time: 116 us
  starting transfers between devices  35 us (30%)
  waiting for transfers between devices  22.5 us (19%)
  blocking collectives  22.3 us (19%)
  Pallas kernels  19.5 us (17%)
  between operations  14.3 us (12%)
  local copies, waits for them, and re-layouts  1.24 us (1%)
    all_gather x1, blocking collectives, shards(): group_totals = lax.all_gather(group_total, DICT, axis=0, tiled=False)  22.3 us
    ppermute x1, waiting for transfers between devices, shards(): lax.ppermute(indexed.reshape(patterns.shape), EVERY, trade)  21.2 us
    ppermute x1, starting transfers between devices, shards(): lax.ppermute(indexed.reshape(patterns.shape), EVERY, trade)  8.15 us
    pallas_call x1, Pallas kernels, shards(): pl.pallas_call(best_scores, grid=(panels.shape[0] // block,), out_shape=(...  8.13 us
    ppermute x1, starting transfers between devices, shards(): low = lax.ppermute(high_edge, DICT, forward)  5.39 us
    ppermute x1, starting transfers between devices, shards(): returned = lax.ppermute(other_best, EVERY, trade)  4.73 us
    ppermute x1, starting transfers between devices, shards(): high = lax.ppermute(low_edge, DICT, backward)  4.69 us
    ppermute x1, starting transfers between devices, shards(): above = lax.ppermute(strip(tile_rows - 1), SCAN, forward)  4 us
  transfers between devices with their start and end apart: 9, of which 3 were waited for; matrix products, arithmetic and copies ran while one was open for 2% of the time, Pallas kernels for 14%

profile of v9, /device:TPU:1, one launch (start us, length us, event | category | flops | bytes accessed | tf_op | source)
XLA Modules:
  0.0 115.6 jit_solution(3206705910074339523)
XLA Ops:
  7.2 3.0 %normalise_templates.1 = bf16[64,3600]{1,0:T(8,128)(2,1)} custom-call(bf16[3600,128]{1,0:T(8,128)(2,1)} %bitcast.14), custom_call_target="tpu_custom_call" | custom-call | tf_op jit(solution)/shard_map/normalise_templates/pallas_call | solution.py:189
  10.3 3.1 %filter_tile.1 = (bf16[16,16,3600]{2,1,0:T(8,128)(2,1)S(1)}, bf16[16,3600]{1,0:T(8,128)(2,1)S(1)}, bf16[16,3600]{1,0:T(8,128)(2,1)S(1)}) custom-call(f32[3600]{0:T(1024)} %background_ref.1, f32[16,16,3600]{2,1,0:T(8,128)} %tile_ref), custom_call_target="tpu_custom_call" | custom-call | tf_op jit(solution)/shard_map/filter_tile/pallas_call | solution.py:202
  13.4 5.4 %collective-permute-start = (bf16[16,3600]{1,0:T(8,128)(2,1)S(1)}, bf16[16,3600]{1,0:T(8,128)(2,1)S(1)}, u32[]{:S(2)}, u32[]{:S(2)}) collective-permute-start(bf16[16,3600]{1,0:T(8,128)(2,1)S(1)} %get-tuple-element.16), channel_id=1, source_target_pairs={{0,32},{32,64},{64,96},{96,128},{128,160},{160,192},{192,224},{224... | collective-permute-start | bytes 345608 | tf_op jit(solution)/shard_map/ppermute | solution.py:229
  18.8 4.7 %collective-permute-start.1 = (bf16[16,3600]{1,0:T(8,128)(2,1)S(1)}, bf16[16,3600]{1,0:T(8,128)(2,1)S(1)}, u32[]{:S(2)}, u32[]{:S(2)}) collective-permute-start(bf16[16,3600]{1,0:T(8,128)(2,1)S(1)} %get-tuple-element.17), channel_id=1, source_target_pairs={{32,0},{64,32},{96,64},{128,96},{160,128},{192,160},{224,192},{256... | collective-permute-start | bytes 345608 | tf_op jit(solution)/shard_map/ppermute | solution.py:230
  23.5 0.1 eq.33
  23.6 0.1 eq.34
  23.8 0.2 select_reduce_fusion
  24.0 1.0 collective-permute-done.1.high_ref
  25.1 1.3 %collective-permute-start.3 = (bf16[18,3600]{1,0:T(8,128)(2,1)S(1)}, bf16[18,3600]{1,0:T(8,128)(2,1)S(1)}, u32[]{:S(2)}, u32[]{:S(2)}) collective-permute-start(bf16[18,3600]{1,0:T(8,128)(2,1)S(1)} %pad_maximum_fusion.1), channel_id=1, source_target_pairs={{1,0},{2,1},{3,2},{4,3},{5,4},{6,5},{7,6},{8,7},{9,8},{10,9},{11,1... | collective-permute-start | bytes 388808 | tf_op jit(solution)/shard_map/ppermute | solution.py:239
  26.4 4.0 %collective-permute-start.2 = (bf16[18,3600]{1,0:T(8,128)(2,1)S(1)}, bf16[18,3600]{1,0:T(8,128)(2,1)S(1)}, u32[]{:S(2)}, u32[]{:S(2)}) collective-permute-start(bf16[18,3600]{1,0:T(8,128)(2,1)S(1)} %pad_maximum_fusion), channel_id=1, source_target_pairs={{0,1},{1,2},{2,3},{3,4},{4,5},{5,6},{6,7},{7,8},{8,9},{9,10},{10,1... | collective-permute-start | bytes 388808 | tf_op jit(solution)/shard_map/ppermute | solution.py:238
  30.4 3.5 %inner_rows.1.inner_ref = bf16[224,3600]{1,0:T(8,128)(2,1)S(1)} custom-call(bf16[16,16,3600]{2,1,0:T(8,128)(2,1)S(1)} %get-tuple-element.15.tile_ref, bf16[16,3600]{1,0:T(8,128)(2,1)S(1)} %collective-permute-done.low_ref, bf16[16,3600]{1,0:T(8,128)(2,1)S(1)} %collective-permute-done.1.high_ref), custom_call_target="tpu_custom_call" | custom-call | flops 9676800 | bytes 12902400 | tf_op jit(solution)/shard_map/inner_rows/pallas_call | solution.py:248
  33.9 0.3 collective-permute-done.2.above_ref
  34.2 1.0 outer_rows.1
  35.2 2.9 %collective-permute-start.6 = (bf16[64,3600]{1,0:T(8,128)(2,1)S(1)}, bf16[64,3600]{1,0:T(8,128)(2,1)S(1)}, u32[]{:S(2)}, u32[]{:S(2)}) collective-permute-start(bf16[64,3600]{1,0:T(8,128)(2,1)S(1)} %get-tuple-element.22), channel_id=1, source_target_pairs={{0,32},{32,0},{1,33},{33,1},{2,34},{34,2},{3,35},{35,3},{4,36},{36... | collective-permute-start | bytes 1382408 | tf_op jit(solution)/shard_map/ppermute | solution.py:284
  38.0 8.1 %collective-permute-start.4 = (bf16[16,16,3600]{2,1,0:T(8,128)(2,1)S(1)}, bf16[16,16,3600]{2,1,0:T(8,128)(2,1)}, u32[]{:S(2)}, u32[]{:S(2)}) collective-permute-start(bf16[16,16,3600]{2,1,0:T(8,128)(2,1)S(1)} %bitcast.13), channel_id=1, source_target_pairs={{0,8},{32,56},{1,9},{33,57},{2,10},{34,58},{3,11},{35,59},{4,12},{... | collective-permute-start | bytes 5529608 | tf_op jit(solution)/shard_map/ppermute | solution.py:285
  46.2 0.1 add_convert_fusion
  46.3 1.0 reshape.38
  47.3 3.9 %all-to-all-start = ((bf16[32,2,3600]{2,1,0:T(2,128)(2,1)}), bf16[32,2,3600]{2,1,0:T(2,128)(2,1)S(1)}, u32[]{:S(2)}, u32[]{:S(2)}) async-start(bf16[32,2,3600]{2,1,0:T(2,128)(2,1)} %reshape.38), calls=%async_computation | async-start | bytes 950272 | tf_op jit(solution)/shard_map/all_to_all | solution.py:289
  51.2 21.2 %collective-permute-done.4 = bf16[16,16,3600]{2,1,0:T(8,128)(2,1)} collective-permute-done((bf16[16,16,3600]{2,1,0:T(8,128)(2,1)S(1)}, bf16[16,16,3600]{2,1,0:T(8,128)(2,1)}, u32[]{:S(2)}, u32[]{:S(2)}) %collective-permute-start.4) | collective-permute-done | bytes 1843232 | tf_op jit(solution)/shard_map/ppermute | solution.py:285
  72.4 8.1 %best_scores.1 = (f32[1,256]{1,0:T(1,128)S(1)}, f32[1,256]{1,0:T(1,128)S(1)}) custom-call(bf16[256,3600]{1,0:T(8,128)(2,1)} %copy-done, bf16[256,3600]{1,0:T(8,128)(2,1)} %bitcast.7.other_ref, bf16[1024,3600]{1,0:T(8,128)(2,1)} %all-gather.4.cloned.1.call-done.panel_ref), custom_call_target="tpu_custom_call" | custom-call | flops 3774873600 | bytes 7372800 | tf_op jit(solution)/shard_map/best_scores/pallas_call | solution.py:291
  80.5 4.7 %collective-permute-start.5 = (f32[1,256]{1,0:T(1,128)S(1)}, f32[1,256]{1,0:T(1,128)S(1)}, u32[]{:S(2)}, u32[]{:S(2)}) collective-permute-start(f32[1,256]{1,0:T(1,128)S(1)} %get-tuple-element.20), channel_id=1, source_target_pairs={{0,8},{32,56},{1,9},{33,57},{2,10},{34,58},{3,11},{35,59},{4,12},{... | collective-permute-start | bytes 3080 | tf_op jit(solution)/shard_map/ppermute | solution.py:314
  85.2 0.4 reduce_sum.25
  85.6 22.3 %all-gather.1.totals_ref = bf16[16,2,3600]{2,1,0:T(2,128)(2,1)S(1)} all-gather(bf16[1,2,3600]{2,1,0:T(2,128)(2,1)S(1)} %bitcast.15), channel_id=2, replica_groups=mesh['z'=8,'core'=2,'x'=4,'y'=8] {'z','core'}, dimensions={0}, use_global_device_ids=true | all-gather | bytes 244800 | tf_op jit(solution)/shard_map/all_gather | solution.py:317
  107.9 0.8 finish.1
  (23 shorter events, 0.3 us)
Async XLA Ops:
  7.2 65.2 %all-gather.4.cloned.1.call-start = ((), (), s32[]{:S(2)}) async-start(), calls=%async_computation.1 | async-start | bytes 8077312 | tf_op jit(solution)/shard_map/all_gather | solution.py:198
  10.3 13.2 %copy-start.1 = (s32[16,16]{1,0:T(8,128)S(1)}, s32[16,16]{1,0:T(8,128)}, u32[]{:S(2)}) copy-start(s32[16,16]{1,0:T(8,128)} %param.10) | copy-start | bytes 3076
  10.3 13.3 %copy-start.2 = (s32[16,16]{1,0:T(8,128)S(1)}, s32[16,16]{1,0:T(8,128)}, u32[]{:S(2)}) copy-start(s32[16,16]{1,0:T(8,128)} %param.9) | copy-start | bytes 3076
  10.3 13.5 %copy-start.3 = (s32[128]{0:T(128)S(1)}, s32[128]{0:T(128)}, u32[]{:S(2)}) copy-start(s32[128]{0:T(128)} %param.11) | copy-start | bytes 1540
  13.4 10.5 %collective-permute-start = (bf16[16,3600]{1,0:T(8,128)(2,1)S(1)}, bf16[16,3600]{1,0:T(8,128)(2,1)S(1)}, u32[]{:S(2)}, u32[]{:S(2)}) collective-permute-start(bf16[16,3600]{1,0:T(8,128)(2,1)S(1)} %get-tuple-element.16), channel_id=1, source_target_pairs={{0,32},{32,64},{64,96},{96,128},{128,160},{160,192},{192,224},{224... | collective-permute-start | bytes 345608 | tf_op jit(solution)/shard_map/ppermute | solution.py:229
  18.8 6.2 %collective-permute-start.1 = (bf16[16,3600]{1,0:T(8,128)(2,1)S(1)}, bf16[16,3600]{1,0:T(8,128)(2,1)S(1)}, u32[]{:S(2)}, u32[]{:S(2)}) collective-permute-start(bf16[16,3600]{1,0:T(8,128)(2,1)S(1)} %get-tuple-element.17), channel_id=1, source_target_pairs={{32,0},{64,32},{96,64},{128,96},{160,128},{192,160},{224,192},{256... | collective-permute-start | bytes 345608 | tf_op jit(solution)/shard_map/ppermute | solution.py:230
  25.1 8.8 %collective-permute-start.3 = (bf16[18,3600]{1,0:T(8,128)(2,1)S(1)}, bf16[18,3600]{1,0:T(8,128)(2,1)S(1)}, u32[]{:S(2)}, u32[]{:S(2)}) collective-permute-start(bf16[18,3600]{1,0:T(8,128)(2,1)S(1)} %pad_maximum_fusion.1), channel_id=1, source_target_pairs={{1,0},{2,1},{3,2},{4,3},{5,4},{6,5},{7,6},{8,7},{9,8},{10,9},{11,1... | collective-permute-start | bytes 388808 | tf_op jit(solution)/shard_map/ppermute | solution.py:239
  26.4 7.7 %collective-permute-start.2 = (bf16[18,3600]{1,0:T(8,128)(2,1)S(1)}, bf16[18,3600]{1,0:T(8,128)(2,1)S(1)}, u32[]{:S(2)}, u32[]{:S(2)}) collective-permute-start(bf16[18,3600]{1,0:T(8,128)(2,1)S(1)} %pad_maximum_fusion), channel_id=1, source_target_pairs={{0,1},{1,2},{2,3},{3,4},{4,5},{5,6},{6,7},{7,8},{8,9},{9,10},{10,1... | collective-permute-start | bytes 388808 | tf_op jit(solution)/shard_map/ppermute | solution.py:238
  35.2 12.1 %copy-start = (bf16[256,3600]{1,0:T(8,128)(2,1)}, bf16[256,3600]{1,0:T(8,128)(2,1)S(1)}, u32[]{:S(2)}) copy-start(bf16[256,3600]{1,0:T(8,128)(2,1)S(1)} %get-tuple-element.18.own_ref) | copy-start | bytes 5529604
  35.2 11.0 %collective-permute-start.6 = (bf16[64,3600]{1,0:T(8,128)(2,1)S(1)}, bf16[64,3600]{1,0:T(8,128)(2,1)S(1)}, u32[]{:S(2)}, u32[]{:S(2)}) collective-permute-start(bf16[64,3600]{1,0:T(8,128)(2,1)S(1)} %get-tuple-element.22), channel_id=1, source_target_pairs={{0,32},{32,0},{1,33},{33,1},{2,34},{34,2},{3,35},{35,3},{4,36},{36... | collective-permute-start | bytes 1382408 | tf_op jit(solution)/shard_map/ppermute | solution.py:284
  38.0 34.3 %collective-permute-start.4 = (bf16[16,16,3600]{2,1,0:T(8,128)(2,1)S(1)}, bf16[16,16,3600]{2,1,0:T(8,128)(2,1)}, u32[]{:S(2)}, u32[]{:S(2)}) collective-permute-start(bf16[16,16,3600]{2,1,0:T(8,128)(2,1)S(1)} %bitcast.13), channel_id=1, source_target_pairs={{0,8},{32,56},{1,9},{33,57},{2,10},{34,58},{3,11},{35,59},{4,12},{... | collective-permute-start | bytes 5529608 | tf_op jit(solution)/shard_map/ppermute | solution.py:285
  47.3 38.0 %all-to-all-start = ((bf16[32,2,3600]{2,1,0:T(2,128)(2,1)}), bf16[32,2,3600]{2,1,0:T(2,128)(2,1)S(1)}, u32[]{:S(2)}, u32[]{:S(2)}) async-start(bf16[32,2,3600]{2,1,0:T(2,128)(2,1)} %reshape.38), calls=%async_computation | async-start | bytes 950272 | tf_op jit(solution)/shard_map/all_to_all | solution.py:289
  80.5 27.4 %collective-permute-start.5 = (f32[1,256]{1,0:T(1,128)S(1)}, f32[1,256]{1,0:T(1,128)S(1)}, u32[]{:S(2)}, u32[]{:S(2)}) collective-permute-start(f32[1,256]{1,0:T(1,128)S(1)} %get-tuple-element.20), channel_id=1, source_target_pairs={{0,8},{32,56},{1,9},{33,57},{2,10},{34,58},{3,11},{35,59},{4,12},{... | collective-permute-start | bytes 3080 | tf_op jit(solution)/shard_map/ppermute | solution.py:314
Sparse Core Ops, SparseCore 0:
  10.4 61.5 all-gather.3

commit v10 on v8

--- a/solution.py
+++ b/solution.py
@@ -36,7 +36,7 @@
         values = panel_ref[start : start + step, :].astype(jnp.float32) - mean
         total = total + jnp.sum(values * values, axis=0, keepdims=True)
     scale = lax.rsqrt(total * (1.0 / pixels) + EPS)
-    first = (lax.axis_index("x") & 1) * held
+    first = ((lax.axis_index("x") + lax.axis_index("y")) & 1) * held
     lane = lax.broadcasted_iota(jnp.int32, (held, lanes), 1)
     place = lax.broadcasted_iota(jnp.int32, (held, lanes), 0)
     chosen = jnp.where(lane == place + first, 1.0, 0.0).astype(jnp.bfloat16)
@@ -102,17 +102,19 @@
 
 def outer_rows(
     point_row_ref, first_ref, second_ref, third_ref, fourth_ref, low_ref, high_ref, above_ref, below_ref,
-    inner_ref, out_ref, kept_ref, sent_ref, shift,
+    inner_ref, upper_ref, lower_ref, kept_ref, sent_ref, shift,
 ):
-    points, pixels = out_ref.shape
+    middle, pixels = upper_ref.shape
     cols = first_ref.shape[0]
-    rows = points // cols
-    out_ref[cols : points - cols, :] = inner_ref[...]
+    points = 2 * middle
+    last = points // cols - 1
+    upper_ref[cols:, :] = inner_ref[: middle - cols, :]
+    lower_ref[: middle - cols, :] = inner_ref[middle - cols :, :]
     low, high = low_ref[...].astype(jnp.float32), high_ref[...].astype(jnp.float32)
     above, below = above_ref[...].astype(jnp.float32), below_ref[...].astype(jnp.float32)
-    for halo, near_ref, next_ref, row, inward in (
-        (above, first_ref, second_ref, 0, 1),
-        (below, fourth_ref, third_ref, rows - 1, -1),
+    for out_ref, start, halo, near_ref, next_ref, row, inward in (
+        (upper_ref, 0, above, first_ref, second_ref, 0, 1),
+        (lower_ref, middle - cols, below, fourth_ref, third_ref, last, -1),
     ):
         column = halo[:cols] + near_ref[...].astype(jnp.float32) + next_ref[...].astype(jnp.float32)
         edges = []
@@ -122,7 +124,7 @@
                 + values[row : row + 1]
                 + values[row + inward : row + inward + 1]
             )
-        out_ref[row * cols : (row + 1) * cols, :] = index_points(column, edges[0], edges[1], shift)
+        out_ref[start : start + cols, :] = index_points(column, edges[0], edges[1], shift)
     half = kept_ref.shape[0]
     k = lax.broadcasted_iota(jnp.int32, (2 * half, points), 0)
     core = lax.axis_index("core") ^ (k // half)
@@ -131,7 +133,9 @@
     step = 1024
     for start in range(0, pixels, step):
         stop = min(start + step, pixels)
-        sums = jnp.dot(selector, out_ref[:, start:stop], preferred_element_type=jnp.float32)
+        sums = jnp.dot(
+            selector[:, :middle], upper_ref[:, start:stop], preferred_element_type=jnp.float32
+        ) + jnp.dot(selector[:, middle:], lower_ref[:, start:stop], preferred_element_type=jnp.float32)
         kept_ref[:, start:stop] = sums[:half]
         sent_ref[:, start:stop] = sums[half:].astype(jnp.bfloat16)
 
@@ -147,11 +151,14 @@
     return lax.dot_general(points, panel, (((1,), (1,)), ((), ())), preferred_element_type=jnp.float32)
 
 
-def best_scores(panel_ref, points_ref, out_ref, best_ref):
+def best_scores(panel_ref, first_ref, second_ref, out_ref, points_ref, best_ref):
     step = pl.program_id(0)
 
     @pl.when(step == 0)
     def _():
+        half = first_ref.shape[0]
+        points_ref[:half, :] = first_ref[...]
+        points_ref[half:, :] = second_ref[...]
         best_ref[...] = jnp.full(best_ref.shape, -jnp.inf, jnp.float32)
 
     best = lane_best(best_ref[...], products(points_ref[...], panel_ref[...]))
@@ -259,31 +266,37 @@
         ),
         name="inner_rows",
     )(filtered, low, high)
-    indexed, kept, sent = pl.pallas_call(
+    upper, lower, kept, sent = pl.pallas_call(
         outer_rows,
         out_shape=(
-            jax.ShapeDtypeStruct((points, pixels), bf16),
+            jax.ShapeDtypeStruct((points // 2, pixels), bf16),
+            jax.ShapeDtypeStruct((points // 2, pixels), bf16),
             jax.ShapeDtypeStruct((grain_count // 2, pixels), f32),
             jax.ShapeDtypeStruct((grain_count // 2, pixels), bf16),
         ),
         in_specs=[pl.BlockSpec(memory_space=VMEM)] * 10,
-        out_specs=[pl.BlockSpec(memory_space=VMEM)] * 3,
+        out_specs=[pl.BlockSpec(memory_space=VMEM)] * 4,
         scratch_shapes=[VMEM((32, pixels), f32)],
         compiler_params=params(10),
         name="outer_rows",
     )(point_row, filtered[0], filtered[1], filtered[-2], filtered[-1], low, high, above, below, inner)
 
     xs, ys = lax.axis_size("x"), lax.axis_size("y")
-    trade = []
+    trades = ([], [])
     for z in range(lax.axis_size("z")):
-        for x in range(xs):
-            for y in range(ys):
-                for core in range(2):
+        for core in range(2):
+            for x in range(xs):
+                for y in range(ys):
                     at = (z * 2 + core) * xs
-                    partner = (((x + core) ^ 1) - core) % xs
-                    trade.append(((at + x) * ys + y, (at + partner) * ys + y))
+                    beside = (((x + core) ^ 1) - core) % xs
+                    trades[0].append(((at + x) * ys + y, (at + beside) * ys + y))
+                    beside = (((y + core) ^ 1) - core) % ys
+                    trades[1].append(((at + x) * ys + y, (at + x) * ys + beside))
     swapped = lax.ppermute(sent, "core", [(0, 1), (1, 0)])
-    other = lax.ppermute(indexed.reshape(patterns.shape), EVERY, trade).reshape(points, pixels)
+    others = [
+        lax.ppermute(half.reshape(-1, tile_cols, pixels), EVERY, trade).reshape(half.shape)
+        for half, trade in zip((upper, lower), trades)
+    ]
 
     chip_sums = (kept + swapped.astype(f32)).astype(bf16)
     chip_sums = chip_sums.reshape(lines, -1, pixels)
@@ -296,10 +309,11 @@
             out_shape=jax.ShapeDtypeStruct((1, points), f32),
             in_specs=[
                 pl.BlockSpec((block, pixels), lambda i: (i, 0)),
-                pl.BlockSpec((points, pixels), lambda i: (0, 0)),
+                pl.BlockSpec((points // 2, pixels), lambda i: (0, 0)),
+                pl.BlockSpec((points // 2, pixels), lambda i: (0, 0)),
             ],
             out_specs=pl.BlockSpec((1, points), lambda i: (0, 0)),
-            scratch_shapes=[VMEM((points, 128), f32)],
+            scratch_shapes=[VMEM((points, pixels), bf16), VMEM((points, 128), f32)],
             compiler_params=params(20),
             cost_estimate=pl.CostEstimate(
                 flops=2 * points * pixels * panels.shape[0],
@@ -310,14 +324,17 @@
         ),
         pltpu.with_memory_space_constraint(panels, pltpu.HBM),
     )
-    own_best = scored(indexed)
+    own_best = scored(upper, lower)
     own_best, parts = lax.optimization_barrier((own_best, parts))
     group_total = jnp.sum(parts.astype(f32), axis=0).astype(bf16)
 
     copies = jnp.broadcast_to(group_total, (columns,) + group_total.shape)
     group_totals = lax.all_to_all(copies, DICT, 0, 0, tiled=True)
-    other_best = scored(other)
-    returned = lax.ppermute(other_best, EVERY, trade)
+    other_best = scored(*others)
+    returned = [
+        lax.ppermute(best, EVERY, trade) for best, trade in zip(jnp.split(other_best, 2, axis=1), trades)
+    ]
+    returned = jnp.concatenate(returned, axis=1)
     returned, group_totals = lax.optimization_barrier((returned, group_totals))
     return pl.pallas_call(
         finish,

time: 107 us -> 109 us (1.019)
  waiting for transfers between devices: 25.7 us -> 19.5 us
  starting transfers between devices: 42.9 us -> 47.5 us
  other arithmetic: 0.76 us -> 2.57 us
    ppermute x2 -> x4, starting transfers between devices: 10.5 us -> 16.9 us  [the longest x2 10.1 us: shards(): lax.ppermute(half.reshape(-1, tile_cols, pixels), EVERY, trade)]
    all_gather x1, waiting for transfers between devices: 20.9 us -> 16.2 us  [shards(): panels = lax.all_gather(panel, DICT, axis=0, tiled=True)]
    all_to_all x1, starting transfers between devices: 10.2 us -> 7.7 us  [shards(): group_totals = lax.all_to_all(copies, DICT, 0, 0, tiled=True)]
    ppermute x2 -> x4, waiting for transfers between devices: 3.16 us -> 1.98 us  [the longest x2 1.98 us: shards(): lax.ppermute(best, EVERY, trade)]
  transfers between devices with their start and end apart: 10 -> 12, of which waited for: 5 -> 4; matrix products, arithmetic and copies ran while one was open for 3% -> 5% of each run, Pallas kernels for 16% -> 16%
where the time goes in v10:
time: 109 us; the launch traced here: 108 us
  starting transfers between devices  47.5 us (44%)
  Pallas kernels  21.4 us (20%)
  waiting for transfers between devices  19.5 us (18%)
  between operations  14.3 us (13%)
  local copies, waits for them, and re-layouts  3.1 us (3%)
  other arithmetic  2.57 us (2%)
    all_gather x1, waiting for transfers between devices, shards(): panels = lax.all_gather(panel, DICT, axis=0, tiled=True)  16.2 us
    ppermute x2, starting transfers between devices, shards(): lax.ppermute(half.reshape(-1, tile_cols, pixels), EVERY, trade)  10.1 us
    all_to_all x1, starting transfers between devices, shards(): group_totals = lax.all_to_all(copies, DICT, 0, 0, tiled=True)  7.7 us
    ppermute x2, starting transfers between devices, shards(): lax.ppermute(best, EVERY, trade)  6.84 us
    ppermute x1, starting transfers between devices, shards(): low = lax.ppermute(high_edge, DICT, forward)  5.39 us
    pallas_call x1, Pallas kernels, shards(): other_best = scored(*others)  5.01 us
    pallas_call x1, Pallas kernels, shards(): own_best = scored(upper, lower)  4.74 us
    ppermute x1, starting transfers between devices, shards(): high = lax.ppermute(low_edge, DICT, backward)  4.7 us
  transfers between devices with their start and end apart: 12, of which 4 were waited for; matrix products, arithmetic and copies ran while one was open for 5% of the time, Pallas kernels for 16%

profile of v10, /device:TPU:1, one launch (start us, length us, event | category | flops | bytes accessed | tf_op | source)
XLA Modules:
  0.0 108.3 jit_solution(5696234968133988002)
XLA Ops:
  7.2 3.1 %normalise_templates.1 = bf16[64,3600]{1,0:T(8,128)(2,1)} custom-call(bf16[3600,128]{1,0:T(8,128)(2,1)} %bitcast.17), custom_call_target="tpu_custom_call" | custom-call | tf_op jit(solution)/shard_map/normalise_templates/pallas_call | solution.py:197
  10.4 3.1 %filter_tile.1 = (bf16[16,16,3600]{2,1,0:T(8,128)(2,1)S(1)}, bf16[16,3600]{1,0:T(8,128)(2,1)S(1)}, bf16[16,3600]{1,0:T(8,128)(2,1)S(1)}) custom-call(f32[3600]{0:T(1024)} %background_ref.1, f32[16,16,3600]{2,1,0:T(8,128)} %tile_ref), custom_call_target="tpu_custom_call" | custom-call | tf_op jit(solution)/shard_map/filter_tile/pallas_call | solution.py:210
  13.5 5.4 %collective-permute-start = (bf16[16,3600]{1,0:T(8,128)(2,1)S(1)}, bf16[16,3600]{1,0:T(8,128)(2,1)S(1)}, u32[]{:S(2)}, u32[]{:S(2)}) collective-permute-start(bf16[16,3600]{1,0:T(8,128)(2,1)S(1)} %get-tuple-element.16), channel_id=1, source_target_pairs={{0,32},{32,64},{64,96},{96,128},{128,160},{160,192},{192,224},{224... | collective-permute-start | bytes 345608 | tf_op jit(solution)/shard_map/ppermute | solution.py:237
  18.9 4.7 %collective-permute-start.1 = (bf16[16,3600]{1,0:T(8,128)(2,1)S(1)}, bf16[16,3600]{1,0:T(8,128)(2,1)S(1)}, u32[]{:S(2)}, u32[]{:S(2)}) collective-permute-start(bf16[16,3600]{1,0:T(8,128)(2,1)S(1)} %get-tuple-element.17), channel_id=1, source_target_pairs={{32,0},{64,32},{96,64},{128,96},{160,128},{192,160},{224,192},{256... | collective-permute-start | bytes 345608 | tf_op jit(solution)/shard_map/ppermute | solution.py:238
  24.1 1.0 collective-permute-done.1.high_ref
  25.1 1.3 %collective-permute-start.3 = (bf16[18,3600]{1,0:T(8,128)(2,1)S(1)}, bf16[18,3600]{1,0:T(8,128)(2,1)S(1)}, u32[]{:S(2)}, u32[]{:S(2)}) collective-permute-start(bf16[18,3600]{1,0:T(8,128)(2,1)S(1)} %pad_maximum_fusion.1), channel_id=1, source_target_pairs={{1,0},{2,1},{3,2},{4,3},{5,4},{6,5},{7,6},{8,7},{9,8},{10,9},{11,1... | collective-permute-start | bytes 388808 | tf_op jit(solution)/shard_map/ppermute | solution.py:247
  26.5 4.0 %collective-permute-start.2 = (bf16[18,3600]{1,0:T(8,128)(2,1)S(1)}, bf16[18,3600]{1,0:T(8,128)(2,1)S(1)}, u32[]{:S(2)}, u32[]{:S(2)}) collective-permute-start(bf16[18,3600]{1,0:T(8,128)(2,1)S(1)} %pad_maximum_fusion), channel_id=1, source_target_pairs={{0,1},{1,2},{2,3},{3,4},{4,5},{5,6},{6,7},{7,8},{8,9},{9,10},{10,1... | collective-permute-start | bytes 388808 | tf_op jit(solution)/shard_map/ppermute | solution.py:246
  30.5 3.5 %inner_rows.1.inner_ref = bf16[224,3600]{1,0:T(8,128)(2,1)S(1)} custom-call(bf16[16,16,3600]{2,1,0:T(8,128)(2,1)S(1)} %get-tuple-element.15.tile_ref, bf16[16,3600]{1,0:T(8,128)(2,1)S(1)} %collective-permute-done.low_ref, bf16[16,3600]{1,0:T(8,128)(2,1)S(1)} %collective-permute-done.1.high_ref), custom_call_target="tpu_custom_call" | custom-call | flops 9676800 | bytes 12902400 | tf_op jit(solution)/shard_map/inner_rows/pallas_call | solution.py:256
  34.2 1.2 %outer_rows.1 = (bf16[128,3600]{1,0:T(8,128)(2,1)S(1)}, bf16[128,3600]{1,0:T(8,128)(2,1)S(1)}, f32[64,3600]{1,0:T(8,128)S(1)}, bf16[64,3600]{1,0:T(8,128)(2,1)S(1)}) custom-call(s32[1,256]{1,0:T(1,128)S(1)} %broadcast_select_fusion.point_row_ref, bf16[16,3600]{1,0:T(8,128)(2,1)S(1)} %get-tuple-element.29.first_ref, ...), custom_call_target="tpu_custom_call" | custom-call | tf_op jit(solution)/shard_map/outer_rows/pallas_call | solution.py:269
  35.4 2.9 %collective-permute-start.4 = (bf16[64,3600]{1,0:T(8,128)(2,1)S(1)}, bf16[64,3600]{1,0:T(8,128)(2,1)S(1)}, u32[]{:S(2)}, u32[]{:S(2)}) collective-permute-start(bf16[64,3600]{1,0:T(8,128)(2,1)S(1)} %get-tuple-element.21), channel_id=1, source_target_pairs={{0,32},{32,0},{1,33},{33,1},{2,34},{34,2},{3,35},{35,3},{4,36},{36... | collective-permute-start | bytes 1382408 | tf_op jit(solution)/shard_map/ppermute | solution.py:295
  38.3 8.2 %collective-permute-start.5 = (bf16[8,16,3600]{2,1,0:T(8,128)(2,1)S(1)}, bf16[8,16,3600]{2,1,0:T(8,128)(2,1)S(1)}, u32[]{:S(2)}, u32[]{:S(2)}) collective-permute-start(bf16[8,16,3600]{2,1,0:T(8,128)(2,1)S(1)} %bitcast.15), channel_id=1, source_target_pairs={{0,8},{1,9},{2,10},{3,11},{4,12},{5,13},{6,14},{7,15},{8,0},{9,1},... | collective-permute-start | bytes 2764808 | tf_op jit(solution)/shard_map/ppermute | solution.py:297
  46.4 1.9 %collective-permute-start.6 = (bf16[8,16,3600]{2,1,0:T(8,128)(2,1)S(1)}, bf16[8,16,3600]{2,1,0:T(8,128)(2,1)}, u32[]{:S(2)}, u32[]{:S(2)}) collective-permute-start(bf16[8,16,3600]{2,1,0:T(8,128)(2,1)S(1)} %bitcast.14), channel_id=1, source_target_pairs={{0,1},{1,0},{2,3},{3,2},{4,5},{5,4},{6,7},{7,6},{8,9},{9,8},{10,11... | collective-permute-start | bytes 2764808 | tf_op jit(solution)/shard_map/ppermute | solution.py:297
  48.4 0.9 add_convert_fusion
  49.2 2.0 %reshape.42 = bf16[32,2,3600]{2,1,0:T(2,128)(2,1)} reshape(bf16[64,3600]{1,0:T(8,128)(2,1)} %add_convert_fusion) | data formatting | bytes 921600 | tf_op jit(solution)/shard_map/reshape | solution.py:302
  51.2 4.6 %all-to-all-start = ((bf16[32,2,3600]{2,1,0:T(2,128)(2,1)}), bf16[32,2,3600]{2,1,0:T(2,128)(2,1)}, u32[]{:S(2)}, u32[]{:S(2)}) async-start(bf16[32,2,3600]{2,1,0:T(2,128)(2,1)} %reshape.42), calls=%async_computation | async-start | bytes 950272 | tf_op jit(solution)/shard_map/all_to_all | solution.py:303
  55.8 16.2 %all-gather.2.cloned.1.call-done.panel_ref = bf16[1024,3600]{1,0:T(8,128)(2,1)} async-done(((bf16[64,3600]{1,0:T(8,128)(2,1)}), bf16[1024,3600]{1,0:T(8,128)(2,1)}) %all-gather.2.cloned.1.call-update) | async-done | bytes 7372816 | tf_op jit(solution)/shard_map/all_gather | solution.py:206
  72.0 4.7 %best_scores.2.own_best_ref = f32[1,256]{1,0:T(1,128)S(1)} custom-call(bf16[1024,3600]{1,0:T(8,128)(2,1)} %all-gather.2.cloned.1.call-done.panel_ref, bf16[128,3600]{1,0:T(8,128)(2,1)S(1)} %get-tuple-element.18.first_ref, bf16[128,3600]{1,0:T(8,128)(2,1)S(1)} %get-tuple-element.19.second_ref), custom_call_target="tpu_custom_call" | custom-call | flops 1887436800 | bytes 7372800 | tf_op jit(solution)/shard_map/best_scores/pallas_call | solution.py:327
  76.8 1.4 %reduce_sum.25 = bf16[2,3600]{1,0:T(2,128)(2,1)S(1)} reduce(bf16[32,2,3600]{2,1,0:T(2,128)(2,1)} %all-to-all-done, bf16[]{:T(256)} %constant.8.clone.1), dimensions={0}, to_apply=%region_1.2 | reduce | flops 223200 | bytes 475202 | tf_op jit(solution)/shard_map/reduce_sum | solution.py:329
  78.2 0.8 broadcast_in_dim.24
  79.1 7.7 %all-to-all-start.1 = ((bf16[16,2,3600]{2,1,0:T(2,128)(2,1)}), bf16[16,2,3600]{2,1,0:T(2,128)(2,1)S(1)}, u32[]{:S(2)}, u32[]{:S(2)}) async-start(bf16[16,2,3600]{2,1,0:T(2,128)(2,1)} %broadcast_in_dim.24), calls=%async_computation.1 | async-start | bytes 475136 | tf_op jit(solution)/shard_map/all_to_all | solution.py:332
  86.8 5.0 %best_scores.3 = f32[1,256]{1,0:T(1,128)S(1)} custom-call(bf16[1024,3600]{1,0:T(8,128)(2,1)} %all-gather.2.cloned.1.call-done.panel_ref, bf16[128,3600]{1,0:T(8,128)(2,1)S(1)} %bitcast.16, bf16[128,3600]{1,0:T(8,128)(2,1)} %bitcast.9.second_ref), custom_call_target="tpu_custom_call" | custom-call | flops 1887436800 | bytes 7372800 | tf_op jit(solution)/shard_map/best_scores/pallas_call | solution.py:333
  91.8 3.3 %collective-permute-start.7 = (f32[1,128]{1,0:T(1,128)S(1)}, f32[1,128]{1,0:T(1,128)S(1)}, u32[]{:S(2)}, u32[]{:S(2)}) collective-permute-start(f32[1,128]{1,0:T(1,128)S(1)} %get-tuple-element.34), channel_id=1, source_target_pairs={{0,8},{1,9},{2,10},{3,11},{4,12},{5,13},{6,14},{7,15},{8,0},{9,1},... | collective-permute-start | bytes 1544 | tf_op jit(solution)/shard_map/ppermute | solution.py:335
  95.2 3.5 %collective-permute-start.8 = (f32[1,128]{1,0:T(1,128)S(1)}, f32[1,128]{1,0:T(1,128)S(1)}, u32[]{:S(2)}, u32[]{:S(2)}) collective-permute-start(f32[1,128]{1,0:T(1,128)S(1)} %get-tuple-element.35), channel_id=1, source_target_pairs={{0,1},{1,0},{2,3},{3,2},{4,5},{5,4},{6,7},{7,6},{8,9},{9,8},{10,11... | collective-permute-start | bytes 1544 | tf_op jit(solution)/shard_map/ppermute | solution.py:335
  98.7 2.0 %collective-permute-done.8 = f32[1,128]{1,0:T(1,128)S(1)} collective-permute-done((f32[1,128]{1,0:T(1,128)S(1)}, f32[1,128]{1,0:T(1,128)S(1)}, u32[]{:S(2)}, u32[]{:S(2)}) %collective-permute-start.8) | collective-permute-done | bytes 544 | tf_op jit(solution)/shard_map/ppermute | solution.py:335
  (30 shorter events, 1.7 us)
Async XLA Ops:
  7.2 64.9 %all-gather.2.cloned.1.call-start = ((), (), s32[]{:S(2)}) async-start(), calls=%async_computation.2 | async-start | bytes 8077312 | tf_op jit(solution)/shard_map/all_gather | solution.py:206
  10.3 13.2 %copy-start = (s32[16,16]{1,0:T(8,128)S(1)}, s32[16,16]{1,0:T(8,128)}, u32[]{:S(2)}) copy-start(s32[16,16]{1,0:T(8,128)} %param.10) | copy-start | bytes 3076
  10.4 13.3 %copy-start.1 = (s32[16,16]{1,0:T(8,128)S(1)}, s32[16,16]{1,0:T(8,128)}, u32[]{:S(2)}) copy-start(s32[16,16]{1,0:T(8,128)} %param.9) | copy-start | bytes 3076
  10.4 13.5 %copy-start.2 = (s32[128]{0:T(128)S(1)}, s32[128]{0:T(128)}, u32[]{:S(2)}) copy-start(s32[128]{0:T(128)} %param.11) | copy-start | bytes 1540
  13.5 10.5 %collective-permute-start = (bf16[16,3600]{1,0:T(8,128)(2,1)S(1)}, bf16[16,3600]{1,0:T(8,128)(2,1)S(1)}, u32[]{:S(2)}, u32[]{:S(2)}) collective-permute-start(bf16[16,3600]{1,0:T(8,128)(2,1)S(1)} %get-tuple-element.16), channel_id=1, source_target_pairs={{0,32},{32,64},{64,96},{96,128},{128,160},{160,192},{192,224},{224... | collective-permute-start | bytes 345608 | tf_op jit(solution)/shard_map/ppermute | solution.py:237
  18.9 6.2 %collective-permute-start.1 = (bf16[16,3600]{1,0:T(8,128)(2,1)S(1)}, bf16[16,3600]{1,0:T(8,128)(2,1)S(1)}, u32[]{:S(2)}, u32[]{:S(2)}) collective-permute-start(bf16[16,3600]{1,0:T(8,128)(2,1)S(1)} %get-tuple-element.17), channel_id=1, source_target_pairs={{32,0},{64,32},{96,64},{128,96},{160,128},{192,160},{224,192},{256... | collective-permute-start | bytes 345608 | tf_op jit(solution)/shard_map/ppermute | solution.py:238
  25.1 8.8 %collective-permute-start.3 = (bf16[18,3600]{1,0:T(8,128)(2,1)S(1)}, bf16[18,3600]{1,0:T(8,128)(2,1)S(1)}, u32[]{:S(2)}, u32[]{:S(2)}) collective-permute-start(bf16[18,3600]{1,0:T(8,128)(2,1)S(1)} %pad_maximum_fusion.1), channel_id=1, source_target_pairs={{1,0},{2,1},{3,2},{4,3},{5,4},{6,5},{7,6},{8,7},{9,8},{10,9},{11,1... | collective-permute-start | bytes 388808 | tf_op jit(solution)/shard_map/ppermute | solution.py:247
  26.5 7.7 %collective-permute-start.2 = (bf16[18,3600]{1,0:T(8,128)(2,1)S(1)}, bf16[18,3600]{1,0:T(8,128)(2,1)S(1)}, u32[]{:S(2)}, u32[]{:S(2)}) collective-permute-start(bf16[18,3600]{1,0:T(8,128)(2,1)S(1)} %pad_maximum_fusion), channel_id=1, source_target_pairs={{0,1},{1,2},{2,3},{3,4},{4,5},{5,6},{6,7},{7,8},{8,9},{9,10},{10,1... | collective-permute-start | bytes 388808 | tf_op jit(solution)/shard_map/ppermute | solution.py:246
  35.4 13.0 %collective-permute-start.4 = (bf16[64,3600]{1,0:T(8,128)(2,1)S(1)}, bf16[64,3600]{1,0:T(8,128)(2,1)S(1)}, u32[]{:S(2)}, u32[]{:S(2)}) collective-permute-start(bf16[64,3600]{1,0:T(8,128)(2,1)S(1)} %get-tuple-element.21), channel_id=1, source_target_pairs={{0,32},{32,0},{1,33},{33,1},{2,34},{34,2},{3,35},{35,3},{4,36},{36... | collective-permute-start | bytes 1382408 | tf_op jit(solution)/shard_map/ppermute | solution.py:295
  38.3 48.5 %collective-permute-start.5 = (bf16[8,16,3600]{2,1,0:T(8,128)(2,1)S(1)}, bf16[8,16,3600]{2,1,0:T(8,128)(2,1)S(1)}, u32[]{:S(2)}, u32[]{:S(2)}) collective-permute-start(bf16[8,16,3600]{2,1,0:T(8,128)(2,1)S(1)} %bitcast.15), channel_id=1, source_target_pairs={{0,8},{1,9},{2,10},{3,11},{4,12},{5,13},{6,14},{7,15},{8,0},{9,1},... | collective-permute-start | bytes 2764808 | tf_op jit(solution)/shard_map/ppermute | solution.py:297
  46.4 40.4 %collective-permute-start.6 = (bf16[8,16,3600]{2,1,0:T(8,128)(2,1)S(1)}, bf16[8,16,3600]{2,1,0:T(8,128)(2,1)}, u32[]{:S(2)}, u32[]{:S(2)}) collective-permute-start(bf16[8,16,3600]{2,1,0:T(8,128)(2,1)S(1)} %bitcast.14), channel_id=1, source_target_pairs={{0,1},{1,0},{2,3},{3,2},{4,5},{5,4},{6,7},{7,6},{8,9},{9,8},{10,11... | collective-permute-start | bytes 2764808 | tf_op jit(solution)/shard_map/ppermute | solution.py:297
  51.2 25.6 %all-to-all-start = ((bf16[32,2,3600]{2,1,0:T(2,128)(2,1)}), bf16[32,2,3600]{2,1,0:T(2,128)(2,1)}, u32[]{:S(2)}, u32[]{:S(2)}) async-start(bf16[32,2,3600]{2,1,0:T(2,128)(2,1)} %reshape.42), calls=%async_computation | async-start | bytes 950272 | tf_op jit(solution)/shard_map/all_to_all | solution.py:303
  79.1 21.6 %all-to-all-start.1 = ((bf16[16,2,3600]{2,1,0:T(2,128)(2,1)}), bf16[16,2,3600]{2,1,0:T(2,128)(2,1)S(1)}, u32[]{:S(2)}, u32[]{:S(2)}) async-start(bf16[16,2,3600]{2,1,0:T(2,128)(2,1)} %broadcast_in_dim.24), calls=%async_computation.1 | async-start | bytes 475136 | tf_op jit(solution)/shard_map/all_to_all | solution.py:332
  91.8 6.9 %collective-permute-start.7 = (f32[1,128]{1,0:T(1,128)S(1)}, f32[1,128]{1,0:T(1,128)S(1)}, u32[]{:S(2)}, u32[]{:S(2)}) collective-permute-start(f32[1,128]{1,0:T(1,128)S(1)} %get-tuple-element.34), channel_id=1, source_target_pairs={{0,8},{1,9},{2,10},{3,11},{4,12},{5,13},{6,14},{7,15},{8,0},{9,1},... | collective-permute-start | bytes 1544 | tf_op jit(solution)/shard_map/ppermute | solution.py:335
  95.2 5.5 %collective-permute-start.8 = (f32[1,128]{1,0:T(1,128)S(1)}, f32[1,128]{1,0:T(1,128)S(1)}, u32[]{:S(2)}, u32[]{:S(2)}) collective-permute-start(f32[1,128]{1,0:T(1,128)S(1)} %get-tuple-element.35), channel_id=1, source_target_pairs={{0,1},{1,0},{2,3},{3,2},{4,5},{5,4},{6,7},{7,6},{8,9},{9,8},{10,11... | collective-permute-start | bytes 1544 | tf_op jit(solution)/shard_map/ppermute | solution.py:335
Sparse Core Ops, SparseCore 0:
  10.5 61.5 all-gather.1

commit v11 on v8

--- a/solution.py
+++ b/solution.py
@@ -237,7 +237,9 @@
     forward = [(i, i + 1) for i in range(lines - 1)]
     backward = [(i + 1, i) for i in range(lines - 1)]
     above = lax.ppermute(strip(tile_rows - 1), SCAN, forward)
-    below = lax.ppermute(strip(0), SCAN, backward)
+    first = strip(0)
+    first, _ = lax.optimization_barrier((first, strip(tile_rows - 1)))
+    below = lax.ppermute(first, SCAN, backward)
 
     grain_count = grain_row.shape[0]
     grain_index = jnp.arange(grain_count, dtype=jnp.int32)

time: 107 us -> 105 us (0.981); the launches traced: 107 us -> 103 us
  starting transfers between devices: 42.9 us -> 37 us
  waiting for transfers between devices: 25.7 us -> 27.5 us
    all_to_all x1, starting transfers between devices: 10.2 us -> 6.03 us  [shards(): group_totals = lax.all_to_all(copies, DICT, 0, 0, tiled=True)]
    ppermute x1, starting transfers between devices: 8.15 us -> 5.14 us  [shards(): lax.ppermute(indexed.reshape(patterns.shape), EVERY, trade)]
    all_to_all x1, starting transfers between devices: 3.89 us -> 6.58 us  [shards(): parts = lax.all_to_all(chip_sums, SCAN, 0, 0, tiled=True)]
    ppermute x1, waiting for transfers between devices: 0.01 us -> 2.16 us  [shards(): below = lax.ppermute(first, SCAN, backward)]
  transfers between devices with their start and end apart: 10 -> 10, of which waited for: 5 -> 5; matrix products, arithmetic and copies ran while one was open for 3% -> 3% of each run, Pallas kernels for 16% -> 17%
where the time goes in v11:
time: 105 us; the launch traced here: 103 us
  starting transfers between devices  37 us (35%)
  waiting for transfers between devices  27.5 us (26%)
  Pallas kernels  21.2 us (20%)
  between operations  14.3 us (14%)
  local copies, waits for them, and re-layouts  2.06 us (2%)
    all_gather x1, waiting for transfers between devices, shards(): panels = lax.all_gather(panel, DICT, axis=0, tiled=True)  21 us
    all_to_all x1, starting transfers between devices, shards(): parts = lax.all_to_all(chip_sums, SCAN, 0, 0, tiled=True)  6.58 us
    all_to_all x1, starting transfers between devices, shards(): group_totals = lax.all_to_all(copies, DICT, 0, 0, tiled=True)  6.03 us
    ppermute x1, starting transfers between devices, shards(): low = lax.ppermute(high_edge, DICT, forward)  5.39 us
    pallas_call x1, Pallas kernels, shards(): other_best = scored(other)  5.23 us
    ppermute x1, starting transfers between devices, shards(): lax.ppermute(indexed.reshape(patterns.shape), EVERY, trade)  5.14 us
    ppermute x1, starting transfers between devices, shards(): high = lax.ppermute(low_edge, DICT, backward)  4.69 us
    pallas_call x1, Pallas kernels, shards(): own_best = scored(indexed)  4.61 us
  transfers between devices with their start and end apart: 10, of which 5 were waited for; matrix products, arithmetic and copies ran while one was open for 3% of the time, Pallas kernels for 17%

profile of v11, /device:TPU:1, one launch (start us, length us, event | category | flops | bytes accessed | tf_op | source)
XLA Modules:
  0.0 102.7 jit_solution(12908384078575160521)
XLA Ops:
  7.2 3.1 %normalise_templates.1 = bf16[64,3600]{1,0:T(8,128)(2,1)} custom-call(bf16[3600,128]{1,0:T(8,128)(2,1)} %bitcast.13), custom_call_target="tpu_custom_call" | custom-call | tf_op jit(solution)/shard_map/normalise_templates/pallas_call | solution.py:190
  10.3 3.1 %filter_tile.1 = (bf16[16,16,3600]{2,1,0:T(8,128)(2,1)S(1)}, bf16[16,3600]{1,0:T(8,128)(2,1)S(1)}, bf16[16,3600]{1,0:T(8,128)(2,1)S(1)}) custom-call(f32[3600]{0:T(1024)} %background_ref.1, f32[16,16,3600]{2,1,0:T(8,128)} %tile_ref), custom_call_target="tpu_custom_call" | custom-call | tf_op jit(solution)/shard_map/filter_tile/pallas_call | solution.py:203
  13.5 5.4 %collective-permute-start = (bf16[16,3600]{1,0:T(8,128)(2,1)S(1)}, bf16[16,3600]{1,0:T(8,128)(2,1)S(1)}, u32[]{:S(2)}, u32[]{:S(2)}) collective-permute-start(bf16[16,3600]{1,0:T(8,128)(2,1)S(1)} %get-tuple-element.16), channel_id=1, source_target_pairs={{0,32},{32,64},{64,96},{96,128},{128,160},{160,192},{192,224},{224... | collective-permute-start | bytes 345608 | tf_op jit(solution)/shard_map/ppermute | solution.py:230
  18.9 4.7 %collective-permute-start.1 = (bf16[16,3600]{1,0:T(8,128)(2,1)S(1)}, bf16[16,3600]{1,0:T(8,128)(2,1)S(1)}, u32[]{:S(2)}, u32[]{:S(2)}) collective-permute-start(bf16[16,3600]{1,0:T(8,128)(2,1)S(1)} %get-tuple-element.17), channel_id=1, source_target_pairs={{32,0},{64,32},{96,64},{128,96},{160,128},{192,160},{224,192},{256... | collective-permute-start | bytes 345608 | tf_op jit(solution)/shard_map/ppermute | solution.py:231
  24.0 1.0 collective-permute-done.1.high_ref
  25.1 3.2 %collective-permute-start.2 = (bf16[18,3600]{1,0:T(8,128)(2,1)S(1)}, bf16[18,3600]{1,0:T(8,128)(2,1)S(1)}, u32[]{:S(2)}, u32[]{:S(2)}) collective-permute-start(bf16[18,3600]{1,0:T(8,128)(2,1)S(1)} %pad_maximum_fusion), channel_id=1, source_target_pairs={{0,1},{1,2},{2,3},{3,4},{4,5},{5,6},{6,7},{7,8},{8,9},{9,10},{10,1... | collective-permute-start | bytes 388808 | tf_op jit(solution)/shard_map/ppermute | solution.py:239
  28.4 1.3 %collective-permute-start.3 = (bf16[18,3600]{1,0:T(8,128)(2,1)S(1)}, bf16[18,3600]{1,0:T(8,128)(2,1)S(1)}, u32[]{:S(2)}, u32[]{:S(2)}) collective-permute-start(bf16[18,3600]{1,0:T(8,128)(2,1)S(1)} %pad_maximum_fusion.1), channel_id=1, source_target_pairs={{1,0},{2,1},{3,2},{4,3},{5,4},{6,5},{7,6},{8,7},{9,8},{10,9},{11,1... | collective-permute-start | bytes 388808 | tf_op jit(solution)/shard_map/ppermute | solution.py:242
  29.7 3.5 %inner_rows.1.inner_ref = bf16[224,3600]{1,0:T(8,128)(2,1)S(1)} custom-call(bf16[16,16,3600]{2,1,0:T(8,128)(2,1)S(1)} %get-tuple-element.15.tile_ref, bf16[16,3600]{1,0:T(8,128)(2,1)S(1)} %collective-permute-done.low_ref, bf16[16,3600]{1,0:T(8,128)(2,1)S(1)} %collective-permute-done.1.high_ref), custom_call_target="tpu_custom_call" | custom-call | flops 9676800 | bytes 12902400 | tf_op jit(solution)/shard_map/inner_rows/pallas_call | solution.py:251
  33.1 2.2 %collective-permute-done.3.below_ref = bf16[18,3600]{1,0:T(8,128)(2,1)S(1)} collective-permute-done((bf16[18,3600]{1,0:T(8,128)(2,1)S(1)}, bf16[18,3600]{1,0:T(8,128)(2,1)S(1)}, u32[]{:S(2)}, u32[]{:S(2)}) %collective-permute-start.3) | collective-permute-done | bytes 129632 | tf_op jit(solution)/shard_map/ppermute | solution.py:242
  35.3 1.0 outer_rows.1
  36.3 1.9 %collective-permute-start.4 = (bf16[64,3600]{1,0:T(8,128)(2,1)S(1)}, bf16[64,3600]{1,0:T(8,128)(2,1)S(1)}, u32[]{:S(2)}, u32[]{:S(2)}) collective-permute-start(bf16[64,3600]{1,0:T(8,128)(2,1)S(1)} %get-tuple-element.21), channel_id=1, source_target_pairs={{0,32},{32,0},{1,33},{33,1},{2,34},{34,2},{3,35},{35,3},{4,36},{36... | collective-permute-start | bytes 1382408 | tf_op jit(solution)/shard_map/ppermute | solution.py:287
  38.2 5.1 %collective-permute-start.5 = (bf16[16,16,3600]{2,1,0:T(8,128)(2,1)S(1)}, bf16[16,16,3600]{2,1,0:T(8,128)(2,1)}, u32[]{:S(2)}, u32[]{:S(2)}) collective-permute-start(bf16[16,16,3600]{2,1,0:T(8,128)(2,1)S(1)} %bitcast.12), channel_id=1, source_target_pairs={{0,8},{32,56},{1,9},{33,57},{2,10},{34,58},{3,11},{35,59},{4,12},{... | collective-permute-start | bytes 5529608 | tf_op jit(solution)/shard_map/ppermute | solution.py:288
  43.5 1.0 reshape.36
  44.4 6.6 %all-to-all-start = ((bf16[32,2,3600]{2,1,0:T(2,128)(2,1)}), bf16[32,2,3600]{2,1,0:T(2,128)(2,1)S(1)}, u32[]{:S(2)}, u32[]{:S(2)}) async-start(bf16[32,2,3600]{2,1,0:T(2,128)(2,1)} %reshape.36), calls=%async_computation | async-start | bytes 950272 | tf_op jit(solution)/shard_map/all_to_all | solution.py:292
  51.0 21.0 %all-gather.2.cloned.1.call-done.panel_ref = bf16[1024,3600]{1,0:T(8,128)(2,1)} async-done(((bf16[64,3600]{1,0:T(8,128)(2,1)}), bf16[1024,3600]{1,0:T(8,128)(2,1)}) %all-gather.2.cloned.1.call-update) | async-done | bytes 7372816 | tf_op jit(solution)/shard_map/all_gather | solution.py:199
  72.0 4.6 %best_scores.2.own_best_ref = f32[1,256]{1,0:T(1,128)S(1)} custom-call(bf16[1024,3600]{1,0:T(8,128)(2,1)} %all-gather.2.cloned.1.call-done.panel_ref, bf16[256,3600]{1,0:T(8,128)(2,1)S(1)} %get-tuple-element.19.points_ref), custom_call_target="tpu_custom_call" | custom-call | flops 1887436800 | bytes 7372800 | tf_op jit(solution)/shard_map/best_scores/pallas_call | solution.py:315
  76.6 0.4 reduce_sum.25
  77.0 0.8 broadcast_in_dim.24
  77.9 6.0 %all-to-all-start.1 = ((bf16[16,2,3600]{2,1,0:T(2,128)(2,1)}), bf16[16,2,3600]{2,1,0:T(2,128)(2,1)S(1)}, u32[]{:S(2)}, u32[]{:S(2)}) async-start(bf16[16,2,3600]{2,1,0:T(2,128)(2,1)} %broadcast_in_dim.24), calls=%async_computation.1 | async-start | bytes 475136 | tf_op jit(solution)/shard_map/all_to_all | solution.py:320
  83.9 5.2 %best_scores.3 = f32[1,256]{1,0:T(1,128)S(1)} custom-call(bf16[1024,3600]{1,0:T(8,128)(2,1)} %all-gather.2.cloned.1.call-done.panel_ref, bf16[256,3600]{1,0:T(8,128)(2,1)} %bitcast.7.points_ref), custom_call_target="tpu_custom_call" | custom-call | flops 1887436800 | bytes 7372800 | tf_op jit(solution)/shard_map/best_scores/pallas_call | solution.py:321
  89.1 2.7 %collective-permute-start.6 = (f32[1,256]{1,0:T(1,128)S(1)}, f32[1,256]{1,0:T(1,128)S(1)}, u32[]{:S(2)}, u32[]{:S(2)}) collective-permute-start(f32[1,256]{1,0:T(1,128)S(1)} %best_scores.3), channel_id=1, source_target_pairs={{0,8},{32,56},{1,9},{33,57},{2,10},{34,58},{3,11},{35,59},{4,12},{... | collective-permute-start | bytes 3080 | tf_op jit(solution)/shard_map/ppermute | solution.py:322
  91.8 2.8 %collective-permute-done.6.returned_ref = f32[1,256]{1,0:T(1,128)S(1)} collective-permute-done((f32[1,256]{1,0:T(1,128)S(1)}, f32[1,256]{1,0:T(1,128)S(1)}, u32[]{:S(2)}, u32[]{:S(2)}) %collective-permute-start.6) | collective-permute-done | bytes 1056 | tf_op jit(solution)/shard_map/ppermute | solution.py:322
  94.7 0.5 all-to-all-done.1.totals_ref
  95.1 0.8 finish.1
  (24 shorter events, 0.7 us)
Async XLA Ops:
  7.2 64.9 %all-gather.2.cloned.1.call-start = ((), (), s32[]{:S(2)}) async-start(), calls=%async_computation.2 | async-start | bytes 8077312 | tf_op jit(solution)/shard_map/all_gather | solution.py:199
  10.3 13.2 %copy-start = (s32[16,16]{1,0:T(8,128)S(1)}, s32[16,16]{1,0:T(8,128)}, u32[]{:S(2)}) copy-start(s32[16,16]{1,0:T(8,128)} %param.10) | copy-start | bytes 3076
  10.3 13.3 %copy-start.1 = (s32[16,16]{1,0:T(8,128)S(1)}, s32[16,16]{1,0:T(8,128)}, u32[]{:S(2)}) copy-start(s32[16,16]{1,0:T(8,128)} %param.9) | copy-start | bytes 3076
  10.3 13.5 %copy-start.2 = (s32[128]{0:T(128)S(1)}, s32[128]{0:T(128)}, u32[]{:S(2)}) copy-start(s32[128]{0:T(128)} %param.11) | copy-start | bytes 1540
  13.5 10.5 %collective-permute-start = (bf16[16,3600]{1,0:T(8,128)(2,1)S(1)}, bf16[16,3600]{1,0:T(8,128)(2,1)S(1)}, u32[]{:S(2)}, u32[]{:S(2)}) collective-permute-start(bf16[16,3600]{1,0:T(8,128)(2,1)S(1)} %get-tuple-element.16), channel_id=1, source_target_pairs={{0,32},{32,64},{64,96},{96,128},{128,160},{160,192},{192,224},{224... | collective-permute-start | bytes 345608 | tf_op jit(solution)/shard_map/ppermute | solution.py:230
  18.9 6.2 %collective-permute-start.1 = (bf16[16,3600]{1,0:T(8,128)(2,1)S(1)}, bf16[16,3600]{1,0:T(8,128)(2,1)S(1)}, u32[]{:S(2)}, u32[]{:S(2)}) collective-permute-start(bf16[16,3600]{1,0:T(8,128)(2,1)S(1)} %get-tuple-element.17), channel_id=1, source_target_pairs={{32,0},{64,32},{96,64},{128,96},{160,128},{192,160},{224,192},{256... | collective-permute-start | bytes 345608 | tf_op jit(solution)/shard_map/ppermute | solution.py:231
  25.1 10.2 %collective-permute-start.2 = (bf16[18,3600]{1,0:T(8,128)(2,1)S(1)}, bf16[18,3600]{1,0:T(8,128)(2,1)S(1)}, u32[]{:S(2)}, u32[]{:S(2)}) collective-permute-start(bf16[18,3600]{1,0:T(8,128)(2,1)S(1)} %pad_maximum_fusion), channel_id=1, source_target_pairs={{0,1},{1,2},{2,3},{3,4},{4,5},{5,6},{6,7},{7,8},{8,9},{9,10},{10,1... | collective-permute-start | bytes 388808 | tf_op jit(solution)/shard_map/ppermute | solution.py:239
  28.4 6.9 %collective-permute-start.3 = (bf16[18,3600]{1,0:T(8,128)(2,1)S(1)}, bf16[18,3600]{1,0:T(8,128)(2,1)S(1)}, u32[]{:S(2)}, u32[]{:S(2)}) collective-permute-start(bf16[18,3600]{1,0:T(8,128)(2,1)S(1)} %pad_maximum_fusion.1), channel_id=1, source_target_pairs={{1,0},{2,1},{3,2},{4,3},{5,4},{6,5},{7,6},{8,7},{9,8},{10,9},{11,1... | collective-permute-start | bytes 388808 | tf_op jit(solution)/shard_map/ppermute | solution.py:242
  36.3 7.1 %collective-permute-start.4 = (bf16[64,3600]{1,0:T(8,128)(2,1)S(1)}, bf16[64,3600]{1,0:T(8,128)(2,1)S(1)}, u32[]{:S(2)}, u32[]{:S(2)}) collective-permute-start(bf16[64,3600]{1,0:T(8,128)(2,1)S(1)} %get-tuple-element.21), channel_id=1, source_target_pairs={{0,32},{32,0},{1,33},{33,1},{2,34},{34,2},{3,35},{35,3},{4,36},{36... | collective-permute-start | bytes 1382408 | tf_op jit(solution)/shard_map/ppermute | solution.py:287
  38.2 45.7 %collective-permute-start.5 = (bf16[16,16,3600]{2,1,0:T(8,128)(2,1)S(1)}, bf16[16,16,3600]{2,1,0:T(8,128)(2,1)}, u32[]{:S(2)}, u32[]{:S(2)}) collective-permute-start(bf16[16,16,3600]{2,1,0:T(8,128)(2,1)S(1)} %bitcast.12), channel_id=1, source_target_pairs={{0,8},{32,56},{1,9},{33,57},{2,10},{34,58},{3,11},{35,59},{4,12},{... | collective-permute-start | bytes 5529608 | tf_op jit(solution)/shard_map/ppermute | solution.py:288
  44.4 32.2 %all-to-all-start = ((bf16[32,2,3600]{2,1,0:T(2,128)(2,1)}), bf16[32,2,3600]{2,1,0:T(2,128)(2,1)S(1)}, u32[]{:S(2)}, u32[]{:S(2)}) async-start(bf16[32,2,3600]{2,1,0:T(2,128)(2,1)} %reshape.36), calls=%async_computation | async-start | bytes 950272 | tf_op jit(solution)/shard_map/all_to_all | solution.py:292
  77.9 17.2 %all-to-all-start.1 = ((bf16[16,2,3600]{2,1,0:T(2,128)(2,1)}), bf16[16,2,3600]{2,1,0:T(2,128)(2,1)S(1)}, u32[]{:S(2)}, u32[]{:S(2)}) async-start(bf16[16,2,3600]{2,1,0:T(2,128)(2,1)} %broadcast_in_dim.24), calls=%async_computation.1 | async-start | bytes 475136 | tf_op jit(solution)/shard_map/all_to_all | solution.py:320
  89.1 5.5 %collective-permute-start.6 = (f32[1,256]{1,0:T(1,128)S(1)}, f32[1,256]{1,0:T(1,128)S(1)}, u32[]{:S(2)}, u32[]{:S(2)}) collective-permute-start(f32[1,256]{1,0:T(1,128)S(1)} %best_scores.3), channel_id=1, source_target_pairs={{0,8},{32,56},{1,9},{33,57},{2,10},{34,58},{3,11},{35,59},{4,12},{... | collective-permute-start | bytes 3080 | tf_op jit(solution)/shard_map/ppermute | solution.py:322
Sparse Core Ops, SparseCore 0:
  10.4 61.5 all-gather.1

commit v12 on v11

--- a/solution.py
+++ b/solution.py
@@ -162,6 +162,12 @@
         out_ref[...] = jnp.max(best.T, axis=0, keepdims=True)
 
 
+def sum_and_repeat(parts_ref, out_ref):
+    total = jnp.sum(parts_ref[...].astype(jnp.float32), axis=0).astype(jnp.bfloat16)
+    for copy in range(out_ref.shape[0]):
+        out_ref[copy] = total
+
+
 def finish(own_best_ref, returned_ref, totals_ref, max_score_ref, patterns_ref):
     pixels = patterns_ref.shape[1]
     rows, cols = max_score_ref.shape
@@ -314,9 +320,14 @@
     )
     own_best = scored(indexed)
     own_best, parts = lax.optimization_barrier((own_best, parts))
-    group_total = jnp.sum(parts.astype(f32), axis=0).astype(bf16)
-
-    copies = jnp.broadcast_to(group_total, (columns,) + group_total.shape)
+    copies = pl.pallas_call(
+        sum_and_repeat,
+        out_shape=jax.ShapeDtypeStruct((columns,) + parts.shape[1:], bf16),
+        in_specs=[pl.BlockSpec(memory_space=VMEM)],
+        out_specs=pl.BlockSpec(memory_space=VMEM),
+        compiler_params=params(4),
+        name="sum_and_repeat",
+    )(parts)
     group_totals = lax.all_to_all(copies, DICT, 0, 0, tiled=True)
     other_best = scored(other)
     returned = lax.ppermute(other_best, EVERY, trade)
@@ -325,7 +336,7 @@
         finish,
         out_shape=(
             jax.ShapeDtypeStruct((tile_rows, tile_cols), f32),
-            jax.ShapeDtypeStruct((2 * group_total.shape[0], pixels), f32),
+            jax.ShapeDtypeStruct((2 * parts.shape[1], pixels), f32),
         ),
         in_specs=[pl.BlockSpec(memory_space=VMEM)] * 3,
         out_specs=[pl.BlockSpec(memory_space=VMEM)] * 2,

time: 105 us -> 105 us (level)
  Pallas kernels: 21.2 us -> 22.4 us
    pallas_call x0 -> x1, Pallas kernels: none -> 1.15 us  [shards(): pl.pallas_call(sum_and_repeat, out_shape=jax.ShapeDtypeStruct((columns,)...]
  transfers between devices with their start and end apart: 10 -> 10, of which waited for: 5 -> 5; matrix products, arithmetic and copies ran while one was open for 3% -> 2% of each run, Pallas kernels for 17% -> 18%
where the time goes in v12:
time: 105 us; the launch traced here: 103 us
  starting transfers between devices  37 us (35%)
  waiting for transfers between devices  27.5 us (26%)
  Pallas kernels  22.4 us (21%)
  between operations  14.3 us (14%)
  local copies, waits for them, and re-layouts  1.26 us (1%)
    all_gather x1, waiting for transfers between devices, shards(): panels = lax.all_gather(panel, DICT, axis=0, tiled=True)  21 us
    all_to_all x1, starting transfers between devices, shards(): parts = lax.all_to_all(chip_sums, SCAN, 0, 0, tiled=True)  6.58 us
    all_to_all x1, starting transfers between devices, shards(): group_totals = lax.all_to_all(copies, DICT, 0, 0, tiled=True)  6.03 us
    ppermute x1, starting transfers between devices, shards(): low = lax.ppermute(high_edge, DICT, forward)  5.39 us
    pallas_call x1, Pallas kernels, shards(): other_best = scored(other)  5.23 us
    ppermute x1, starting transfers between devices, shards(): lax.ppermute(indexed.reshape(patterns.shape), EVERY, trade)  5.14 us
    ppermute x1, starting transfers between devices, shards(): high = lax.ppermute(low_edge, DICT, backward)  4.69 us
    pallas_call x1, Pallas kernels, shards(): own_best = scored(indexed)  4.62 us
  transfers between devices with their start and end apart: 10, of which 5 were waited for; matrix products, arithmetic and copies ran while one was open for 2% of the time, Pallas kernels for 18%

profile of v12, /device:TPU:1, one launch (start us, length us, event | category | flops | bytes accessed | tf_op | source)
XLA Modules:
  0.0 102.7 jit_solution(115127297039066697)
XLA Ops:
  7.2 3.1 %normalise_templates.1 = bf16[64,3600]{1,0:T(8,128)(2,1)} custom-call(bf16[3600,128]{1,0:T(8,128)(2,1)} %bitcast.13), custom_call_target="tpu_custom_call" | custom-call | tf_op jit(solution)/shard_map/normalise_templates/pallas_call | solution.py:196
  10.3 3.1 %filter_tile.1 = (bf16[16,16,3600]{2,1,0:T(8,128)(2,1)S(1)}, bf16[16,3600]{1,0:T(8,128)(2,1)S(1)}, bf16[16,3600]{1,0:T(8,128)(2,1)S(1)}) custom-call(f32[3600]{0:T(1024)} %background_ref.1, f32[16,16,3600]{2,1,0:T(8,128)} %tile_ref), custom_call_target="tpu_custom_call" | custom-call | tf_op jit(solution)/shard_map/filter_tile/pallas_call | solution.py:209
  13.4 5.4 %collective-permute-start = (bf16[16,3600]{1,0:T(8,128)(2,1)S(1)}, bf16[16,3600]{1,0:T(8,128)(2,1)S(1)}, u32[]{:S(2)}, u32[]{:S(2)}) collective-permute-start(bf16[16,3600]{1,0:T(8,128)(2,1)S(1)} %get-tuple-element.16), channel_id=1, source_target_pairs={{0,32},{32,64},{64,96},{96,128},{128,160},{160,192},{192,224},{224... | collective-permute-start | bytes 345608 | tf_op jit(solution)/shard_map/ppermute | solution.py:236
  18.8 4.7 %collective-permute-start.1 = (bf16[16,3600]{1,0:T(8,128)(2,1)S(1)}, bf16[16,3600]{1,0:T(8,128)(2,1)S(1)}, u32[]{:S(2)}, u32[]{:S(2)}) collective-permute-start(bf16[16,3600]{1,0:T(8,128)(2,1)S(1)} %get-tuple-element.17), channel_id=1, source_target_pairs={{32,0},{64,32},{96,64},{128,96},{160,128},{192,160},{224,192},{256... | collective-permute-start | bytes 345608 | tf_op jit(solution)/shard_map/ppermute | solution.py:237
  23.8 0.2 select_reduce_fusion
  24.0 1.0 collective-permute-done.1.high_ref
  25.1 3.2 %collective-permute-start.2 = (bf16[18,3600]{1,0:T(8,128)(2,1)S(1)}, bf16[18,3600]{1,0:T(8,128)(2,1)S(1)}, u32[]{:S(2)}, u32[]{:S(2)}) collective-permute-start(bf16[18,3600]{1,0:T(8,128)(2,1)S(1)} %pad_maximum_fusion), channel_id=1, source_target_pairs={{0,1},{1,2},{2,3},{3,4},{4,5},{5,6},{6,7},{7,8},{8,9},{9,10},{10,1... | collective-permute-start | bytes 388808 | tf_op jit(solution)/shard_map/ppermute | solution.py:245
  28.3 1.3 %collective-permute-start.3 = (bf16[18,3600]{1,0:T(8,128)(2,1)S(1)}, bf16[18,3600]{1,0:T(8,128)(2,1)S(1)}, u32[]{:S(2)}, u32[]{:S(2)}) collective-permute-start(bf16[18,3600]{1,0:T(8,128)(2,1)S(1)} %pad_maximum_fusion.1), channel_id=1, source_target_pairs={{1,0},{2,1},{3,2},{4,3},{5,4},{6,5},{7,6},{8,7},{9,8},{10,9},{11,1... | collective-permute-start | bytes 388808 | tf_op jit(solution)/shard_map/ppermute | solution.py:248
  29.7 3.5 %inner_rows.1.inner_ref = bf16[224,3600]{1,0:T(8,128)(2,1)S(1)} custom-call(bf16[16,16,3600]{2,1,0:T(8,128)(2,1)S(1)} %get-tuple-element.15.tile_ref, bf16[16,3600]{1,0:T(8,128)(2,1)S(1)} %collective-permute-done.low_ref, bf16[16,3600]{1,0:T(8,128)(2,1)S(1)} %collective-permute-done.1.high_ref), custom_call_target="tpu_custom_call" | custom-call | flops 9676800 | bytes 12902400 | tf_op jit(solution)/shard_map/inner_rows/pallas_call | solution.py:257
  33.1 2.2 %collective-permute-done.3.below_ref = bf16[18,3600]{1,0:T(8,128)(2,1)S(1)} collective-permute-done((bf16[18,3600]{1,0:T(8,128)(2,1)S(1)}, bf16[18,3600]{1,0:T(8,128)(2,1)S(1)}, u32[]{:S(2)}, u32[]{:S(2)}) %collective-permute-start.3) | collective-permute-done | bytes 129632 | tf_op jit(solution)/shard_map/ppermute | solution.py:248
  35.3 1.0 outer_rows.1
  36.3 1.9 %collective-permute-start.4 = (bf16[64,3600]{1,0:T(8,128)(2,1)S(1)}, bf16[64,3600]{1,0:T(8,128)(2,1)S(1)}, u32[]{:S(2)}, u32[]{:S(2)}) collective-permute-start(bf16[64,3600]{1,0:T(8,128)(2,1)S(1)} %get-tuple-element.21), channel_id=1, source_target_pairs={{0,32},{32,0},{1,33},{33,1},{2,34},{34,2},{3,35},{35,3},{4,36},{36... | collective-permute-start | bytes 1382408 | tf_op jit(solution)/shard_map/ppermute | solution.py:293
  38.2 5.1 %collective-permute-start.5 = (bf16[16,16,3600]{2,1,0:T(8,128)(2,1)S(1)}, bf16[16,16,3600]{2,1,0:T(8,128)(2,1)}, u32[]{:S(2)}, u32[]{:S(2)}) collective-permute-start(bf16[16,16,3600]{2,1,0:T(8,128)(2,1)S(1)} %bitcast.12), channel_id=1, source_target_pairs={{0,8},{32,56},{1,9},{33,57},{2,10},{34,58},{3,11},{35,59},{4,12},{... | collective-permute-start | bytes 5529608 | tf_op jit(solution)/shard_map/ppermute | solution.py:294
  43.4 1.0 reshape.36
  44.4 6.6 %all-to-all-start = ((bf16[32,2,3600]{2,1,0:T(2,128)(2,1)}), bf16[32,2,3600]{2,1,0:T(2,128)(2,1)S(1)}, u32[]{:S(2)}, u32[]{:S(2)}) async-start(bf16[32,2,3600]{2,1,0:T(2,128)(2,1)} %reshape.36), calls=%async_computation | async-start | bytes 950272 | tf_op jit(solution)/shard_map/all_to_all | solution.py:298
  51.0 21.0 %all-gather.2.cloned.1.call-done.panel_ref = bf16[1024,3600]{1,0:T(8,128)(2,1)} async-done(((bf16[64,3600]{1,0:T(8,128)(2,1)}), bf16[1024,3600]{1,0:T(8,128)(2,1)}) %all-gather.2.cloned.1.call-update) | async-done | bytes 7372816 | tf_op jit(solution)/shard_map/all_gather | solution.py:205
  72.0 4.6 %best_scores.2.own_best_ref = f32[1,256]{1,0:T(1,128)S(1)} custom-call(bf16[1024,3600]{1,0:T(8,128)(2,1)} %all-gather.2.cloned.1.call-done.panel_ref, bf16[256,3600]{1,0:T(8,128)(2,1)S(1)} %get-tuple-element.19.points_ref), custom_call_target="tpu_custom_call" | custom-call | flops 1887436800 | bytes 7372800 | tf_op jit(solution)/shard_map/best_scores/pallas_call | solution.py:321
  76.6 1.1 %sum_and_repeat.1 = bf16[16,2,3600]{2,1,0:T(2,128)(2,1)} custom-call(bf16[32,2,3600]{2,1,0:T(2,128)(2,1)S(1)} %all-to-all-done.parts_ref), custom_call_target="tpu_custom_call" | custom-call | tf_op jit(solution)/shard_map/sum_and_repeat/pallas_call | solution.py:323
  77.8 6.0 %all-to-all-start.1 = ((bf16[16,2,3600]{2,1,0:T(2,128)(2,1)}), bf16[16,2,3600]{2,1,0:T(2,128)(2,1)S(1)}, u32[]{:S(2)}, u32[]{:S(2)}) async-start(bf16[16,2,3600]{2,1,0:T(2,128)(2,1)} %sum_and_repeat.1), calls=%async_computation.1 | async-start | bytes 475136 | tf_op jit(solution)/shard_map/all_to_all | solution.py:331
  83.8 5.2 %best_scores.3 = f32[1,256]{1,0:T(1,128)S(1)} custom-call(bf16[1024,3600]{1,0:T(8,128)(2,1)} %all-gather.2.cloned.1.call-done.panel_ref, bf16[256,3600]{1,0:T(8,128)(2,1)} %bitcast.7.points_ref), custom_call_target="tpu_custom_call" | custom-call | flops 1887436800 | bytes 7372800 | tf_op jit(solution)/shard_map/best_scores/pallas_call | solution.py:332
  89.1 2.7 %collective-permute-start.6 = (f32[1,256]{1,0:T(1,128)S(1)}, f32[1,256]{1,0:T(1,128)S(1)}, u32[]{:S(2)}, u32[]{:S(2)}) collective-permute-start(f32[1,256]{1,0:T(1,128)S(1)} %best_scores.3), channel_id=1, source_target_pairs={{0,8},{32,56},{1,9},{33,57},{2,10},{34,58},{3,11},{35,59},{4,12},{... | collective-permute-start | bytes 3080 | tf_op jit(solution)/shard_map/ppermute | solution.py:333
  91.7 2.8 %collective-permute-done.6.returned_ref = f32[1,256]{1,0:T(1,128)S(1)} collective-permute-done((f32[1,256]{1,0:T(1,128)S(1)}, f32[1,256]{1,0:T(1,128)S(1)}, u32[]{:S(2)}, u32[]{:S(2)}) %collective-permute-start.6) | collective-permute-done | bytes 1056 | tf_op jit(solution)/shard_map/ppermute | solution.py:333
  94.6 0.4 all-to-all-done.1.totals_ref
  95.0 0.8 finish.1
  (23 shorter events, 0.5 us)
Async XLA Ops:
  7.2 64.8 %all-gather.2.cloned.1.call-start = ((), (), s32[]{:S(2)}) async-start(), calls=%async_computation.2 | async-start | bytes 8077312 | tf_op jit(solution)/shard_map/all_gather | solution.py:205
  10.3 13.2 %copy-start = (s32[16,16]{1,0:T(8,128)S(1)}, s32[16,16]{1,0:T(8,128)}, u32[]{:S(2)}) copy-start(s32[16,16]{1,0:T(8,128)} %param.10) | copy-start | bytes 3076
  10.3 13.3 %copy-start.1 = (s32[16,16]{1,0:T(8,128)S(1)}, s32[16,16]{1,0:T(8,128)}, u32[]{:S(2)}) copy-start(s32[16,16]{1,0:T(8,128)} %param.9) | copy-start | bytes 3076
  10.3 13.5 %copy-start.2 = (s32[128]{0:T(128)S(1)}, s32[128]{0:T(128)}, u32[]{:S(2)}) copy-start(s32[128]{0:T(128)} %param.11) | copy-start | bytes 1540
  13.4 10.5 %collective-permute-start = (bf16[16,3600]{1,0:T(8,128)(2,1)S(1)}, bf16[16,3600]{1,0:T(8,128)(2,1)S(1)}, u32[]{:S(2)}, u32[]{:S(2)}) collective-permute-start(bf16[16,3600]{1,0:T(8,128)(2,1)S(1)} %get-tuple-element.16), channel_id=1, source_target_pairs={{0,32},{32,64},{64,96},{96,128},{128,160},{160,192},{192,224},{224... | collective-permute-start | bytes 345608 | tf_op jit(solution)/shard_map/ppermute | solution.py:236
  18.8 6.2 %collective-permute-start.1 = (bf16[16,3600]{1,0:T(8,128)(2,1)S(1)}, bf16[16,3600]{1,0:T(8,128)(2,1)S(1)}, u32[]{:S(2)}, u32[]{:S(2)}) collective-permute-start(bf16[16,3600]{1,0:T(8,128)(2,1)S(1)} %get-tuple-element.17), channel_id=1, source_target_pairs={{32,0},{64,32},{96,64},{128,96},{160,128},{192,160},{224,192},{256... | collective-permute-start | bytes 345608 | tf_op jit(solution)/shard_map/ppermute | solution.py:237
  25.1 10.2 %collective-permute-start.2 = (bf16[18,3600]{1,0:T(8,128)(2,1)S(1)}, bf16[18,3600]{1,0:T(8,128)(2,1)S(1)}, u32[]{:S(2)}, u32[]{:S(2)}) collective-permute-start(bf16[18,3600]{1,0:T(8,128)(2,1)S(1)} %pad_maximum_fusion), channel_id=1, source_target_pairs={{0,1},{1,2},{2,3},{3,4},{4,5},{5,6},{6,7},{7,8},{8,9},{9,10},{10,1... | collective-permute-start | bytes 388808 | tf_op jit(solution)/shard_map/ppermute | solution.py:245
  28.3 6.9 %collective-permute-start.3 = (bf16[18,3600]{1,0:T(8,128)(2,1)S(1)}, bf16[18,3600]{1,0:T(8,128)(2,1)S(1)}, u32[]{:S(2)}, u32[]{:S(2)}) collective-permute-start(bf16[18,3600]{1,0:T(8,128)(2,1)S(1)} %pad_maximum_fusion.1), channel_id=1, source_target_pairs={{1,0},{2,1},{3,2},{4,3},{5,4},{6,5},{7,6},{8,7},{9,8},{10,9},{11,1... | collective-permute-start | bytes 388808 | tf_op jit(solution)/shard_map/ppermute | solution.py:248
  36.3 7.1 %collective-permute-start.4 = (bf16[64,3600]{1,0:T(8,128)(2,1)S(1)}, bf16[64,3600]{1,0:T(8,128)(2,1)S(1)}, u32[]{:S(2)}, u32[]{:S(2)}) collective-permute-start(bf16[64,3600]{1,0:T(8,128)(2,1)S(1)} %get-tuple-element.21), channel_id=1, source_target_pairs={{0,32},{32,0},{1,33},{33,1},{2,34},{34,2},{3,35},{35,3},{4,36},{36... | collective-permute-start | bytes 1382408 | tf_op jit(solution)/shard_map/ppermute | solution.py:293
  38.2 45.6 %collective-permute-start.5 = (bf16[16,16,3600]{2,1,0:T(8,128)(2,1)S(1)}, bf16[16,16,3600]{2,1,0:T(8,128)(2,1)}, u32[]{:S(2)}, u32[]{:S(2)}) collective-permute-start(bf16[16,16,3600]{2,1,0:T(8,128)(2,1)S(1)} %bitcast.12), channel_id=1, source_target_pairs={{0,8},{32,56},{1,9},{33,57},{2,10},{34,58},{3,11},{35,59},{4,12},{... | collective-permute-start | bytes 5529608 | tf_op jit(solution)/shard_map/ppermute | solution.py:294
  44.4 32.2 %all-to-all-start = ((bf16[32,2,3600]{2,1,0:T(2,128)(2,1)}), bf16[32,2,3600]{2,1,0:T(2,128)(2,1)S(1)}, u32[]{:S(2)}, u32[]{:S(2)}) async-start(bf16[32,2,3600]{2,1,0:T(2,128)(2,1)} %reshape.36), calls=%async_computation | async-start | bytes 950272 | tf_op jit(solution)/shard_map/all_to_all | solution.py:298
  77.8 17.2 %all-to-all-start.1 = ((bf16[16,2,3600]{2,1,0:T(2,128)(2,1)}), bf16[16,2,3600]{2,1,0:T(2,128)(2,1)S(1)}, u32[]{:S(2)}, u32[]{:S(2)}) async-start(bf16[16,2,3600]{2,1,0:T(2,128)(2,1)} %sum_and_repeat.1), calls=%async_computation.1 | async-start | bytes 475136 | tf_op jit(solution)/shard_map/all_to_all | solution.py:331
  89.1 5.5 %collective-permute-start.6 = (f32[1,256]{1,0:T(1,128)S(1)}, f32[1,256]{1,0:T(1,128)S(1)}, u32[]{:S(2)}, u32[]{:S(2)}) collective-permute-start(f32[1,256]{1,0:T(1,128)S(1)} %best_scores.3), channel_id=1, source_target_pairs={{0,8},{32,56},{1,9},{33,57},{2,10},{34,58},{3,11},{35,59},{4,12},{... | collective-permute-start | bytes 3080 | tf_op jit(solution)/shard_map/ppermute | solution.py:333
Sparse Core Ops, SparseCore 0:
  10.4 61.5 all-gather.1
